TPU v7x, 32 devices: a whole 2x2x4 slice. The times are simulated.
32 devices in a mesh: dp: 8 (over y, x, core), head: 4 (over z).
Axes of the slice: x: 2, y: 2, z: 4, core: 2. Of those that a mesh axis runs over, the one named last changes fastest.
Arguments:
- block_input: bfloat16 [8192, 1536], P(('dp', 'head')), may hold values from -6 to 6
- seq_lengths: int32 [32], P('dp'), may hold values from 1 to 256, 5120 in all
- cotangent: bfloat16 [8192, 1536], P(('dp', 'head')), may hold values from -6 to 6
- norm_gain: float32 [1536], replicated, may hold values from 0.5 to 1.5
- proj_zx: float32 [1536, 2, 3072], P('dp', None, 'head'), may hold values from -0.15625 to 0.15625
- proj_dt: float32 [1536, 48], P('dp', 'head'), may hold values from -0.15625 to 0.15625
- proj_bc: float32 [1536, 256], P('dp'), may hold values from -0.15625 to 0.15625
- chan_params: float32 [6, 3072], P(None, 'head'), may hold values from -2 to 2, as said below
- conv_bc: float32 [5, 256], replicated, may hold values from -3 to 3, as said below
- head_params: float32 [3, 48], P(None, 'head'), may hold values from -5 to 3.2, as said below
- out_proj: float32 [3072, 1536], P(('head', 'dp')), may hold values from -0.109375 to 0.109375
- gain_moments: float32 [2, 1536], replicated, may hold values from -40 to 40, as said below
- zx_moments: float32 [2, 1536, 2, 3072], P(None, 'dp', None, 'head'), may hold values from -40 to 40, as said below
- dt_moments: float32 [2, 1536, 48], P(None, 'dp', 'head'), may hold values from -40 to 40, as said below
- bc_moments: float32 [2, 1536, 256], P(None, 'dp'), may hold values from -40 to 40, as said below
- chan_moments: float32 [2, 6, 3072], P(None, None, 'head'), may hold values from -40 to 40, as said below
- convbc_moments: float32 [2, 5, 256], replicated, may hold values from -40 to 40, as said below
- head_moments: float32 [2, 3, 48], P(None, None, 'head'), may hold values from -40 to 40, as said below
- out_moments: float32 [2, 3072, 1536], P(None, ('head', 'dp')), may hold values from -40 to 40, as said below
Outputs:
- block_output: bfloat16 [8192, 1536], P(('dp', 'head'))
- input_grad: float32 [8192, 1536], P(('dp', 'head'))
- gain_next: float32 [1536], replicated
- gain_state: float32 [2, 1536], replicated
- zx_next: float32 [1536, 2, 3072], P('dp', None, 'head')
- zx_state: float32 [2, 1536, 2, 3072], P(None, 'dp', None, 'head')
- dt_next: float32 [1536, 48], P('dp', 'head')
- dt_state: float32 [2, 1536, 48], P(None, 'dp', 'head')
- bc_next: float32 [1536, 256], P('dp')
- bc_state: float32 [2, 1536, 256], P(None, 'dp')
- chan_next: float32 [6, 3072], P(None, 'head')
- chan_state: float32 [2, 6, 3072], P(None, None, 'head')
- convbc_next: float32 [5, 256], replicated
- convbc_state: float32 [2, 5, 256], replicated
- head_next: float32 [3, 48], P(None, 'head')
- head_state: float32 [2, 3, 48], P(None, None, 'head')
- outproj_next: float32 [3072, 1536], P(('head', 'dp'))
- outproj_state: float32 [2, 3072, 1536], P(None, ('head', 'dp'))
Inputs may be any that keep to these rules, and one draw needn't show every extreme that they name: Each padded sequence is live on its first seq_lengths positions; the lengths sum to 5120 and some sequence is live on all 256 positions. `chan_params`: taps in -2 to 2, bias in -0.5 to 0.5, gate gains in 0.5 to 1.5. `conv_bc`: taps and biases of B and C. `head_params`: A_log in -3 to 3.2, step bias in -5 to -1, skip coefficient in 0.5 to 1.5. `gain_moments`: root second moments lie in 3 to 40. `zx_moments`: root second moments lie in 3 to 40. `dt_moments`: root second moments lie in 3 to 40. `bc_moments`: root second moments lie in 3 to 40. `chan_moments`: root second moments lie in 3 to 40. `convbc_moments`: root second moments lie in 3 to 40. `head_moments`: root second moments lie in 3 to 40. `out_moments`: root second moments lie in 3 to 40.
All inputs are finite; a program needn't handle non-finite values. No bound on the sum of `seq_lengths` on one device may be relied on, other than what follows from the above.
Results may differ from a plain program's by a relative error of at most 0.012.
Values may be sent and summed in bfloat16 or wider, within the bound.
No kernel may reach another device: no remote copies, remote signals or barrier semaphores. Data moves between devices by JAX's collectives and lax.ppermute only.
A program may use at most 128 MiB of HBM per device.

v0:
```python
import jax
import jax.numpy as jnp
from jax import lax
from jax.sharding import PartitionSpec as P

norm_eps = 1e-05
beta_one = 0.9
beta_two = 0.95
adam_eps = 1e-08
step_count = 3.0
rate_matrix = 0.005
rate_vector = 0.2
weight_decay = 0.1
highest = lax.Precision.HIGHEST


def causal(values, tap_rows):
    kernel = tap_rows.shape[0] - 1
    length = values.shape[0]
    padded = jnp.pad(values, ((kernel - 1, 0), (0, 0)))
    summed = jnp.broadcast_to(tap_rows[kernel][None, :], values.shape)
    for offset in range(kernel):
        summed = summed + tap_rows[offset][None, :] * padded[offset : offset + length]
    return summed


def mixer_slot(proj_rows, bc_rows, step_raw, conv_taps, conv_shared, head_table):
    length = proj_rows.shape[0]
    inner_loc = conv_taps.shape[1]
    heads_loc = head_table.shape[1]
    headdim = inner_loc // heads_loc
    state_dim = bc_rows.shape[1] // 2
    gate_pre = proj_rows[:, :inner_loc]
    conv_x = jax.nn.silu(causal(proj_rows[:, inner_loc:], conv_taps))
    shared = jax.nn.silu(causal(bc_rows, conv_shared))
    input_map = shared[:, :state_dim]
    output_map = shared[:, state_dim:]
    step_size = jax.nn.softplus(step_raw + head_table[1][None, :])
    decay_rate = -jnp.exp(head_table[0])
    row_pos = lax.broadcasted_iota(jnp.int32, (length, length), 0)
    col_pos = lax.broadcasted_iota(jnp.int32, (length, length), 1)
    causal_mask = row_pos >= col_pos
    lower_ones = causal_mask.astype(jnp.float32)
    cum_log = jnp.dot(lower_ones, step_size * decay_rate[None, :], precision=highest).T
    log_gap = cum_log[:, :, None] - cum_log[:, None, :]
    decay_mat = jnp.exp(jnp.where(causal_mask[None], log_gap, -1e30))
    scores = jnp.dot(output_map, input_map.T, precision=highest)
    weights = scores[None] * decay_mat * step_size.T[:, None, :]
    head_values = conv_x.reshape(length, heads_loc, headdim)
    output = jnp.einsum("hts,shp->thp", weights, head_values, precision=highest)
    output = output + head_table[2][None, :, None] * head_values
    return output.reshape(length, inner_loc) * jax.nn.silu(gate_pre)


def adam_update(parameter, moments, gradient, learn_rate, decay_coef):
    first_mom = beta_one * moments[0] + (1.0 - beta_one) * gradient
    second_mom = beta_two * moments[1] * moments[1] + (1.0 - beta_two) * gradient * gradient
    second_root = jnp.sqrt(second_mom)
    first_hat = first_mom / (1.0 - beta_one**step_count)
    second_hat = second_mom / (1.0 - beta_two**step_count)
    updated = parameter - learn_rate * (
        first_hat / (jnp.sqrt(second_hat) + adam_eps) + decay_coef * parameter
    )
    return (updated, jnp.stack([first_mom, second_root]))


def shards(
    block_input,
    seq_lengths,
    cotangent,
    norm_gain,
    proj_zx,
    proj_dt,
    proj_bc,
    chan_params,
    conv_bc,
    head_params,
    out_proj,
    gain_moments,
    zx_moments,
    dt_moments,
    bc_moments,
    chan_moments,
    convbc_moments,
    head_moments,
    out_moments,
):
    slot_count = seq_lengths.shape[0]
    rows_own = block_input.shape[0]
    rows_dev = rows_own * lax.axis_size("head")
    seq_len = rows_dev // slot_count
    model_width = block_input.shape[1]
    inner_loc = chan_params.shape[1]
    inner_all = inner_loc * lax.axis_size("head")
    heads_loc = head_params.shape[1]
    kernel = chan_params.shape[0] - 2
    state_two = conv_bc.shape[1]
    row_start = lax.axis_index("head") * rows_own
    zx_full, dt_full, bc_full, out_full = (
        lax.all_gather(proj_zx.astype(jnp.bfloat16), "dp", axis=0, tiled=True),
        lax.all_gather(proj_dt.astype(jnp.bfloat16), "dp", axis=0, tiled=True),
        lax.all_gather(proj_bc.astype(jnp.bfloat16), "dp", axis=0, tiled=True),
        lax.all_gather(out_proj.astype(jnp.bfloat16), "dp", axis=0, tiled=True),
    )
    zx_mat = zx_full.reshape(model_width, 2 * inner_loc)
    positions = lax.broadcasted_iota(jnp.int32, (slot_count, seq_len), 1)
    live_mask = (positions < seq_lengths[:, None]).astype(jnp.float32).reshape(rows_dev, 1)
    live_own = lax.dynamic_slice_in_dim(live_mask, row_start, rows_own, 0)
    input_all = lax.all_gather(block_input, "head", axis=0, tiled=True)
    input_float = input_all.astype(jnp.float32)
    inv_norm = lax.rsqrt(jnp.mean(input_float * input_float, axis=-1, keepdims=True) + norm_eps)
    input_hat = input_float * inv_norm
    gain_float = lax.optimization_barrier(norm_gain.astype(jnp.bfloat16)).astype(jnp.float32)
    normed_in = (input_hat * gain_float[None, :]).astype(jnp.bfloat16)
    proj_out = jnp.dot(normed_in, zx_mat, preferred_element_type=jnp.float32)
    step_raw = jnp.dot(normed_in, dt_full, preferred_element_type=jnp.float32)
    bc_out = jnp.dot(normed_in, bc_full, preferred_element_type=jnp.float32)
    proj_slots = proj_out.reshape(slot_count, seq_len, 2 * inner_loc)
    bc_slots = bc_out.reshape(slot_count, seq_len, state_two)
    step_slots = step_raw.reshape(slot_count, seq_len, heads_loc)
    conv_taps = chan_params[: kernel + 1]
    gate_gain = chan_params[kernel + 1]

    def forward_slot(members_slot):
        return mixer_slot(
            members_slot[0], members_slot[1], members_slot[2], conv_taps, conv_bc, head_params
        )

    gated_rows = lax.map(forward_slot, (proj_slots, bc_slots, step_slots)).reshape(
        rows_dev, inner_loc
    )
    square_sum = lax.psum(jnp.sum(gated_rows * gated_rows, axis=-1), "head")
    inv_gate = lax.rsqrt(square_sum[:, None] / inner_all + norm_eps)
    normed_out = (gated_rows * inv_gate * gate_gain[None, :]).astype(jnp.bfloat16)
    branch = lax.psum_scatter(
        jnp.dot(normed_out, out_full, preferred_element_type=jnp.float32).astype(jnp.bfloat16),
        "head",
        scatter_dimension=0,
        tiled=True,
    ).astype(jnp.float32)
    block_output = (block_input.astype(jnp.float32) + live_own * branch).astype(jnp.bfloat16)
    cot_all = lax.all_gather(cotangent, "head", axis=0, tiled=True)
    cot_live = (cot_all.astype(jnp.float32) * live_mask).astype(jnp.bfloat16)
    grad_normed = jnp.dot(cot_live, out_full.T, preferred_element_type=jnp.float32)
    grad_out = jnp.dot(normed_out.T, cot_live, preferred_element_type=jnp.float32)
    grad_gate = jnp.sum(grad_normed * gated_rows * inv_gate, axis=0)
    scaled = grad_normed * gate_gain[None, :]
    cross_sum = lax.psum(jnp.sum(scaled * gated_rows, axis=-1), "head")
    grad_gated = inv_gate * scaled - gated_rows * inv_gate**3 * cross_sum[:, None] / inner_all

    def backward_slot(slot_totals, members_slot):
        unused, pullback = jax.vjp(
            mixer_slot,
            members_slot[0],
            members_slot[1],
            members_slot[2],
            conv_taps,
            conv_bc,
            head_params,
        )
        pieces = pullback(members_slot[3])
        return (
            (slot_totals[0] + pieces[3], slot_totals[1] + pieces[4], slot_totals[2] + pieces[5]),
            (pieces[0], pieces[1], pieces[2]),
        )

    zero_slot = (jnp.zeros_like(conv_taps), jnp.zeros_like(conv_bc), jnp.zeros_like(head_params))
    slot_grads, slot_cots = lax.scan(
        backward_slot,
        zero_slot,
        (proj_slots, bc_slots, step_slots, grad_gated.reshape(slot_count, seq_len, inner_loc)),
    )
    cot_proj = slot_cots[0].reshape(rows_dev, 2 * inner_loc).astype(jnp.bfloat16)
    cot_bc = slot_cots[1].reshape(rows_dev, state_two).astype(jnp.bfloat16)
    cot_step = slot_cots[2].reshape(rows_dev, heads_loc).astype(jnp.bfloat16)
    cot_input = jnp.dot(cot_proj, zx_mat.T, preferred_element_type=jnp.float32)
    cot_input = cot_input + jnp.dot(cot_step, dt_full.T, preferred_element_type=jnp.float32)
    cot_input = cot_input + jnp.dot(cot_bc, bc_full.T, preferred_element_type=jnp.float32)
    grad_zx = jnp.dot(normed_in.T, cot_proj, preferred_element_type=jnp.float32).reshape(
        model_width, 2, inner_loc
    )
    grad_dt = jnp.dot(normed_in.T, cot_step, preferred_element_type=jnp.float32)
    grad_bc = jnp.dot(normed_in.T, cot_bc, preferred_element_type=jnp.float32)
    inv_own = lax.dynamic_slice_in_dim(inv_norm, row_start, rows_own, 0)
    own_hat = block_input.astype(jnp.float32) * inv_own
    cot_whole = lax.psum(cot_input.astype(jnp.bfloat16), "head").astype(jnp.float32)
    row_dot = jnp.sum(cot_whole * gain_float[None, :] * input_hat, axis=-1, keepdims=True)
    cot_own = lax.dynamic_slice_in_dim(cot_whole, row_start, rows_own, 0)
    row_own = lax.dynamic_slice_in_dim(row_dot, row_start, rows_own, 0)
    input_grad = cotangent.astype(jnp.float32) + inv_own * (
        cot_own * gain_float[None, :] - own_hat * row_own / model_width
    )
    grad_gain = jnp.sum(cot_own * own_hat, axis=0)
    grad_zx, grad_dt, grad_bc, grad_out = (
        lax.psum_scatter(
            grad_zx.astype(jnp.bfloat16), "dp", scatter_dimension=0, tiled=True
        ).astype(jnp.float32),
        lax.psum_scatter(
            grad_dt.astype(jnp.bfloat16), "dp", scatter_dimension=0, tiled=True
        ).astype(jnp.float32),
        lax.psum_scatter(
            grad_bc.astype(jnp.bfloat16), "dp", scatter_dimension=0, tiled=True
        ).astype(jnp.float32),
        lax.psum_scatter(
            grad_out.astype(jnp.bfloat16), "dp", scatter_dimension=0, tiled=True
        ).astype(jnp.float32),
    )
    grad_chan = jnp.concatenate([slot_grads[0], grad_gate[None, :]], axis=0)
    grad_gain, grad_chan, grad_head, grad_convbc = lax.psum(
        (grad_gain, grad_chan, slot_grads[2], slot_grads[1]), "dp"
    )
    grad_bc, grad_convbc, grad_gain = (
        lax.psum(grad_bc.astype(jnp.bfloat16), "head").astype(jnp.float32),
        lax.psum(grad_convbc.astype(jnp.bfloat16), "head").astype(jnp.float32),
        lax.psum(grad_gain.astype(jnp.bfloat16), "head").astype(jnp.float32),
    )
    gain_next, gain_state = adam_update(norm_gain, gain_moments, grad_gain, rate_vector, 0.0)
    zx_next, zx_state = adam_update(proj_zx, zx_moments, grad_zx, rate_matrix, weight_decay)
    dt_next, dt_state = adam_update(proj_dt, dt_moments, grad_dt, rate_matrix, weight_decay)
    bc_next, bc_state = adam_update(proj_bc, bc_moments, grad_bc, rate_matrix, weight_decay)
    chan_next, chan_state = adam_update(chan_params, chan_moments, grad_chan, rate_vector, 0.0)
    convbc_next, convbc_state = adam_update(conv_bc, convbc_moments, grad_convbc, rate_vector, 0.0)
    head_next, head_state = adam_update(head_params, head_moments, grad_head, rate_vector, 0.0)
    outproj_next, outproj_state = adam_update(
        out_proj, out_moments, grad_out, rate_matrix, weight_decay
    )
    return (
        block_output,
        input_grad,
        gain_next,
        gain_state,
        zx_next,
        zx_state,
        dt_next,
        dt_state,
        bc_next,
        bc_state,
        chan_next,
        chan_state,
        convbc_next,
        convbc_state,
        head_next,
        head_state,
        outproj_next,
        outproj_state,
    )


def solution(mesh):
    placed = (
        P(("dp", "head"), None),
        P("dp"),
        P(("dp", "head"), None),
        P(),
        P("dp", None, "head"),
        P("dp", "head"),
        P("dp", None),
        P(None, "head"),
        P(),
        P(None, "head"),
        P(("head", "dp"), None),
        P(),
        P(None, "dp", None, "head"),
        P(None, "dp", "head"),
        P(None, "dp", None),
        P(None, None, "head"),
        P(),
        P(None, None, "head"),
        P(None, ("head", "dp"), None),
    )
    return jax.shard_map(
        shards,
        mesh=mesh,
        in_specs=placed,
        out_specs=(
            P(("dp", "head"), None),
            P(("dp", "head"), None),
            P(),
            P(),
            P("dp", None, "head"),
            P(None, "dp", None, "head"),
            P("dp", "head"),
            P(None, "dp", "head"),
            P("dp", None),
            P(None, "dp", None),
            P(None, "head"),
            P(None, None, "head"),
            P(),
            P(),
            P(None, "head"),
            P(None, None, "head"),
            P(("head", "dp"), None),
            P(None, ("head", "dp"), None),
        ),
        check_vma=False,
    )
```

profile of v0, /device:TPU:0, one launch (start us, length us, event | category | flops | bytes accessed | tf_op | source)
XLA Modules:
  0.0 714.8 jit_solution(882251160323522166)
XLA Ops:
  12.2 12.9 %all_gather.20 = bf16[1536,256]{1,0:T(8,128)(2,1)} all-gather(bf16[192,256]{1,0:T(8,128)(2,1)S(1)} %convert_element_type.153), channel_id=1, replica_groups=mesh['dp'=8,'head'=4] {'dp'}, dimensions={0}, use_global_device_ids=true | all-gather | bytes 884736 | tf_op jit(solution)/shard_map/all_gather | solution.py:102
  25.1 9.1 %all-gather = bf16[8,192,12]{1,2,0:T(8,128)(2,1)S(1)} all-gather(bf16[1,192,12]{1,2,0:T(8,128)(2,1)S(1)} %convert_bitcast_fusion), channel_id=1, replica_groups=mesh['dp'=8,'head'=4] {'dp'}, dimensions={0}, use_global_device_ids=true | all-gather | bytes 41472 | tf_op jit(solution)/shard_map/all_gather | solution.py:101
  35.1 40.8 %all-gather.6.cloned.1.call-done = bf16[1024,1536]{1,0:T(8,128)(2,1)} async-done(((bf16[256,1536]{1,0:T(8,128)(2,1)}), bf16[1024,1536]{1,0:T(8,128)(2,1)}) %all-gather.6.cloned.1.call-update) | async-done | bytes 3145744 | tf_op jit(solution)/shard_map/all_gather | solution.py:109
  82.8 33.0 %all-gather.8.cloned.1.call-done = bf16[1536,2,768]{2,1,0:T(2,128)(2,1)} async-done(((bf16[192,2,768]{2,1,0:T(2,128)(2,1)}), bf16[1536,2,768]{2,1,0:T(2,128)(2,1)}) %all-gather.8.cloned.1.call-update) | async-done | bytes 4718608 | tf_op jit(solution)/shard_map/all_gather | solution.py:100
  115.8 11.4 %reshape.322 = bf16[1536,1536,1]{1,0,2:T(8,128)(2,1)} reshape(bf16[1536,2,768]{2,1,0:T(2,128)(2,1)} %all-gather.8.cloned.1.call-done) | data formatting | bytes 9437184 | tf_op jit(solution)/shard_map/reshape | solution.py:105
  127.2 9.4 %fusion.160 = f32[4,256,1536]{1,2,0:T(8,128)} fusion(bf16[4,256,1536]{2,1,0:T(8,128)(2,1)S(1)} %bitcast.438, bf16[1536,1536,1]{1,0,2:T(8,128)(2,1)} %reshape.322), kind=kOutput, calls=%fused_computation.316 | convolution fusion | flops 4831838208 | bytes 14155776 | tf_op jit(solution)/shard_map/dot_general | solution.py:115
  136.6 39.3 %while.36 = (s32[]{:T(128)}, f32[4,256,768]{1,2,0:T(8,128)}, f32[5,768]{1,0:T(8,128)S(1)}, f32[4,256,1536]{1,2,0:T(8,128)}, f32[5,256]{1,0:T(8,128)S(1)}, /*inde...) while((s32[]{:T(128)}, f32[4,256,768]{1,2,0:T(8,128)}, ...), condition=%wide.region_2.3_spmd, body=%wide.region_1.2_spmd.sunk | while | flops 721925120 | bytes 12330901 | solution.py:129
  179.9 12.4 %psum.70 = f32[1024]{0:T(1024)S(1)} all-reduce(f32[1024]{0:T(1024)S(1)} %bitcast.479), channel_id=1, replica_groups=mesh['dp'=8,'head'=4] {'head'}, use_global_device_ids=true, to_apply=%region_4.5 | all-reduce | flops 1024 | bytes 8192 | tf_op jit(solution)/shard_map/psum | solution.py:132
  192.3 20.0 %all-gather.12.cloned.1.call-done = bf16[1024,1536]{1,0:T(8,128)(2,1)} async-done(((bf16[256,1536]{1,0:T(8,128)(2,1)}), bf16[1024,1536]{1,0:T(8,128)(2,1)}) %all-gather.12.cloned.1.call-update) | async-done | bytes 3145744 | tf_op jit(solution)/shard_map/all_gather | solution.py:142
  212.3 8.8 %fusion.111 = (f32[768]{0:T(1024)}, f32[1024]{0:T(1024)S(1)}, f32[1024,768]{1,0:T(8,128)}) fusion(f32[4,256,768]{2,1,0:T(8,128)} %copy.117, f32[1024]{0:T(1024)S(1)} %get-tuple-element.747, f32[768]{0:T(1024)S(1)} %slice_reduce_fusion.11, bf16[768,1536]{1,0:T(8,128)(2,1)} %all-gather.10.cloned.1.call-done, ...), kind=kOutput, calls=%fused_computation.196 | convolution fusion | flops 2425354496 | bytes 11814912 | tf_op jit(solution)/shard_map/dot_general | solution.py:144
  221.1 9.0 %psum.71 = f32[1024]{0:T(1024)S(1)} all-reduce(f32[1024]{0:T(1024)S(1)} %get-tuple-element.611), channel_id=1, replica_groups=mesh['dp'=8,'head'=4] {'head'}, use_global_device_ids=true, to_apply=%region_7.8 | all-reduce | flops 1024 | bytes 8192 | tf_op jit(solution)/shard_map/psum | solution.py:148
  230.1 4.2 fusion.108
  234.3 98.4 %while.37 = (s32[]{:T(128)}, f32[5,768]{1,0:T(8,128)S(1)}, f32[5,256]{1,0:T(8,128)S(1)}, f32[3,12]{1,0:T(4,128)S(1)}, bf16[4,256,1536]{2,1,0:T(8,128)(2,1)}, /*i...) while((s32[]{:T(128)}, f32[5,768]{1,0:T(8,128)S(1)}, ...), condition=%wide.region_27.28_spmd.clone, body=%wide.region_8.27_spmd.clone.sunk | while | flops 2164275456 | bytes 51899236 | solution.py:168
  244.5 4.8 fusion.259
  269.0 4.8 fusion.259
  293.4 4.8 fusion.259
  317.9 4.8 fusion.259
  338.6 6.6 convolution_convert_fusion.2
  350.5 5.1 fusion.163
  358.3 12.6 %reduce-scatter.12.cloned.1.call-done = bf16[192,256]{1,0:T(8,128)(2,1)} async-done(((bf16[1536,256]{1,0:T(8,128)(2,1)}), bf16[192,256]{1,0:T(8,128)(2,1)}) %reduce-scatter.12.cloned.1.call-update) | async-done | bytes 98320 | tf_op jit(solution)/shard_map/reduce_scatter | solution.py:201
  371.0 6.4 convolution_convert_fusion.1
  377.5 4.9 copy.144
  382.3 8.8 %convolution_convert_fusion = bf16[1536,2,768]{2,0,1:T(8,128)(2,1)} fusion(bf16[2,768,1024]{2,1,0:T(8,128)(2,1)} %bitcast.448, bf16[1024,1536]{1,0:T(8,128)(2,1)S(1)} %copy-done.1), kind=kOutput, calls=%fused_computation.181 | convolution fusion | flops 4834197504 | bytes 11010048 | tf_op jit(solution)/shard_map/dot_general | solution.py:179
  399.3 9.0 %reduce-scatter.16.cloned.1.call-done = bf16[192,12]{1,0:T(8,128)(2,1)} async-done(((bf16[1536,12]{1,0:T(8,128)(2,1)}), bf16[192,12]{1,0:T(8,128)(2,1)}) %reduce-scatter.16.cloned.1.call-update) | async-done | bytes 4624
  410.5 44.1 %reduce-scatter.14.cloned.1.call-done = bf16[96,1536]{1,0:T(8,128)(2,1)} async-done(((bf16[768,1536]{1,0:T(8,128)(2,1)}), bf16[96,1536]{1,0:T(8,128)(2,1)}) %reduce-scatter.14.cloned.1.call-update) | async-done | bytes 294928 | tf_op jit(solution)/shard_map/reduce_scatter | solution.py:204
  458.5 122.8 %all-reduce.34.cloned.1.call-done = (bf16[1024,1536]{1,0:T(8,128)(2,1)}, bf16[192,256]{1,0:T(8,128)(2,1)}) async-done(((bf16[1024,1536]{1,0:T(8,128)(2,1)}, bf16[192,256]{1,0:T(8,128)(2,1)}), (bf16[1024,1536]{1,0:T(8,128)(2,1)}, bf16[192,256]{1,0:T(8,128)(2,1)})) %all-reduce.34.cloned.1.call-update) | async-done | bytes 3244048 | tf_op jit(solution)/shard_map/psum | solution.py:186
  581.3 5.6 convert_element_type.172
  590.6 52.5 %reduce-scatter.8.cloned.1.call-done = bf16[256,1536]{1,0:T(8,128)(2,1)} async-done(((bf16[1024,1536]{1,0:T(8,128)(2,1)}), bf16[256,1536]{1,0:T(8,128)(2,1)}) %reduce-scatter.8.cloned.1.call-update) | async-done | bytes 786448 | tf_op jit(solution)/shard_map/reduce_scatter | solution.py:135
  643.1 4.9 fusion.118
  648.0 25.3 %all-reduce.29 = (bf16[1536]{0:T(1024)(128)(2,1)}, f32[6,768]{1,0:T(8,128)}, bf16[5,256]{1,0:T(8,128)(2,1)}, f32[3,12]{1,0:T(4,128)}) all-reduce(f32[1536]{0:T(1024)} %get-tuple-element.712, f32[6,768]{1,0:T(8,128)} %pad_maximum_fusion.5, f32[5,256]{1,0:T(8,128)S(1)} %get-tuple-element.358, ...), channel_id=1, replica_groups=mesh['dp'=8,'head'=4] {'dp'}, use_global_device_ids=true, to_apply=%region_31.32 | all-reduce | flops 7460 | bytes 54048 | tf_op jit(solution)/shard_map/psum | solution.py:209
  675.2 11.6 %all-reduce.30 = (bf16[1536]{0:T(1024)(128)(2,1)S(1)}, bf16[5,256]{1,0:T(8,128)(2,1)S(1)}) all-reduce(bf16[1536]{0:T(1024)(128)(2,1)} %get-tuple-element.664, bf16[5,256]{1,0:T(8,128)(2,1)} %get-tuple-element.666), channel_id=1, replica_groups=mesh['dp'=8,'head'=4] {'head'}, use_global_device_ids=true, to_apply=%region_32.33 | all-reduce | flops 2816 | bytes 11264 | tf_op jit(solution)/shard_map/psum | solution.py:215
  692.8 7.3 %reduce-scatter.10.cloned.1.call-done = bf16[192,2,768]{2,0,1:T(8,128)(2,1)} async-done(((bf16[1536,2,768]{2,0,1:T(8,128)(2,1)}), bf16[192,2,768]{2,0,1:T(8,128)(2,1)}) %reduce-scatter.10.cloned.1.call-update) | async-done | bytes 589840 | tf_op jit(solution)/shard_map/reduce_scatter | solution.py:195
  (416 shorter events, 180.3 us)
Async XLA Ops:
  7.2 17.9 %copy-start.30 = (f32[192,12]{0,1:T(8,128)S(1)}, f32[192,12]{0,1:T(8,128)}, u32[]{:S(2)}) copy-start(f32[192,12]{0,1:T(8,128)} %param.28) | copy-start | bytes 27652
  7.2 27.1 %copy-start.27 = (f32[3,12]{1,0:T(4,128)S(1)}, f32[3,12]{1,0:T(4,128)}, u32[]{:S(2)}) copy-start(f32[3,12]{1,0:T(4,128)} %param.32) | copy-start | bytes 436
  7.2 27.1 %copy-start.42 = (s32[4]{0:T(128)S(1)}, s32[4]{0:T(128)}, u32[]{:S(2)}) copy-start(s32[4]{0:T(128)} %param.24) | copy-start | bytes 52
  7.3 27.8 %copy-start.13 = (f32[6,768]{1,0:T(8,128)S(1)}, f32[6,768]{1,0:T(8,128)}, u32[]{:S(2)}) copy-start(f32[6,768]{1,0:T(8,128)} %param.30) | copy-start | bytes 55300
  7.3 68.6 %all-gather.6.cloned.1.call-start = ((), (), s32[]{:S(2)}) async-start(), calls=%async_computation.5 | async-start | bytes 3932160 | tf_op jit(solution)/shard_map/all_gather | solution.py:109
  8.0 107.8 %all-gather.8.cloned.1.call-start = ((), (), s32[]{:S(2)}) async-start(), calls=%async_computation.6 | async-start | bytes 5308416 | tf_op jit(solution)/shard_map/all_gather | solution.py:100
  10.6 181.7 %all-gather.10.cloned.1.call-start = ((), (), s32[]{:S(2)}) async-start(), calls=%async_computation.7 | async-start | bytes 2654208 | tf_op jit(solution)/shard_map/all_gather | solution.py:103
  11.4 200.9 %all-gather.12.cloned.1.call-start = ((), (), s32[]{:S(2)}) async-start(), calls=%async_computation.9 | async-start | bytes 3932160 | tf_op jit(solution)/shard_map/all_gather | solution.py:142
  12.0 358.9 %reduce-scatter.12.cloned.1.call-start = ((), (), s32[]{:S(2)}) async-start(), calls=%async_computation.11 | async-start | bytes 884736 | tf_op jit(solution)/shard_map/reduce_scatter | solution.py:201
  12.1 67.4 %copy-start.24 = (f32[1536]{0:T(1024)}, f32[1536]{0:T(1024)S(1)}, u32[]{:S(2)}) copy-start(f32[1536]{0:T(1024)S(1)} %convert_element_type.150) | copy-start | bytes 18436
  79.8 47.4 %copy-start = (bf16[1024,1536]{1,0:T(8,128)(2,1)}, bf16[1024,1536]{1,0:T(8,128)(2,1)S(1)}, u32[]{:S(2)}) copy-start(bf16[1024,1536]{1,0:T(8,128)(2,1)S(1)} %fusion.100) | copy-start | bytes 9437188
  127.2 9.4 %copy-start.22 = (f32[5,256]{1,0:T(8,128)S(1)}, f32[5,256]{1,0:T(8,128)}, u32[]{:S(2)}) copy-start(f32[5,256]{1,0:T(8,128)} %param.31) | copy-start | bytes 15364
  212.3 17.8 %copy-start.6 = (f32[4,256,768]{2,1,0:T(8,128)S(1)}, f32[4,256,768]{2,1,0:T(8,128)}, u32[]{:S(2)}) copy-start(f32[4,256,768]{2,1,0:T(8,128)} %copy.117) | copy-start | bytes 9437188
  250.7 5.6 copy-start.20
  275.2 5.6 copy-start.20
  299.6 5.6 copy-start.20
  324.1 5.6 copy-start.20
  336.9 71.4 %reduce-scatter.16.cloned.1.call-start = ((), (), s32[]{:S(2)}) async-start(), calls=%async_computation.13 | async-start | bytes 442368
  338.5 116.1 %reduce-scatter.14.cloned.1.call-start = ((), (), s32[]{:S(2)}) async-start(), calls=%async_computation.12 | async-start | bytes 2654208 | tf_op jit(solution)/shard_map/reduce_scatter | solution.py:204
  345.2 236.1 %all-reduce.34.cloned.1.call-start = ((), (), s32[]{:S(2)}) async-start(), calls=%async_computation.14 | async-start | bytes 6488064 | tf_op jit(solution)/shard_map/psum | solution.py:186
  350.5 5.1 copy-start.21
  370.9 272.2 %reduce-scatter.8.cloned.1.call-start = ((), (), s32[]{:S(2)}) async-start(), calls=%async_computation.8 | async-start | bytes 3932160 | tf_op jit(solution)/shard_map/reduce_scatter | solution.py:135
  377.4 322.7 %reduce-scatter.10.cloned.1.call-start = ((), (), s32[]{:S(2)}) async-start(), calls=%async_computation.10 | async-start | bytes 5308416 | tf_op jit(solution)/shard_map/reduce_scatter | solution.py:195
  391.2 7.5 %copy-start.40 = (f32[768]{0:T(1024)S(1)}, f32[768]{0:T(1024)}, u32[]{:S(2)}) copy-start(f32[768]{0:T(1024)} %get-tuple-element.610) | copy-start | bytes 9220
  391.2 7.5 %copy-start.16 = (f32[5,768]{1,0:T(8,128)S(1)}, f32[5,768]{1,0:T(8,128)}, u32[]{:S(2)}) copy-start(f32[5,768]{1,0:T(8,128)} %copy-done.15) | copy-start | bytes 46084
  391.2 18.0 %copy-start.31 = (f32[192,12]{0,1:T(8,128)S(1)}, f32[192,12]{0,1:T(8,128)}, u32[]{:S(2)}) copy-start(f32[192,12]{0,1:T(8,128)} %param.28) | copy-start | bytes 27652
  391.2 63.4 %copy-start.12 = (f32[96,1536]{1,0:T(8,128)S(1)}, f32[96,1536]{1,0:T(8,128)}, u32[]{:S(2)}) copy-start(f32[96,1536]{1,0:T(8,128)} %param.33) | copy-start | bytes 1769476
  581.3 5.6 copy-start.3
  581.3 5.6 copy-start.5
  581.3 5.6 copy-start.25
  581.3 5.6 copy-start.33
  643.1 57.0 %copy-start.7 = (f32[192,2,768]{2,1,0:T(2,128)S(1)}, f32[192,2,768]{2,1,0:T(2,128)}, u32[]{:S(2)}) copy-start(f32[192,2,768]{2,1,0:T(2,128)} %param.27) | copy-start | bytes 3538948
  (27 other events, 73.2 us)
Sparse Core Ops, SparseCore 0:
  9.6 66.1 all-gather.5
  78.3 37.4 all-gather.7
  118.2 28.8 all-gather.9
  148.6 63.6 all-gather.11
  337.0 33.8 reduce-scatter.11
  374.4 33.8 reduce-scatter.15
  412.2 42.3 reduce-scatter.13
  457.0 124.2 all-reduce.33
  583.6 59.4 reduce-scatter.7
  646.4 53.6 reduce-scatter.9
where the time goes:
time: 721 us; the launch traced here: 715 us
  waiting for transfers between devices  343 us (48%)
  matrix products  125 us (17%)
  blocking collectives  80.3 us (11%)
  other arithmetic  75.3 us (10%)
  local copies, waits for them, and re-layouts  73.4 us (10%)
  between operations  15 us (2%)
    psum x1, waiting for transfers between devices, shards(): lax.psum(cot_input.astype(jnp.bfloat16), 'head').astype(jnp.float32)  123 us
    dot_general x16, matrix products, mixer_slot(): output = jnp.einsum('hts,shp->thp', weights, head_values, precision=highest)  59.5 us
    reduce_scatter x1, waiting for transfers between devices, shards(): lax.psum_scatter(jnp.dot(normed_out, out_full, preferred_element_type=jnp...  52.5 us
    reduce_scatter x1, waiting for transfers between devices, shards(): lax.psum_scatter(grad_out.astype(jnp.bfloat16), 'dp', scatter_dimension=0...  44.1 us
    all_gather x1, waiting for transfers between devices, shards(): input_all = lax.all_gather(block_input, 'head', axis=0, tiled=True)  40.8 us
    all_gather x1, waiting for transfers between devices, shards(): lax.all_gather(proj_zx.astype(jnp.bfloat16), 'dp', axis=0, tiled=True)  33 us
    psum x1, blocking collectives, shards(): lax.psum((grad_gain, grad_chan, slot_grads[2], slot_grads[1]), 'dp')  25.3 us
    squeeze x16, local copies, waits for them, and re-layouts, shards(): lax.map(forward_slot, (proj_slots, bc_slots, step_slots))  20.2 us
  transfers between devices with their start and end apart: 10, of which 9 were waited for; matrix products, arithmetic and copies ran while one was open for 21% of the time, Pallas kernels for 0%

commit v1 on v0

v1 whole, which is shorter than its diff:
```python
import functools

import jax
import jax.numpy as jnp
from jax import lax
from jax.experimental import pallas as pl
from jax.experimental.pallas import tpu as pltpu
from jax.sharding import PartitionSpec as P

norm_eps = 1e-05
beta_one = 0.9
beta_two = 0.95
adam_eps = 1e-08
step_count = 3.0
rate_matrix = 0.005
rate_vector = 0.2
weight_decay = 0.1
lanes = 128
sub = 8
f32 = jnp.float32
bf16 = jnp.bfloat16


def dot(lhs, rhs, over=(1, 0)):
    return lax.dot_general(
        lhs, rhs, (((over[0],), (over[1],)), ((), ())), preferred_element_type=f32
    )


def dot_exact(lhs, rhs, over=(1, 0)):
    return lax.dot_general(
        lhs,
        rhs,
        (((over[0],), (over[1],)), ((), ())),
        precision=lax.Precision.HIGHEST,
        preferred_element_type=f32,
    )


def iota(shape, axis):
    return lax.broadcasted_iota(jnp.int32, shape, axis)


def later(values, count):
    if count == 0:
        return values
    rolled = pltpu.roll(values, count, 0)
    return jnp.where(iota(values.shape, 0) >= count, rolled, 0.0)


def earlier(values, count):
    if count == 0:
        return values
    length = values.shape[0]
    rolled = pltpu.roll(values, length - count, 0)
    return jnp.where(iota(values.shape, 0) < length - count, rolled, 0.0)


def conv(values, taps, kernel):
    summed = taps[kernel : kernel + 1] + taps[kernel - 1 : kernel] * values
    for offset in range(kernel - 1):
        summed = summed + taps[offset : offset + 1] * later(values, kernel - 1 - offset)
    return summed


def conv_back(grads, taps, kernel):
    summed = taps[kernel - 1 : kernel] * grads
    for offset in range(kernel - 1):
        summed = summed + taps[offset : offset + 1] * earlier(grads, kernel - 1 - offset)
    return summed


def conv_sums(grads, values, kernel):
    rows = [
        jnp.sum(grads * later(values, kernel - 1 - offset), axis=0, keepdims=True)
        for offset in range(kernel)
    ]
    rows.append(jnp.sum(grads, axis=0, keepdims=True))
    return rows


def sigmoid(values):
    return 1.0 / (1.0 + jnp.exp(-values))


def shared_parts(proj_ref, cbc_ref, head_ref, inner, state, kernel):
    bc_rows = proj_ref[:, 2 * inner : 2 * inner + 2 * state]
    step_raw = proj_ref[:, 2 * inner + 2 * state :] + head_ref[1:2, :]
    length = bc_rows.shape[0]
    bc_pre = conv(bc_rows, cbc_ref, kernel)
    bc_sig = sigmoid(bc_pre)
    shared = bc_pre * bc_sig
    step = jnp.maximum(step_raw, 0.0) + jnp.log1p(jnp.exp(-jnp.abs(step_raw)))
    rate = -jnp.exp(head_ref[0:1, :])
    lower = (iota((length, length), 0) >= iota((length, length), 1)).astype(f32)
    cum = dot_exact(lower, step * rate)
    in_map = shared[:, :state].astype(bf16)
    out_map = shared[:, state:].astype(bf16)
    scores = dot(out_map, in_map, (1, 1)) * lower
    return dict(
        bc_rows=bc_rows,
        bc_pre=bc_pre,
        bc_sig=bc_sig,
        step_raw=step_raw,
        step=step,
        rate=rate,
        cum=cum,
        cum_t=cum.T,
        in_map=in_map,
        out_map=out_map,
        scores=scores,
    )


def pick(values, pair, first):
    return jnp.where(
        first, values[:, 2 * pair : 2 * pair + 1], values[:, 2 * pair + 1 : 2 * pair + 2]
    )


def blocks_of(length):
    half = length // 2
    return [((0, half), (0, half)), ((half, length), (0, length))]


def forward_kernel(
    x_ref, w_ref, taps_ref, cbc_ref, head_ref, proj_ref, y_ref, gated_ref, *, inner, state, kernel
):
    length = x_ref.shape[0]
    width = w_ref.shape[1]
    rows = x_ref[...]
    for start in range(0, width, 256):
        stop = min(width, start + 256)
        proj_ref[:, start:stop] = dot(rows, w_ref[:, start:stop])
    part = shared_parts(proj_ref, cbc_ref, head_ref, inner, state, kernel)
    step, cum, cum_t, scores = part["step"], part["cum"], part["cum_t"], part["scores"]
    first = iota((length, lanes), 1) < lanes // 2
    for pair in range(inner // lanes):
        cols = slice(pair * lanes, (pair + 1) * lanes)
        taps = taps_ref[:, cols]
        gate = proj_ref[:, cols]
        values = conv(
            proj_ref[:, inner + pair * lanes : inner + (pair + 1) * lanes], taps, kernel
        )
        values = values * sigmoid(values)
        scaled = values * pick(step, pair, first)
        halves = (
            jnp.where(first, scaled, 0.0).astype(bf16),
            jnp.where(first, 0.0, scaled).astype(bf16),
        )
        pieces = []
        for (r0, r1), (c0, c1) in blocks_of(length):
            total = None
            for side in range(2):
                head = 2 * pair + side
                gap = cum[r0:r1, head : head + 1] - cum_t[head : head + 1, c0:c1]
                weights = (scores[r0:r1, c0:c1] * jnp.exp(jnp.minimum(gap, 0.0))).astype(bf16)
                term = dot(weights, halves[side][c0:c1])
                total = term if total is None else total + term
            pieces.append(total)
        output = jnp.concatenate(pieces, axis=0)
        y_ref[:, cols] = output
        gated_ref[:, cols] = (output + taps[kernel + 2 : kernel + 3] * values) * (
            gate * sigmoid(gate)
        )


def gate_kernel(cot_ref, out_ref, gated_ref, taps_ref, grad_ref, stats_ref, branch_ref, *, kernel):
    gain = taps_ref[kernel + 1 : kernel + 2, :]
    weights = out_ref[...]
    grad = dot(cot_ref[...], weights, (1, 1))
    grad_ref[...] = grad
    gated = gated_ref[...]
    lifted = gated * gain
    branch_ref[...] = dot(lifted.astype(bf16), weights).astype(bf16)
    ones = jnp.ones((sub, gated.shape[1]), f32)
    squares = dot_exact(ones, gated * gated, (1, 1))
    cross = dot_exact(ones, grad * lifted, (1, 1))
    stats_ref[...] = jnp.where(iota(squares.shape, 0) == 0, squares, cross)


def backward_kernel(
    *refs, inner, state, kernel, inner_all, stat_parts
):
    stat_refs = refs[:stat_parts]
    (
        proj_ref,
        y_ref,
        grad_ref,
        taps_ref,
        cbc_ref,
        head_ref,
        cot_ref,
        normed_ref,
        tap_sums_ref,
        cbc_sums_ref,
        head_sums_ref,
        score_ref,
    ) = refs[stat_parts:]
    length = proj_ref.shape[0]
    half_lanes = lanes // 2

    @pl.when(pl.program_id(0) == 0)
    def clear():
        tap_sums_ref[...] = jnp.zeros(tap_sums_ref.shape, f32)
        cbc_sums_ref[...] = jnp.zeros(cbc_sums_ref.shape, f32)
        head_sums_ref[...] = jnp.zeros(head_sums_ref.shape, f32)

    stats = stat_refs[0][...]
    for more in stat_refs[1:]:
        stats = stats + more[...]
    unit = (iota((length, length), 0) == iota((length, length), 1)).astype(f32)
    columns = dot_exact(unit, stats, (1, 1))
    inv = lax.rsqrt(columns[:, 0:1] / inner_all + norm_eps)
    pull = inv * inv * inv * columns[:, 1:2] / inner_all

    part = shared_parts(proj_ref, cbc_ref, head_ref, inner, state, kernel)
    step, cum, cum_t, scores = part["step"], part["cum"], part["cum_t"], part["scores"]
    first = iota((length, lanes), 1) < half_lanes
    score_ref[...] = jnp.zeros(score_ref.shape, f32)
    cum_grad = jnp.zeros((length, lanes), f32)
    step_grad = jnp.zeros((length, lanes), f32)
    for pair in range(inner // lanes):
        cols = slice(pair * lanes, (pair + 1) * lanes)
        xcols = slice(inner + pair * lanes, inner + (pair + 1) * lanes)
        taps = taps_ref[:, cols]
        gain = taps[kernel + 1 : kernel + 2]
        skip = taps[kernel + 2 : kernel + 3]
        gate = proj_ref[:, cols]
        raw = proj_ref[:, xcols]
        pre = conv(raw, taps, kernel)
        pre_sig = sigmoid(pre)
        values = pre * pre_sig
        spread = pick(step, pair, first)
        scaled = values * spread
        gate_sig = sigmoid(gate)
        lift = gate * gate_sig
        plain = y_ref[:, cols]
        output = plain + skip * values
        gated = output * lift
        normed = gated * inv
        grad = grad_ref[:, cols]
        normed_ref[:, cols] = (normed * gain).astype(bf16)
        gain_row = jnp.sum(grad * normed, axis=0, keepdims=True)
        gated_grad = inv * (grad * gain) - gated * pull
        cot_ref[:, cols] = (
            gated_grad * output * (gate_sig * (1.0 + gate * (1.0 - gate_sig)))
        ).astype(bf16)
        out_grad = gated_grad * lift
        skip_row = jnp.sum(out_grad * values, axis=0, keepdims=True)
        out_low = out_grad.astype(bf16)
        scaled_low = scaled.astype(bf16)
        zero = jnp.zeros_like(out_low)
        sides = (jnp.where(first, out_low, zero), jnp.where(first, zero, out_low))
        half = length // 2
        pulled = [jnp.zeros((half, lanes), f32), jnp.zeros((half, lanes), f32)]
        for (r0, r1), (c0, c1) in blocks_of(length):
            score_sum = score_ref[r0:r1, c0:c1]
            for side in range(2):
                head = 2 * pair + side
                gap = cum[r0:r1, head : head + 1] - cum_t[head : head + 1, c0:c1]
                decay = jnp.exp(jnp.minimum(gap, 0.0))
                weights = (scores[r0:r1, c0:c1] * decay).astype(bf16)
                score_sum = score_sum + dot(sides[side][r0:r1], scaled_low[c0:c1], (1, 1)) * decay
                back = dot(weights, sides[side][r0:r1], (0, 0))
                pulled[0] = pulled[0] + back[:half]
                if c1 > half:
                    pulled[1] = pulled[1] + back[half:]
            score_ref[r0:r1, c0:c1] = score_sum
        scaled_grad = jnp.concatenate(pulled, axis=0)
        hot = (
            2 * pair + (iota((lanes, lanes), 0) >= half_lanes).astype(jnp.int32)
            == iota((lanes, lanes), 1)
        ).astype(f32)
        balance = out_low.astype(f32) * plain - scaled_low.astype(f32) * scaled_grad
        cum_grad = cum_grad + dot_exact(balance, hot)
        step_grad = step_grad + dot_exact(values * scaled_grad, hot)
        value_grad = skip * out_grad + scaled_grad * spread
        pre_grad = value_grad * (pre_sig * (1.0 + pre * (1.0 - pre_sig)))
        cot_ref[:, xcols] = conv_back(pre_grad, taps, kernel).astype(bf16)
        rows = conv_sums(pre_grad, raw, kernel) + [gain_row, skip_row]
        rows = rows + [jnp.zeros_like(gain_row)] * (tap_sums_ref.shape[0] - len(rows))
        tap_sums_ref[:, cols] = tap_sums_ref[:, cols] + jnp.concatenate(rows, axis=0)

    lower = iota((length, length), 0) >= iota((length, length), 1)
    score_low = jnp.where(lower, score_ref[...], 0.0).astype(bf16)
    shared_grad = jnp.concatenate(
        [dot(score_low, part["out_map"], (0, 0)), dot(score_low, part["in_map"])], axis=1
    )
    bc_pre, bc_sig = part["bc_pre"], part["bc_sig"]
    bc_grad = shared_grad * (bc_sig * (1.0 + bc_pre * (1.0 - bc_sig)))
    cot_ref[:, 2 * inner : 2 * inner + 2 * state] = conv_back(bc_grad, cbc_ref, kernel).astype(bf16)
    rows = conv_sums(bc_grad, part["bc_rows"], kernel)
    rows = rows + [jnp.zeros_like(rows[0])] * (cbc_sums_ref.shape[0] - len(rows))
    cbc_sums_ref[...] = cbc_sums_ref[...] + jnp.concatenate(rows, axis=0)
    decay_grad = dot_exact(lower.astype(f32), cum_grad, (0, 0))
    raw_grad = (step_grad + decay_grad * part["rate"]) * sigmoid(part["step_raw"])
    cot_ref[:, 2 * inner + 2 * state :] = raw_grad.astype(bf16)
    rows = [
        part["rate"] * jnp.sum(step * decay_grad, axis=0, keepdims=True),
        jnp.sum(raw_grad, axis=0, keepdims=True),
    ]
    rows = rows + [jnp.zeros_like(rows[0])] * (head_sums_ref.shape[0] - len(rows))
    head_sums_ref[...] = head_sums_ref[...] + jnp.concatenate(rows, axis=0)


def whole(array):
    return pl.BlockSpec(array.shape, lambda step: (0,) * array.ndim, pipeline_mode=pl.Buffered(1))


def rows_spec(length, width):
    return pl.BlockSpec((length, width), lambda step: (step, 0))


def stat_spec(length, slots, back):
    return pl.BlockSpec((sub, length), lambda step: (lax.rem(step + slots - back, slots), 0))


def call_params():
    return pltpu.CompilerParams(
        dimension_semantics=("arbitrary",), vmem_limit_bytes=56 * 1024 * 1024
    )


def run_forward(normed, weights, taps, cbc, head, seq_len, inner, state, kernel):
    rows, width = normed.shape[0], weights.shape[1]
    return pl.pallas_call(
        functools.partial(forward_kernel, inner=inner, state=state, kernel=kernel),
        grid=(rows // seq_len,),
        in_specs=[
            rows_spec(seq_len, normed.shape[1]),
            whole(weights),
            whole(taps),
            whole(cbc),
            whole(head),
        ],
        out_specs=[
            rows_spec(seq_len, width),
            rows_spec(seq_len, inner),
            rows_spec(seq_len, inner),
        ],
        out_shape=[
            jax.ShapeDtypeStruct((rows, width), f32),
            jax.ShapeDtypeStruct((rows, inner), f32),
            jax.ShapeDtypeStruct((rows, inner), f32),
        ],
        compiler_params=call_params(),
        name="mixer_forward",
    )(normed, weights, taps, cbc, head)


def run_gate(cot, out_full, gated, taps, seq_len, kernel):
    rows, inner = gated.shape
    slots = rows // seq_len
    return pl.pallas_call(
        functools.partial(gate_kernel, kernel=kernel),
        grid=(slots,),
        in_specs=[
            rows_spec(seq_len, cot.shape[1]),
            whole(out_full),
            rows_spec(seq_len, inner),
            whole(taps),
        ],
        out_specs=[
            rows_spec(seq_len, inner),
            rows_spec(sub, seq_len),
            rows_spec(seq_len, cot.shape[1]),
        ],
        out_shape=[
            jax.ShapeDtypeStruct((rows, inner), f32),
            jax.ShapeDtypeStruct((slots * sub, seq_len), f32),
            jax.ShapeDtypeStruct((rows, cot.shape[1]), bf16),
        ],
        compiler_params=call_params(),
        name="gate_products",
    )(cot, out_full, gated, taps)


def run_backward(stats, proj, plain, grad, taps, cbc, head, seq_len, inner, state, kernel, inner_all, turned):
    rows, width = proj.shape
    return pl.pallas_call(
        functools.partial(
            backward_kernel,
            inner=inner,
            state=state,
            kernel=kernel,
            inner_all=inner_all,
            stat_parts=len(stats),
        ),
        grid=(rows // seq_len,),
        in_specs=[stat_spec(seq_len, rows // seq_len, back if turned else 0) for back in range(len(stats))]
        + [
            rows_spec(seq_len, width),
            rows_spec(seq_len, inner),
            rows_spec(seq_len, inner),
            whole(taps),
            whole(cbc),
            whole(head),
        ],
        out_specs=[
            rows_spec(seq_len, width),
            rows_spec(seq_len, inner),
            pl.BlockSpec(taps.shape, lambda step: (0, 0)),
            pl.BlockSpec(cbc.shape, lambda step: (0, 0)),
            pl.BlockSpec(head.shape, lambda step: (0, 0)),
        ],
        out_shape=[
            jax.ShapeDtypeStruct((rows, width), bf16),
            jax.ShapeDtypeStruct((rows, inner), bf16),
            jax.ShapeDtypeStruct(taps.shape, f32),
            jax.ShapeDtypeStruct(cbc.shape, f32),
            jax.ShapeDtypeStruct(head.shape, f32),
        ],
        scratch_shapes=[pltpu.VMEM((seq_len, seq_len), f32)],
        compiler_params=call_params(),
        name="mixer_backward",
    )(*stats, proj, plain, grad, taps, cbc, head)


def adam_update(parameter, moments, gradient, learn_rate, decay_coef):
    first_mom = beta_one * moments[0] + (1.0 - beta_one) * gradient
    second_mom = beta_two * moments[1] * moments[1] + (1.0 - beta_two) * gradient * gradient
    second_root = jnp.sqrt(second_mom)
    first_hat = first_mom / (1.0 - beta_one**step_count)
    second_hat = second_mom / (1.0 - beta_two**step_count)
    updated = parameter - learn_rate * (
        first_hat / (jnp.sqrt(second_hat) + adam_eps) + decay_coef * parameter
    )
    return (updated, jnp.stack([first_mom, second_root]))


def shift_by(values, axis, count, amount):
    return lax.ppermute(values, axis, [(i, (i + amount) % count) for i in range(count)])


def swap_by(values, axis, count, mask):
    return lax.ppermute(values, axis, [(i, i ^ mask) for i in range(count)])


def pad_to(values, rows, cols):
    return jnp.pad(values, ((0, rows - values.shape[0]), (0, cols - values.shape[1])))


def gather_dp(piece, count):
    if count != 8:
        return lax.all_gather(piece, "dp", axis=0, tiled=True)
    rows = piece.shape[0]
    half = rows // 2
    place = lax.axis_index("dp")
    by_two = swap_by(piece, "dp", count, 2)
    by_four = swap_by(piece, "dp", count, 4)
    six_top = swap_by(by_two[:half], "dp", count, 4)
    six_low = swap_by(by_four[half:], "dp", count, 2)
    known = [(0, 0, piece), (2, 0, by_two), (4, 0, by_four), (6, 0, six_top), (6, half, six_low)]
    known = known + [
        (mask ^ 1, at, swap_by(values, "dp", count, 1)) for mask, at, values in known
    ]
    gathered = jnp.zeros((count * rows, piece.shape[1]), piece.dtype)
    for mask, at, values in known:
        gathered = lax.dynamic_update_slice(gathered, values, ((place ^ mask) * rows + at, 0))
    return gathered


def scatter_dp(full, count):
    if count != 8:
        return lax.psum_scatter(full, "dp", scatter_dimension=0, tiled=True).astype(f32)
    rows = full.shape[0] // count
    half = rows // 2
    place = lax.axis_index("dp")

    def piece(mask, start, size):
        return lax.dynamic_slice_in_dim(full, (place ^ mask) * rows + start, size, 0)

    def send(values, mask):
        return swap_by(values.astype(bf16), "dp", count, mask).astype(f32)

    def paired(mask, start, size):
        return piece(mask, start, size).astype(f32) + send(piece(mask ^ 1, start, size), 1)

    own = paired(0, 0, rows)
    six_top, six_low = paired(6, 0, half), paired(6, half, half)
    two_top, two_low = paired(2, 0, half), paired(2, half, half)
    four_top, four_low = paired(4, 0, half), paired(4, half, half)
    four_top = four_top + send(six_top, 2)
    two_low = two_low + send(six_low, 4)
    own_top = own[:half] + send(two_top, 2) + send(four_top, 4)
    own_low = own[half:] + send(two_low, 2) + send(four_low, 4)
    return jnp.concatenate([own_top, own_low], axis=0)


def sum_over(values, axis, count, keep_type=True):
    if count > 8:
        return lax.psum(values, axis)
    total = values
    for amount in range(1, count):
        total = total + shift_by(values, axis, count, amount)
    return total


def shards(
    block_input,
    seq_lengths,
    cotangent,
    norm_gain,
    proj_zx,
    proj_dt,
    proj_bc,
    chan_params,
    conv_bc,
    head_params,
    out_proj,
    gain_moments,
    zx_moments,
    dt_moments,
    bc_moments,
    chan_moments,
    convbc_moments,
    head_moments,
    out_moments,
):
    heads_axis = lax.axis_size("head")
    dp_axis = lax.axis_size("dp")
    slot_count = seq_lengths.shape[0]
    rows_own, model_width = block_input.shape
    rows_dev = rows_own * heads_axis
    seq_len = rows_dev // slot_count
    rows_dp = proj_zx.shape[0]
    inner = chan_params.shape[1]
    inner_all = inner * heads_axis
    heads_loc = head_params.shape[1]
    headdim = inner // heads_loc
    kernel = chan_params.shape[0] - 2
    state = conv_bc.shape[1] // 2
    place = lax.axis_index("head")
    whole_slots = rows_own == seq_len and heads_axis <= 4

    positions = iota((slot_count, seq_len), 1)
    live_mask = (positions < seq_lengths[:, None]).astype(f32).reshape(rows_dev, 1)
    live_own = lax.dynamic_slice_in_dim(live_mask, place * rows_own, rows_own, 0)
    gain_float = lax.optimization_barrier(norm_gain.astype(bf16)).astype(f32)
    input_float = block_input.astype(f32)
    inv_own = lax.rsqrt(jnp.mean(input_float * input_float, axis=-1, keepdims=True) + norm_eps)
    own_hat = input_float * inv_own
    normed_own = (own_hat * gain_float[None, :]).astype(bf16)
    cot_float = cotangent.astype(f32)
    cot_own = (cot_float * live_own).astype(bf16)

    def gather_head(own):
        if not whole_slots:
            return lax.all_gather(own, "head", axis=0, tiled=True)
        return jnp.concatenate(
            [own] + [shift_by(own, "head", heads_axis, k) for k in range(1, heads_axis)], axis=0
        )

    def scatter_head(full):
        if not whole_slots:
            return lax.psum_scatter(full, "head", scatter_dimension=0, tiled=True).astype(f32)
        total = full[:rows_own].astype(f32)
        for k in range(1, heads_axis):
            piece = full[k * rows_own : (k + 1) * rows_own]
            total = total + shift_by(piece, "head", heads_axis, heads_axis - k).astype(f32)
        return total

    piece_in = jnp.concatenate(
        [
            proj_zx.astype(bf16).reshape(rows_dp, 2 * inner),
            proj_bc.astype(bf16),
            pad_to(proj_dt.astype(bf16), rows_dp, lanes),
        ],
        axis=1,
    )
    normed_all = gather_head(normed_own)
    weights_in = gather_dp(piece_in, dp_axis)
    out_full = gather_dp(out_proj.astype(bf16), dp_axis)
    cot_all = gather_head(cot_own)

    taps = pad_to(
        jnp.concatenate([chan_params, jnp.repeat(head_params[2:3], headdim, axis=1)], axis=0),
        sub,
        inner,
    )
    cbc = pad_to(conv_bc, sub, 2 * state)
    head_table = pad_to(head_params, sub, lanes)

    proj, plain, gated = run_forward(
        normed_all, weights_in, taps, cbc, head_table, seq_len, inner, state, kernel
    )
    grad_normed, stats, branch = run_gate(cot_all, out_full, gated, taps, seq_len, kernel)
    if heads_axis <= 4:
        stat_parts = [stats] + [shift_by(stats, "head", heads_axis, k) for k in range(1, heads_axis)]
    else:
        stat_parts = [lax.psum(stats, "head")]
    cot_proj, normed_out, tap_sums, cbc_sums, head_sums = run_backward(
        stat_parts,
        proj,
        plain,
        grad_normed,
        taps,
        cbc,
        head_table,
        seq_len,
        inner,
        state,
        kernel,
        inner_all,
        whole_slots,
    )
    grad_out = dot(normed_out, cot_all, (0, 0)).astype(bf16)
    grad_in = dot(normed_all, cot_proj, (0, 0)).astype(bf16)
    cot_input = dot(cot_proj, weights_in, (1, 1))
    grad_gain = jnp.sum(cot_input * normed_all.astype(f32), axis=0)
    cot_input = cot_input.astype(bf16)

    if whole_slots:
        square_own = stat_parts[0][:1]
        for k in range(1, heads_axis):
            at = (heads_axis - k) * sub
            square_own = square_own + stat_parts[k][at : at + 1]
        gate_own = lax.rsqrt(square_own / inner_all + norm_eps).reshape(rows_own, 1)
    else:
        total = sum(stat_parts).reshape(slot_count, sub, seq_len)[:, 0].reshape(rows_dev, 1)
        gate_own = lax.rsqrt(
            lax.dynamic_slice_in_dim(total, place * rows_own, rows_own, 0) / inner_all + norm_eps
        )
    branch_own = scatter_head(branch) * gate_own
    block_output = (input_float + live_own * branch_own).astype(bf16)
    cot_whole = scatter_head(cot_input)
    lifted = cot_whole * gain_float[None, :]
    row_dot = jnp.sum(lifted * own_hat, axis=-1, keepdims=True)
    input_grad = cot_float + inv_own * (lifted - own_hat * row_dot / model_width)

    grad_out = scatter_dp(grad_out, dp_axis)
    grad_in = scatter_dp(grad_in, dp_axis)
    grad_zx = grad_in[:, : 2 * inner].reshape(rows_dp, 2, inner)
    grad_bc = grad_in[:, 2 * inner : 2 * inner + 2 * state]
    grad_dt = grad_in[:, 2 * inner + 2 * state :][:, :heads_loc]
    if heads_axis <= 4:
        grad_bc = grad_bc + sum(
            shift_by(grad_bc.astype(bf16), "head", heads_axis, k).astype(f32)
            for k in range(1, heads_axis)
        )
    else:
        grad_bc = lax.psum(grad_bc.astype(bf16), "head").astype(f32)

    both = jnp.concatenate([cbc_sums.reshape(-1, lanes), grad_gain.reshape(-1, lanes)], axis=0)
    both_rows = both.shape[0]
    small = jnp.concatenate([both, tap_sums.reshape(-1, lanes), head_sums], axis=0)
    small = sum_over(small, "dp", dp_axis)
    both = sum_over(small[:both_rows], "head", heads_axis)
    cbc_rows = sub * 2 * state // lanes
    grad_convbc = both[:cbc_rows].reshape(sub, 2 * state)[: kernel + 1]
    grad_gain = both[cbc_rows:].reshape(model_width) / gain_float
    tap_rows = sub * inner // lanes
    tap_sums = small[both_rows : both_rows + tap_rows].reshape(sub, inner)
    head_sums = small[both_rows + tap_rows :]
    grad_chan = tap_sums[: kernel + 2]
    grad_skip = jnp.sum(tap_sums[kernel + 2].reshape(heads_loc, headdim), axis=1)
    grad_head = jnp.concatenate([head_sums[:2, :heads_loc], grad_skip[None, :]], axis=0)

    gain_next, gain_state = adam_update(norm_gain, gain_moments, grad_gain, rate_vector, 0.0)
    zx_next, zx_state = adam_update(proj_zx, zx_moments, grad_zx, rate_matrix, weight_decay)
    dt_next, dt_state = adam_update(proj_dt, dt_moments, grad_dt, rate_matrix, weight_decay)
    bc_next, bc_state = adam_update(proj_bc, bc_moments, grad_bc, rate_matrix, weight_decay)
    chan_next, chan_state = adam_update(chan_params, chan_moments, grad_chan, rate_vector, 0.0)
    convbc_next, convbc_state = adam_update(conv_bc, convbc_moments, grad_convbc, rate_vector, 0.0)
    head_next, head_state = adam_update(head_params, head_moments, grad_head, rate_vector, 0.0)
    outproj_next, outproj_state = adam_update(
        out_proj, out_moments, grad_out, rate_matrix, weight_decay
    )
    return (
        block_output,
        input_grad,
        gain_next,
        gain_state,
        zx_next,
        zx_state,
        dt_next,
        dt_state,
        bc_next,
        bc_state,
        chan_next,
        chan_state,
        convbc_next,
        convbc_state,
        head_next,
        head_state,
        outproj_next,
        outproj_state,
    )


def solution(mesh):
    placed = (
        P(("dp", "head"), None),
        P("dp"),
        P(("dp", "head"), None),
        P(),
        P("dp", None, "head"),
        P("dp", "head"),
        P("dp", None),
        P(None, "head"),
        P(),
        P(None, "head"),
        P(("head", "dp"), None),
        P(),
        P(None, "dp", None, "head"),
        P(None, "dp", "head"),
        P(None, "dp", None),
        P(None, None, "head"),
        P(),
        P(None, None, "head"),
        P(None, ("head", "dp"), None),
    )
    return jax.shard_map(
        shards,
        mesh=mesh,
        in_specs=placed,
        out_specs=(
            P(("dp", "head"), None),
            P(("dp", "head"), None),
            P(),
            P(),
            P("dp", None, "head"),
            P(None, "dp", None, "head"),
            P("dp", "head"),
            P(None, "dp", "head"),
            P("dp", None),
            P(None, "dp", None),
            P(None, "head"),
            P(None, None, "head"),
            P(),
            P(),
            P(None, "head"),
            P(None, None, "head"),
            P(("head", "dp"), None),
            P(None, ("head", "dp"), None),
        ),
        check_vma=False,
    )
```

time: 721 us -> 514 us (0.71)
  waiting for transfers between devices: 343 us -> 197 us
  starting transfers between devices: 0.4 us -> 114 us
  matrix products: 125 us -> 20.2 us
  blocking collectives: 80.3 us -> 0 us
  Pallas kernels: 0 us -> 58.4 us
  local copies, waits for them, and re-layouts: 73.4 us -> 52.4 us
  other arithmetic: 75.3 us -> 60.3 us
  between operations: 15 us -> 2.08 us
    ppermute x0 -> x72, waiting for transfers between devices: none -> 197 us  [the longest x28 168 us: shift_by(): lax.ppermute(values, axis, [(i, (i + amount) % count) for i in range(coun...]
    psum x1 -> x0, waiting for transfers between devices: 123 us -> none  [shards(): lax.psum(cot_input.astype(jnp.bfloat16), 'head').astype(jnp.float32)]
    reduce_scatter x4 -> x0, waiting for transfers between devices: 116 us -> none  [the longest x1 52.5 us: shards(): lax.psum_scatter(jnp.dot(normed_out, out_full, preferred_element_type=jnp...]
    ppermute x0 -> x72, starting transfers between devices: none -> 114 us  [the longest x28 86.4 us: shift_by(): lax.ppermute(values, axis, [(i, (i + amount) % count) for i in range(coun...]
    dot_general x56 -> x3, matrix products: 125 us -> 20.2 us  [dot(): lax.dot_general(lhs, rhs, (((over[0],), (over[1],)), ((), ())), preferred...]
    all_gather x4 -> x0, waiting for transfers between devices: 93.7 us -> none  [the longest x1 40.8 us: shards(): input_all = lax.all_gather(block_input, 'head', axis=0, tiled=True)]
    pallas_call x0 -> x3, Pallas kernels: none -> 58.4 us  [the longest x1 26.1 us: run_backward(): pl.pallas_call(functools.partial(backward_kernel, inner=inner, state=stat...]
    psum x4 -> x0, blocking collectives: 58.2 us -> none  [the longest x1 25.3 us: shards(): lax.psum((grad_gain, grad_chan, slot_grads[2], slot_grads[1]), 'dp')]
  transfers between devices with their start and end apart: 10 -> 72, of which waited for: 9 -> 21; matrix products, arithmetic and copies ran while one was open for 21% -> 21% of each run, Pallas kernels for 0% -> 0%
where the time goes in v1:
time: 514 us; the launch traced here: 504 us
  waiting for transfers between devices  197 us (38%)
  starting transfers between devices  114 us (22%)
  other arithmetic  60.3 us (12%)
  Pallas kernels  58.4 us (11%)
  local copies, waits for them, and re-layouts  52.4 us (10%)
  matrix products  20.2 us (4%)
    ppermute x28, waiting for transfers between devices, shift_by(): lax.ppermute(values, axis, [(i, (i + amount) % count) for i in range(coun...  168 us
    ppermute x28, starting transfers between devices, shift_by(): lax.ppermute(values, axis, [(i, (i + amount) % count) for i in range(coun...  86.4 us
    ppermute x44, waiting for transfers between devices, swap_by(): return lax.ppermute(values, axis, [(i, i ^ mask) for i in range(count)])  28.8 us
    ppermute x44, starting transfers between devices, swap_by(): return lax.ppermute(values, axis, [(i, i ^ mask) for i in range(count)])  27.1 us
    pallas_call x1, Pallas kernels, run_backward(): pl.pallas_call(functools.partial(backward_kernel, inner=inner, state=stat...  26.1 us
    dot_general x3, matrix products, dot(): lax.dot_general(lhs, rhs, (((over[0],), (over[1],)), ((), ())), preferred...  20.2 us
    pallas_call x1, Pallas kernels, run_forward(): pl.pallas_call(functools.partial(forward_kernel, inner=inner, state=state...  18.8 us
    pallas_call x1, Pallas kernels, run_gate(): pl.pallas_call(functools.partial(gate_kernel, kernel=kernel), grid=(slots...  13.6 us
  transfers between devices with their start and end apart: 72, of which 21 were waited for; matrix products, arithmetic and copies ran while one was open for 21% of the time, Pallas kernels for 0%

profile of v1, /device:TPU:0, one launch (start us, length us, event | category | flops | bytes accessed | tf_op | source)
XLA Modules:
  0.0 504.2 jit_solution(4894389506472272309)
XLA Ops:
  2.7 2.9 broadcast_in_dim.20
  6.8 3.0 collective-permute-start.15
  28.6 4.3 collective-permute-done.3
  42.4 3.6 collective-permute-done.6
  49.2 2.6 collective-permute-start.13
  56.5 2.8 collective-permute-start.2
  63.4 24.9 %collective-permute-done.13 = bf16[256,1536]{1,0:T(8,128)(2,1)S(1)} collective-permute-done((bf16[256,1536]{1,0:T(8,128)(2,1)S(1)}, bf16[256,1536]{1,0:T(8,128)(2,1)S(1)}, u32[]{:S(2)}, u32[]{:S(2)}) %collective-permute-start.13) | collective-permute-done | bytes 786464 | tf_op jit(solution)/shard_map/ppermute | solution.py:433
  88.3 17.5 %collective-permute-done.14 = bf16[256,1536]{1,0:T(8,128)(2,1)S(1)} collective-permute-done((bf16[256,1536]{1,0:T(8,128)(2,1)S(1)}, bf16[256,1536]{1,0:T(8,128)(2,1)S(1)}, u32[]{:S(2)}, u32[]{:S(2)}) %collective-permute-start.14) | collective-permute-done | bytes 786464 | tf_op jit(solution)/shard_map/ppermute | solution.py:433
  110.7 44.2 %collective-permute-done.1 = bf16[256,1536]{1,0:T(8,128)(2,1)S(1)} collective-permute-done((bf16[256,1536]{1,0:T(8,128)(2,1)S(1)}, bf16[256,1536]{1,0:T(8,128)(2,1)S(1)}, u32[]{:S(2)}, u32[]{:S(2)}) %collective-permute-start.1) | collective-permute-done | bytes 786464 | tf_op jit(solution)/shard_map/ppermute | solution.py:433
  163.8 18.8 %mixer_forward.1 = (f32[1024,1920]{1,0:T(8,128)}, f32[1024,768]{1,0:T(8,128)}, f32[1024,768]{1,0:T(8,128)}) custom-call(bf16[1024,1536]{1,0:T(8,128)(2,1)} %pad_maximum_fusion.1.x_ref, bf16[1536,1920]{1,0:T(8,128)(2,1)} %constant_dynamic-update-slice_fusion.w_ref, f32[8,768]{1,0:T(8,128)} %select_maximum_fusion.taps_ref.refs_7_, ...), custom_call_target="tpu_custom_call" | custom-call | tf_op jit(solution)/shard_map/mixer_forward/pallas_call | solution.py:327
  182.6 13.6 %gate_products.1 = (f32[1024,768]{1,0:T(8,128)}, f32[32,256]{1,0:T(8,128)}, bf16[1024,1536]{1,0:T(8,128)(2,1)}) custom-call(bf16[1024,1536]{1,0:T(8,128)(2,1)} %pad_maximum_fusion.cot_ref, bf16[768,1536]{1,0:T(8,128)(2,1)} %copy-done.2, f32[1024,768]{1,0:T(8,128)} %get-tuple-element.29.gated_ref, f32[8,768]{1,0:T(8,128)} %select_maximum_fusion.taps_ref.refs_7_), custom_call_target="tpu_custom_call" | custom-call | tf_op jit(solution)/shard_map/gate_products/pallas_call | solution.py:355
  196.1 17.0 %collective-permute-start.27 = (f32[32,256]{1,0:T(8,128)}, f32[32,256]{1,0:T(8,128)S(1)}, u32[]{:S(2)}, u32[]{:S(2)}) collective-permute-start(f32[32,256]{1,0:T(8,128)} %get-tuple-element.31.refs_0_), channel_id=1, source_target_pairs={{0,1},{1,2},{2,3},{3,0},{4,5},{5,6},{6,7},{7,4},{8,9},{9,10},{10,1... | collective-permute-start | bytes 98312 | tf_op jit(solution)/shard_map/ppermute | solution.py:433
  215.7 2.7 fusion.80
  219.9 26.1 %mixer_backward.1 = (bf16[1024,1920]{1,0:T(8,128)(2,1)}, bf16[1024,768]{1,0:T(8,128)(2,1)}, f32[8,768]{1,0:T(8,128)}, f32[8,256]{1,0:T(8,128)}, f32[8,128]{1,0:T(8,128)}) custom-call(f32[32,256]{1,0:T(8,128)} %get-tuple-element.31.refs_0_, f32[32,256]{1,0:T(8,128)} %copy-done.45, f32[32,256]{1,0:T(8,128)} %copy-done.46, f32[32,256]{1,0:T(8,128)} %copy-done.47, ...), custom_call_target="tpu_custom_call" | custom-call | tf_op jit(solution)/shard_map/mixer_backward/pallas_call | solution.py:381
  247.5 10.5 %multiply_reduce_fusion = (f32[1536]{0:T(1024)S(1)}, bf16[1024,1536]{1,0:T(8,128)(2,1)S(1)}) fusion(bf16[256,1536]{1,0:T(8,128)(2,1)} %copy-done.23, bf16[256,1536]{1,0:T(8,128)(2,1)} %copy-done.21, bf16[256,1536]{1,0:T(8,128)(2,1)} %copy-done.19, bf16[256,1536]{1,0:T(8,128)(2,1)S(1)} %copy-done.9, bf16[1024,1920]{1,0:T(8,128)(2,1)} %get-tuple-element.35, ...), kind=kOutput, calls=%fused_computation.1 | convolution fusion | flops 6057097728 | bytes 16128000 | tf_op jit(solution)/shard_map/dot_general | solution.py:25
  260.3 2.5 collective-permute-start.35
  263.5 2.9 convolution_convert_fusion.1
  271.3 6.8 %convolution_convert_fusion = bf16[1536,1920]{0,1:T(8,128)(2,1)S(1)} fusion(bf16[1024,1920]{1,0:T(8,128)(2,1)S(1)} %copy-done.61, bf16[256,1536]{1,0:T(8,128)(2,1)S(1)} %copy-done.24, bf16[256,1536]{1,0:T(8,128)(2,1)S(1)} %copy-done.22, bf16[256,1536]{1,0:T(8,128)(2,1)S(1)} %copy-done.20, bf16[256,1536]{1,0:T(8,128)(2,1)S(1)} %copy-done.9), kind=kOutput, calls=%fused_computation | convolution fusion | flops 6055329792 | bytes 12976128 | tf_op jit(solution)/shard_map/dot_general | solution.py:25
  278.1 3.2 constant_dynamic-slice_fusion.9
  332.8 4.3 collective-permute-done.52
  337.1 3.8 add_convert_fusion.1
  343.9 4.9 collective-permute-done.30
  348.7 3.5 collective-permute-start.24
  352.3 47.9 %collective-permute-done.31 = bf16[256,1536]{1,0:T(8,128)(2,1)S(1)} collective-permute-done((bf16[256,1536]{1,0:T(8,128)(2,1)}, bf16[256,1536]{1,0:T(8,128)(2,1)S(1)}, u32[]{:S(2)}, u32[]{:S(2)}) %collective-permute-start.31) | collective-permute-done | bytes 786464 | tf_op jit(solution)/shard_map/ppermute | solution.py:433
  400.2 33.1 %collective-permute-start.26 = (bf16[256,1536]{1,0:T(8,128)(2,1)S(1)}, bf16[256,1536]{1,0:T(8,128)(2,1)S(1)}, u32[]{:S(2)}, u32[]{:S(2)}) collective-permute-start(bf16[256,1536]{1,0:T(8,128)(2,1)S(1)} %get-tuple-element.158), channel_id=1, source_target_pairs={{0,1},{1,2},{2,3},{3,0},{4,5},{5,6},{6,7},{7,4},{8,9},{9,10},{10,1... | collective-permute-start | bytes 2359304 | tf_op jit(solution)/shard_map/ppermute | solution.py:433
  439.0 28.1 %collective-permute-done.25 = bf16[256,1536]{1,0:T(8,128)(2,1)S(1)} collective-permute-done((bf16[256,1536]{1,0:T(8,128)(2,1)S(1)}, bf16[256,1536]{1,0:T(8,128)(2,1)S(1)}, u32[]{:S(2)}, u32[]{:S(2)}) %collective-permute-start.25) | collective-permute-done | bytes 786464 | tf_op jit(solution)/shard_map/ppermute | solution.py:433
  468.4 3.8 convert_add_fusion.2
  472.2 7.6 %collective-permute-done.49 = bf16[96,1920]{0,1:T(8,128)(2,1)S(1)} collective-permute-done((bf16[96,1920]{0,1:T(8,128)(2,1)S(1)}, bf16[96,1920]{0,1:T(8,128)(2,1)S(1)}, u32[]{:S(2)}, u32[]{:S(2)}) %collective-permute-start.49) | collective-permute-done | bytes 368672 | tf_op jit(solution)/shard_map/ppermute | solution.py:437
  481.1 3.7 collective-permute-start.58
  488.9 4.0 multiply_add_fusion
  492.9 4.6 multiply_subtract_fusion
  497.4 2.5 pad_maximum_fusion.2
  (373 shorter events, 141.0 us)
Async XLA Ops:
  6.8 46.4 %collective-permute-start.15 = (bf16[192,1920]{1,0:T(8,128)(2,1)}, bf16[192,1920]{1,0:T(8,128)(2,1)}, u32[]{:S(2)}, u32[]{:S(2)}) collective-permute-start(bf16[192,1920]{1,0:T(8,128)(2,1)} %get-tuple-element.178), channel_id=1, source_target_pairs={{0,8},{4,12},{8,0},{12,4},{16,24},{20,28},{24,16},{28,20},{1,9},{5... | collective-permute-start | bytes 2211848 | tf_op jit(solution)/shard_map/ppermute | solution.py:437
  9.8 45.2 %collective-permute-start.16 = (bf16[192,1920]{1,0:T(8,128)(2,1)}, bf16[192,1920]{1,0:T(8,128)(2,1)}, u32[]{:S(2)}, u32[]{:S(2)}) collective-permute-start(bf16[192,1920]{1,0:T(8,128)(2,1)} %get-tuple-element.178), channel_id=1, source_target_pairs={{0,16},{4,20},{8,24},{12,28},{16,0},{20,4},{24,8},{28,12},{1,17},{... | collective-permute-start | bytes 2211848 | tf_op jit(solution)/shard_map/ppermute | solution.py:437
  13.3 19.6 %collective-permute-start.3 = (bf16[96,1536]{1,0:T(8,128)(2,1)}, bf16[96,1536]{1,0:T(8,128)(2,1)}, u32[]{:S(2)}, u32[]{:S(2)}) collective-permute-start(bf16[96,1536]{1,0:T(8,128)(2,1)} %get-tuple-element.139), channel_id=1, source_target_pairs={{0,8},{4,12},{8,0},{12,4},{16,24},{20,28},{24,16},{28,20},{1,9},{5... | collective-permute-start | bytes 884744 | tf_op jit(solution)/shard_map/ppermute | solution.py:437
  13.9 21.8 %collective-permute-start.4 = (bf16[96,1536]{1,0:T(8,128)(2,1)}, bf16[96,1536]{1,0:T(8,128)(2,1)}, u32[]{:S(2)}, u32[]{:S(2)}) collective-permute-start(bf16[96,1536]{1,0:T(8,128)(2,1)} %get-tuple-element.139), channel_id=1, source_target_pairs={{0,16},{4,20},{8,24},{12,28},{16,0},{20,4},{24,8},{28,12},{1,17},{... | collective-permute-start | bytes 884744 | tf_op jit(solution)/shard_map/ppermute | solution.py:437
  13.9 32.1 %collective-permute-start.7 = (bf16[96,1536]{1,0:T(8,128)(2,1)}, bf16[96,1536]{1,0:T(8,128)(2,1)}, u32[]{:S(2)}, u32[]{:S(2)}) collective-permute-start(bf16[96,1536]{1,0:T(8,128)(2,1)} %get-tuple-element.139), channel_id=1, source_target_pairs={{0,4},{4,0},{8,12},{12,8},{16,20},{20,16},{24,28},{28,24},{1,5},{5... | collective-permute-start | bytes 884744 | tf_op jit(solution)/shard_map/ppermute | solution.py:437
  32.9 23.5 %collective-permute-start.12 = (bf16[256,1536]{1,0:T(8,128)(2,1)}, bf16[256,1536]{1,0:T(8,128)(2,1)S(1)}, u32[]{:S(2)}, u32[]{:S(2)}) collective-permute-start(bf16[256,1536]{1,0:T(8,128)(2,1)} %fusion.4), channel_id=1, source_target_pairs={{0,1},{1,2},{2,3},{3,0},{4,5},{5,6},{6,7},{7,4},{8,9},{9,10},{10,1... | collective-permute-start | bytes 2359304 | tf_op jit(solution)/shard_map/ppermute | solution.py:433
  49.2 39.1 %collective-permute-start.13 = (bf16[256,1536]{1,0:T(8,128)(2,1)S(1)}, bf16[256,1536]{1,0:T(8,128)(2,1)S(1)}, u32[]{:S(2)}, u32[]{:S(2)}) collective-permute-start(bf16[256,1536]{1,0:T(8,128)(2,1)S(1)} %copy-done.8), channel_id=1, source_target_pairs={{0,2},{1,3},{2,0},{3,1},{4,6},{5,7},{6,4},{7,5},{8,10},{9,11},{10,... | collective-permute-start | bytes 2359304 | tf_op jit(solution)/shard_map/ppermute | solution.py:433
  51.8 53.9 %collective-permute-start.14 = (bf16[256,1536]{1,0:T(8,128)(2,1)S(1)}, bf16[256,1536]{1,0:T(8,128)(2,1)S(1)}, u32[]{:S(2)}, u32[]{:S(2)}) collective-permute-start(bf16[256,1536]{1,0:T(8,128)(2,1)S(1)} %copy-done.8), channel_id=1, source_target_pairs={{0,3},{1,0},{2,1},{3,2},{4,7},{5,4},{6,5},{7,6},{8,11},{9,8},{10,9... | collective-permute-start | bytes 2359304 | tf_op jit(solution)/shard_map/ppermute | solution.py:433
  53.2 55.9 %collective-permute-start = (bf16[256,1536]{1,0:T(8,128)(2,1)S(1)}, bf16[256,1536]{1,0:T(8,128)(2,1)S(1)}, u32[]{:S(2)}, u32[]{:S(2)}) collective-permute-start(bf16[256,1536]{1,0:T(8,128)(2,1)S(1)} %copy-done.10), channel_id=1, source_target_pairs={{0,1},{1,2},{2,3},{3,0},{4,5},{5,6},{6,7},{7,4},{8,9},{9,10},{10,1... | collective-permute-start | bytes 2359304 | tf_op jit(solution)/shard_map/ppermute | solution.py:433
  55.0 99.9 %collective-permute-start.1 = (bf16[256,1536]{1,0:T(8,128)(2,1)S(1)}, bf16[256,1536]{1,0:T(8,128)(2,1)S(1)}, u32[]{:S(2)}, u32[]{:S(2)}) collective-permute-start(bf16[256,1536]{1,0:T(8,128)(2,1)S(1)} %copy-done.10), channel_id=1, source_target_pairs={{0,2},{1,3},{2,0},{3,1},{4,6},{5,7},{6,4},{7,5},{8,10},{9,11},{10,... | collective-permute-start | bytes 2359304 | tf_op jit(solution)/shard_map/ppermute | solution.py:433
  56.5 98.4 %collective-permute-start.2 = (bf16[256,1536]{1,0:T(8,128)(2,1)S(1)}, bf16[256,1536]{1,0:T(8,128)(2,1)S(1)}, u32[]{:S(2)}, u32[]{:S(2)}) collective-permute-start(bf16[256,1536]{1,0:T(8,128)(2,1)S(1)} %copy-done.10), channel_id=1, source_target_pairs={{0,3},{1,0},{2,1},{3,2},{4,7},{5,4},{6,5},{7,6},{8,11},{9,8},{10,9... | collective-permute-start | bytes 2359304 | tf_op jit(solution)/shard_map/ppermute | solution.py:433
  88.3 71.2 %collective-permute-start.19 = (bf16[192,1920]{1,0:T(8,128)(2,1)}, bf16[192,1920]{1,0:T(8,128)(2,1)S(1)}, u32[]{:S(2)}, u32[]{:S(2)}) collective-permute-start(bf16[192,1920]{1,0:T(8,128)(2,1)} %get-tuple-element.178), channel_id=1, source_target_pairs={{0,4},{4,0},{8,12},{12,8},{16,20},{20,16},{24,28},{28,24},{1,5},{5... | collective-permute-start | bytes 2211848 | tf_op jit(solution)/shard_map/ppermute | solution.py:437
  105.7 51.6 %collective-permute-start.17 = (bf16[96,1920]{1,0:T(8,128)(2,1)S(1)}, bf16[96,1920]{1,0:T(8,128)(2,1)S(1)}, u32[]{:S(2)}, u32[]{:S(2)}) collective-permute-start(bf16[96,1920]{1,0:T(8,128)(2,1)S(1)} %slice.221), channel_id=1, source_target_pairs={{0,16},{4,20},{8,24},{12,28},{16,0},{20,4},{24,8},{28,12},{1,17},{... | collective-permute-start | bytes 1105928 | tf_op jit(solution)/shard_map/ppermute | solution.py:437
  109.1 48.4 %collective-permute-start.18 = (bf16[96,1920]{1,0:T(8,128)(2,1)S(1)}, bf16[96,1920]{1,0:T(8,128)(2,1)S(1)}, u32[]{:S(2)}, u32[]{:S(2)}) collective-permute-start(bf16[96,1920]{1,0:T(8,128)(2,1)S(1)} %slice.222), channel_id=1, source_target_pairs={{0,8},{4,12},{8,0},{12,4},{16,24},{20,28},{24,16},{28,20},{1,9},{5... | collective-permute-start | bytes 1105928 | tf_op jit(solution)/shard_map/ppermute | solution.py:437
  196.1 22.2 %collective-permute-start.27 = (f32[32,256]{1,0:T(8,128)}, f32[32,256]{1,0:T(8,128)S(1)}, u32[]{:S(2)}, u32[]{:S(2)}) collective-permute-start(f32[32,256]{1,0:T(8,128)} %get-tuple-element.31.refs_0_), channel_id=1, source_target_pairs={{0,1},{1,2},{2,3},{3,0},{4,5},{5,6},{6,7},{7,4},{8,9},{9,10},{10,1... | collective-permute-start | bytes 98312 | tf_op jit(solution)/shard_map/ppermute | solution.py:433
  258.8 23.2 %collective-permute-start.33 = (f32[84,128]{1,0:T(8,128)}, f32[84,128]{1,0:T(8,128)}, u32[]{:S(2)}, u32[]{:S(2)}) collective-permute-start(f32[84,128]{1,0:T(8,128)} %pad_maximum_fusion.9), channel_id=1, source_target_pairs={{0,4},{4,8},{8,12},{12,16},{16,20},{20,24},{24,28},{28,0},{1,5},{5... | collective-permute-start | bytes 129032 | tf_op jit(solution)/shard_map/ppermute | solution.py:433
  258.8 24.6 %collective-permute-start.34 = (f32[84,128]{1,0:T(8,128)}, f32[84,128]{1,0:T(8,128)}, u32[]{:S(2)}, u32[]{:S(2)}) collective-permute-start(f32[84,128]{1,0:T(8,128)} %pad_maximum_fusion.9), channel_id=1, source_target_pairs={{0,8},{4,12},{8,16},{12,20},{16,24},{20,28},{24,0},{28,4},{1,9},{5... | collective-permute-start | bytes 129032 | tf_op jit(solution)/shard_map/ppermute | solution.py:433
  260.3 28.3 %collective-permute-start.35 = (f32[84,128]{1,0:T(8,128)}, f32[84,128]{1,0:T(8,128)}, u32[]{:S(2)}, u32[]{:S(2)}) collective-permute-start(f32[84,128]{1,0:T(8,128)} %pad_maximum_fusion.9), channel_id=1, source_target_pairs={{0,12},{4,16},{8,20},{12,24},{16,28},{20,0},{24,4},{28,8},{1,13},{... | collective-permute-start | bytes 129032 | tf_op jit(solution)/shard_map/ppermute | solution.py:433
  262.7 25.8 %collective-permute-start.36 = (f32[84,128]{1,0:T(8,128)}, f32[84,128]{1,0:T(8,128)}, u32[]{:S(2)}, u32[]{:S(2)}) collective-permute-start(f32[84,128]{1,0:T(8,128)} %pad_maximum_fusion.9), channel_id=1, source_target_pairs={{0,16},{4,20},{8,24},{12,28},{16,0},{20,4},{24,8},{28,12},{1,17},{... | collective-permute-start | bytes 129032 | tf_op jit(solution)/shard_map/ppermute | solution.py:433
  263.2 25.9 %collective-permute-start.37 = (f32[84,128]{1,0:T(8,128)}, f32[84,128]{1,0:T(8,128)}, u32[]{:S(2)}, u32[]{:S(2)}) collective-permute-start(f32[84,128]{1,0:T(8,128)} %pad_maximum_fusion.9), channel_id=1, source_target_pairs={{0,20},{4,24},{8,28},{12,0},{16,4},{20,8},{24,12},{28,16},{1,21},{... | collective-permute-start | bytes 129032 | tf_op jit(solution)/shard_map/ppermute | solution.py:433
  328.4 105.6 %collective-permute-start.46 = (bf16[96,1920]{0,1:T(8,128)(2,1)}, bf16[96,1920]{0,1:T(8,128)(2,1)S(1)}, u32[]{:S(2)}, u32[]{:S(2)}) collective-permute-start(bf16[96,1920]{0,1:T(8,128)(2,1)} %get-tuple-element.150), channel_id=1, source_target_pairs={{0,4},{4,0},{8,12},{12,8},{16,20},{20,16},{24,28},{28,24},{1,5},{5... | collective-permute-start | bytes 1105928 | tf_op jit(solution)/shard_map/ppermute | solution.py:437
  328.5 20.3 %collective-permute-start.30 = (bf16[256,1536]{1,0:T(8,128)(2,1)}, bf16[256,1536]{1,0:T(8,128)(2,1)S(1)}, u32[]{:S(2)}, u32[]{:S(2)}) collective-permute-start(bf16[256,1536]{1,0:T(8,128)(2,1)} %get-tuple-element.154), channel_id=1, source_target_pairs={{0,3},{1,0},{2,1},{3,2},{4,7},{5,4},{6,5},{7,6},{8,11},{9,8},{10,9... | collective-permute-start | bytes 2359304 | tf_op jit(solution)/shard_map/ppermute | solution.py:433
  329.7 70.5 %collective-permute-start.31 = (bf16[256,1536]{1,0:T(8,128)(2,1)}, bf16[256,1536]{1,0:T(8,128)(2,1)S(1)}, u32[]{:S(2)}, u32[]{:S(2)}) collective-permute-start(bf16[256,1536]{1,0:T(8,128)(2,1)} %get-tuple-element.156), channel_id=1, source_target_pairs={{0,2},{1,3},{2,0},{3,1},{4,6},{5,7},{6,4},{7,5},{8,10},{9,11},{10,... | collective-permute-start | bytes 2359304 | tf_op jit(solution)/shard_map/ppermute | solution.py:433
  331.0 69.2 %collective-permute-start.32 = (bf16[256,1536]{1,0:T(8,128)(2,1)}, bf16[256,1536]{1,0:T(8,128)(2,1)S(1)}, u32[]{:S(2)}, u32[]{:S(2)}) collective-permute-start(bf16[256,1536]{1,0:T(8,128)(2,1)} %get-tuple-element.155), channel_id=1, source_target_pairs={{0,1},{1,2},{2,3},{3,0},{4,5},{5,6},{6,7},{7,4},{8,9},{9,10},{10,1... | collective-permute-start | bytes 2359304 | tf_op jit(solution)/shard_map/ppermute | solution.py:433
  340.9 94.2 %collective-permute-start.48 = (bf16[96,1920]{0,1:T(8,128)(2,1)S(1)}, bf16[96,1920]{0,1:T(8,128)(2,1)S(1)}, u32[]{:S(2)}, u32[]{:S(2)}) collective-permute-start(bf16[96,1920]{0,1:T(8,128)(2,1)S(1)} %get-tuple-element.144), channel_id=1, source_target_pairs={{0,8},{4,12},{8,0},{12,4},{16,24},{20,28},{24,16},{28,20},{1,9},{5... | collective-permute-start | bytes 1105928 | tf_op jit(solution)/shard_map/ppermute | solution.py:437
  348.7 88.8 %collective-permute-start.24 = (bf16[256,1536]{1,0:T(8,128)(2,1)S(1)}, bf16[256,1536]{1,0:T(8,128)(2,1)S(1)}, u32[]{:S(2)}, u32[]{:S(2)}) collective-permute-start(bf16[256,1536]{1,0:T(8,128)(2,1)S(1)} %copy-done.18), channel_id=1, source_target_pairs={{0,3},{1,0},{2,1},{3,2},{4,7},{5,4},{6,5},{7,6},{8,11},{9,8},{10,9... | collective-permute-start | bytes 2359304 | tf_op jit(solution)/shard_map/ppermute | solution.py:433
  400.2 66.9 %collective-permute-start.25 = (bf16[256,1536]{1,0:T(8,128)(2,1)S(1)}, bf16[256,1536]{1,0:T(8,128)(2,1)S(1)}, u32[]{:S(2)}, u32[]{:S(2)}) collective-permute-start(bf16[256,1536]{1,0:T(8,128)(2,1)S(1)} %get-tuple-element.159), channel_id=1, source_target_pairs={{0,2},{1,3},{2,0},{3,1},{4,6},{5,7},{6,4},{7,5},{8,10},{9,11},{10,... | collective-permute-start | bytes 2359304 | tf_op jit(solution)/shard_map/ppermute | solution.py:433
  400.2 68.2 %collective-permute-start.26 = (bf16[256,1536]{1,0:T(8,128)(2,1)S(1)}, bf16[256,1536]{1,0:T(8,128)(2,1)S(1)}, u32[]{:S(2)}, u32[]{:S(2)}) collective-permute-start(bf16[256,1536]{1,0:T(8,128)(2,1)S(1)} %get-tuple-element.158), channel_id=1, source_target_pairs={{0,1},{1,2},{2,3},{3,0},{4,5},{5,6},{6,7},{7,4},{8,9},{9,10},{10,1... | collective-permute-start | bytes 2359304 | tf_op jit(solution)/shard_map/ppermute | solution.py:433
  434.0 38.1 %collective-permute-start.45 = (bf16[96,1920]{0,1:T(8,128)(2,1)S(1)}, bf16[96,1920]{0,1:T(8,128)(2,1)S(1)}, u32[]{:S(2)}, u32[]{:S(2)}) collective-permute-start(bf16[96,1920]{0,1:T(8,128)(2,1)S(1)} %get-tuple-element.145), channel_id=1, source_target_pairs={{0,8},{4,12},{8,0},{12,4},{16,24},{20,28},{24,16},{28,20},{1,9},{5... | collective-permute-start | bytes 1105928 | tf_op jit(solution)/shard_map/ppermute | solution.py:437
  435.1 37.0 %collective-permute-start.53 = (bf16[96,1920]{0,1:T(8,128)(2,1)S(1)}, bf16[96,1920]{0,1:T(8,128)(2,1)S(1)}, u32[]{:S(2)}, u32[]{:S(2)}) collective-permute-start(bf16[96,1920]{0,1:T(8,128)(2,1)S(1)} %get-tuple-element.142), channel_id=1, source_target_pairs={{0,8},{4,12},{8,0},{12,4},{16,24},{20,28},{24,16},{28,20},{1,9},{5... | collective-permute-start | bytes 1105928 | tf_op jit(solution)/shard_map/ppermute | solution.py:437
  437.6 34.6 %collective-permute-start.55 = (bf16[96,1920]{0,1:T(8,128)(2,1)S(1)}, bf16[96,1920]{0,1:T(8,128)(2,1)S(1)}, u32[]{:S(2)}, u32[]{:S(2)}) collective-permute-start(bf16[96,1920]{0,1:T(8,128)(2,1)S(1)} %get-tuple-element.143), channel_id=1, source_target_pairs={{0,16},{4,20},{8,24},{12,28},{16,0},{20,4},{24,8},{28,12},{1,17},{... | collective-permute-start | bytes 1105928 | tf_op jit(solution)/shard_map/ppermute | solution.py:437
  481.0 19.6 %collective-permute-start.56 = (bf16[192,256]{0,1:T(8,128)(2,1)}, bf16[192,256]{0,1:T(8,128)(2,1)}, u32[]{:S(2)}, u32[]{:S(2)}) collective-permute-start(bf16[192,256]{0,1:T(8,128)(2,1)} %get-tuple-element.134), channel_id=1, source_target_pairs={{0,1},{1,2},{2,3},{3,0},{4,5},{5,6},{6,7},{7,4},{8,9},{9,10},{10,1... | collective-permute-start | bytes 294920 | tf_op jit(solution)/shard_map/ppermute | solution.py:433
  (103 other events, 1369.2 us)

commit v2 on v1

v2 whole, which is shorter than its diff:
```python
import functools

import jax
import jax.numpy as jnp
from jax import lax
from jax.experimental import pallas as pl
from jax.experimental.pallas import tpu as pltpu
from jax.sharding import PartitionSpec as P

norm_eps = 1e-05
beta_one = 0.9
beta_two = 0.95
adam_eps = 1e-08
step_count = 3.0
rate_matrix = 0.005
rate_vector = 0.2
weight_decay = 0.1
lanes = 128
sub = 8
f32 = jnp.float32
bf16 = jnp.bfloat16


def dot(lhs, rhs, over=(1, 0)):
    return lax.dot_general(
        lhs, rhs, (((over[0],), (over[1],)), ((), ())), preferred_element_type=f32
    )


def dot_exact(lhs, rhs, over=(1, 0)):
    return lax.dot_general(
        lhs,
        rhs,
        (((over[0],), (over[1],)), ((), ())),
        precision=lax.Precision.HIGHEST,
        preferred_element_type=f32,
    )


def iota(shape, axis):
    return lax.broadcasted_iota(jnp.int32, shape, axis)


def later(values, count):
    if count == 0:
        return values
    rolled = pltpu.roll(values, count, 0)
    return jnp.where(iota(values.shape, 0) >= count, rolled, 0.0)


def earlier(values, count):
    if count == 0:
        return values
    length = values.shape[0]
    rolled = pltpu.roll(values, length - count, 0)
    return jnp.where(iota(values.shape, 0) < length - count, rolled, 0.0)


def conv(values, taps, kernel):
    summed = taps[kernel : kernel + 1] + taps[kernel - 1 : kernel] * values
    for offset in range(kernel - 1):
        summed = summed + taps[offset : offset + 1] * later(values, kernel - 1 - offset)
    return summed


def conv_back(grads, taps, kernel):
    summed = taps[kernel - 1 : kernel] * grads
    for offset in range(kernel - 1):
        summed = summed + taps[offset : offset + 1] * earlier(grads, kernel - 1 - offset)
    return summed


def conv_sums(grads, values, kernel):
    rows = [
        jnp.sum(grads * later(values, kernel - 1 - offset), axis=0, keepdims=True)
        for offset in range(kernel)
    ]
    rows.append(jnp.sum(grads, axis=0, keepdims=True))
    return rows


def sigmoid(values):
    return 1.0 / (1.0 + jnp.exp(-values))


def shared_parts(bc_rows, step_raw, cbc_ref, head_ref, state, kernel):
    step_raw = step_raw + head_ref[1:2, :]
    length = bc_rows.shape[0]
    bc_pre = conv(bc_rows, cbc_ref, kernel)
    bc_sig = sigmoid(bc_pre)
    shared = bc_pre * bc_sig
    step = jnp.maximum(step_raw, 0.0) + jnp.log1p(jnp.exp(-jnp.abs(step_raw)))
    rate = -jnp.exp(head_ref[0:1, :])
    lower = (iota((length, length), 0) >= iota((length, length), 1)).astype(f32)
    cum = dot_exact(lower, step * rate)
    in_map = shared[:, :state].astype(bf16)
    out_map = shared[:, state:].astype(bf16)
    scores = dot(out_map, in_map, (1, 1)) * lower
    return dict(
        bc_rows=bc_rows,
        bc_pre=bc_pre,
        bc_sig=bc_sig,
        step_raw=step_raw,
        step=step,
        rate=rate,
        cum=cum,
        cum_t=cum.T,
        in_map=in_map,
        out_map=out_map,
        scores=scores,
    )


def pick(values, pair, first):
    return jnp.where(
        first, values[:, 2 * pair : 2 * pair + 1], values[:, 2 * pair + 1 : 2 * pair + 2]
    )


def blocks_of(length):
    half = length // 2
    return [((0, half), (0, half)), ((half, length), (0, length))]


def place_pieces(place, pieces, target, sems):
    copies = []
    for at, (mask, ref) in enumerate(pieces):
        rows = ref.shape[0]
        start = pl.multiple_of((place ^ mask) * rows, 32)
        copies.append(
            pltpu.make_async_copy(ref, target.at[pl.ds(start, rows), :], sems.at[at])
        )
    for copy in copies:
        copy.start()
    return copies


piece_masks = (0, 2, 4, 6, 1, 3, 5, 7)


def forward_kernel(*refs, inner, state, kernel, split, primary):
    if split:
        place_ref, x_ref = refs[:2]
        pieces_a, pieces_b = refs[2:10], refs[10:18]
        rest = refs[18:]
    else:
        x_ref, wa_ref, wb_ref = refs[:3]
        rest = refs[3:]
    if not primary:
        bc_ref = rest[0]
        rest = rest[1:]
    taps_ref, cbc_ref, head_ref, proja_ref, projb_ref, y_ref, gated_ref = rest[:7]
    if split:
        wa_ref, wb_ref, sems = rest[7:]

        @pl.when(pl.program_id(0) == 0)
        def assemble():
            place = place_ref[0]
            copies = place_pieces(place, list(zip(piece_masks, pieces_a)), wa_ref, sems.at[0])
            copies = copies + place_pieces(
                place, list(zip(piece_masks, pieces_b)), wb_ref, sems.at[1]
            )
            for copy in copies:
                copy.wait()

    length = x_ref.shape[0]
    rows = x_ref[...]
    for weights, target in ((wa_ref, proja_ref), (wb_ref, projb_ref)):
        width = weights.shape[1]
        for start in range(0, width, 256):
            stop = min(width, start + 256)
            target[:, start:stop] = dot(rows, weights[:, start:stop])
    bc_rows = proja_ref[:, inner:] if primary else bc_ref[...]
    part = shared_parts(bc_rows, projb_ref[:, inner:], cbc_ref, head_ref, state, kernel)
    step, cum, cum_t, scores = part["step"], part["cum"], part["cum_t"], part["scores"]
    first = iota((length, lanes), 1) < lanes // 2
    for pair in range(inner // lanes):
        cols = slice(pair * lanes, (pair + 1) * lanes)
        taps = taps_ref[:, cols]
        gate = proja_ref[:, cols]
        values = conv(projb_ref[:, cols], taps, kernel)
        values = values * sigmoid(values)
        scaled = values * pick(step, pair, first)
        halves = (
            jnp.where(first, scaled, 0.0).astype(bf16),
            jnp.where(first, 0.0, scaled).astype(bf16),
        )
        pieces = []
        for (r0, r1), (c0, c1) in blocks_of(length):
            total = None
            for side in range(2):
                head = 2 * pair + side
                gap = cum[r0:r1, head : head + 1] - cum_t[head : head + 1, c0:c1]
                weights = (scores[r0:r1, c0:c1] * jnp.exp(jnp.minimum(gap, 0.0))).astype(bf16)
                term = dot(weights, halves[side][c0:c1])
                total = term if total is None else total + term
            pieces.append(total)
        output = jnp.concatenate(pieces, axis=0)
        y_ref[:, cols] = output
        gated_ref[:, cols] = (output + taps[kernel + 2 : kernel + 3] * values) * (
            gate * sigmoid(gate)
        )


def gate_kernel(*refs, kernel, split, blocks):
    if split:
        place_ref, cot_ref = refs[:2]
        pieces = [refs[2 + 8 * at : 10 + 8 * at] for at in range(blocks)]
        rest = refs[2 + 8 * blocks :]
    else:
        cot_ref = refs[0]
        out_refs = refs[1 : 1 + blocks]
        rest = refs[1 + blocks :]
    gated_refs, taps_refs = rest[:blocks], rest[blocks : 2 * blocks]
    grad_refs = rest[2 * blocks : 3 * blocks]
    stats_ref, branch_ref, lifted_ref = rest[3 * blocks : 3 * blocks + 3]
    if split:
        out_refs = rest[3 * blocks + 3 : 4 * blocks + 3]
        sems = rest[4 * blocks + 3]

        @pl.when(pl.program_id(0) == 0)
        def assemble():
            place = place_ref[0]
            copies = []
            for at in range(blocks):
                copies = copies + place_pieces(
                    place, list(zip(piece_masks, pieces[at])), out_refs[at], sems.at[at]
                )
            for copy in copies:
                copy.wait()

    cot = cot_ref[...]
    branch, squares, cross = None, None, None
    for at in range(blocks):
        gain = taps_refs[at][kernel + 1 : kernel + 2, :]
        weights = out_refs[at][...]
        grad = dot(cot, weights, (1, 1))
        grad_refs[at][...] = grad
        gated = gated_refs[at][...]
        inner = gated.shape[1]
        lifted = gated * gain
        low = lifted.astype(bf16)
        lifted_ref[:, at * inner : (at + 1) * inner] = low
        term = dot(low, weights)
        branch = term if branch is None else branch + term
        ones = jnp.ones((sub, inner), f32)
        term = dot_exact(ones, gated * gated, (1, 1))
        squares = term if squares is None else squares + term
        term = dot_exact(ones, grad * lifted, (1, 1))
        cross = term if cross is None else cross + term
    branch_ref[...] = branch.astype(bf16)
    stats_ref[...] = jnp.where(iota(squares.shape, 0) == 0, squares, cross)


def backward_kernel(*refs, inner, state, kernel, inner_all, stat_parts, primary, joined):
    stat_refs = refs[:stat_parts]
    proja_ref, projb_ref = refs[stat_parts : stat_parts + 2]
    rest = refs[stat_parts + 2 :]
    if not primary:
        bc_ref = rest[0]
        rest = rest[1:]
    if joined:
        joined_ref = rest[0]
        rest = rest[1:]
    y_ref, grad_ref, taps_ref, cbc_ref, head_ref, cota_ref, cotb_ref = rest[:7]
    tap_sums_ref, head_sums_ref = rest[7:9]
    bc_out_ref = rest[9]
    score_ref = rest[10]
    length = proja_ref.shape[0]
    half_lanes = lanes // 2

    @pl.when(pl.program_id(0) == 0)
    def clear():
        tap_sums_ref[...] = jnp.zeros(tap_sums_ref.shape, f32)
        head_sums_ref[...] = jnp.zeros(head_sums_ref.shape, f32)
        if primary:
            bc_out_ref[...] = jnp.zeros(bc_out_ref.shape, f32)

    stats = stat_refs[0][...]
    for more in stat_refs[1:]:
        stats = stats + more[...]
    unit = (iota((length, length), 0) == iota((length, length), 1)).astype(f32)
    columns = dot_exact(unit, stats, (1, 1))
    inv = lax.rsqrt(columns[:, 0:1] / inner_all + norm_eps)
    pull = inv * inv * inv * columns[:, 1:2] / inner_all

    bc_rows = proja_ref[:, inner:] if primary else bc_ref[...]
    part = shared_parts(bc_rows, projb_ref[:, inner:], cbc_ref, head_ref, state, kernel)
    step, cum, cum_t, scores = part["step"], part["cum"], part["cum_t"], part["scores"]
    first = iota((length, lanes), 1) < half_lanes
    score_ref[...] = jnp.zeros(score_ref.shape, f32)
    cum_grad = jnp.zeros((length, lanes), f32)
    step_grad = jnp.zeros((length, lanes), f32)
    for pair in range(inner // lanes):
        cols = slice(pair * lanes, (pair + 1) * lanes)
        taps = taps_ref[:, cols]
        gain = taps[kernel + 1 : kernel + 2]
        skip = taps[kernel + 2 : kernel + 3]
        gate = proja_ref[:, cols]
        raw = projb_ref[:, cols]
        pre = conv(raw, taps, kernel)
        pre_sig = sigmoid(pre)
        values = pre * pre_sig
        spread = pick(step, pair, first)
        scaled = values * spread
        gate_sig = sigmoid(gate)
        lift = gate * gate_sig
        plain = y_ref[:, cols]
        output = plain + skip * values
        gated = output * lift
        normed = gated * inv
        grad = grad_ref[:, cols]
        gain_row = jnp.sum(grad * normed, axis=0, keepdims=True)
        gated_grad = inv * (grad * gain) - gated * pull
        cota_ref[:, cols] = (
            gated_grad * output * (gate_sig * (1.0 + gate * (1.0 - gate_sig)))
        ).astype(bf16)
        out_grad = gated_grad * lift
        skip_row = jnp.sum(out_grad * values, axis=0, keepdims=True)
        out_low = out_grad.astype(bf16)
        scaled_low = scaled.astype(bf16)
        zero = jnp.zeros_like(out_low)
        sides = (jnp.where(first, out_low, zero), jnp.where(first, zero, out_low))
        half = length // 2
        pulled = [jnp.zeros((half, lanes), f32), jnp.zeros((half, lanes), f32)]
        for (r0, r1), (c0, c1) in blocks_of(length):
            score_sum = score_ref[r0:r1, c0:c1]
            for side in range(2):
                head = 2 * pair + side
                gap = cum[r0:r1, head : head + 1] - cum_t[head : head + 1, c0:c1]
                decay = jnp.exp(jnp.minimum(gap, 0.0))
                weights = (scores[r0:r1, c0:c1] * decay).astype(bf16)
                score_sum = score_sum + dot(sides[side][r0:r1], scaled_low[c0:c1], (1, 1)) * decay
                back = dot(weights, sides[side][r0:r1], (0, 0))
                pulled[0] = pulled[0] + back[:half]
                if c1 > half:
                    pulled[1] = pulled[1] + back[half:]
            score_ref[r0:r1, c0:c1] = score_sum
        scaled_grad = jnp.concatenate(pulled, axis=0)
        hot = (
            2 * pair + (iota((lanes, lanes), 0) >= half_lanes).astype(jnp.int32)
            == iota((lanes, lanes), 1)
        ).astype(f32)
        balance = out_low.astype(f32) * plain - scaled_low.astype(f32) * scaled_grad
        cum_grad = cum_grad + dot_exact(balance, hot)
        step_grad = step_grad + dot_exact(values * scaled_grad, hot)
        value_grad = skip * out_grad + scaled_grad * spread
        pre_grad = value_grad * (pre_sig * (1.0 + pre * (1.0 - pre_sig)))
        cotb_ref[:, cols] = conv_back(pre_grad, taps, kernel).astype(bf16)
        rows = conv_sums(pre_grad, raw, kernel) + [gain_row, skip_row]
        rows = rows + [jnp.zeros_like(gain_row)] * (tap_sums_ref.shape[0] - len(rows))
        tap_sums_ref[:, cols] = tap_sums_ref[:, cols] + jnp.concatenate(rows, axis=0)

    lower = iota((length, length), 0) >= iota((length, length), 1)
    score_low = jnp.where(lower, score_ref[...], 0.0).astype(bf16)
    shared_grad = jnp.concatenate(
        [dot(score_low, part["out_map"], (0, 0)), dot(score_low, part["in_map"])], axis=1
    )
    if joined:
        shared_grad = shared_grad + joined_ref[...]
    if primary:
        bc_pre, bc_sig = part["bc_pre"], part["bc_sig"]
        bc_grad = shared_grad * (bc_sig * (1.0 + bc_pre * (1.0 - bc_sig)))
        cota_ref[:, inner:] = conv_back(bc_grad, cbc_ref, kernel).astype(bf16)
        rows = conv_sums(bc_grad, part["bc_rows"], kernel)
        rows = rows + [jnp.zeros_like(rows[0])] * (bc_out_ref.shape[0] - len(rows))
        bc_out_ref[...] = bc_out_ref[...] + jnp.concatenate(rows, axis=0)
    else:
        bc_out_ref[...] = shared_grad
    decay_grad = dot_exact(lower.astype(f32), cum_grad, (0, 0))
    raw_grad = (step_grad + decay_grad * part["rate"]) * sigmoid(part["step_raw"])
    cotb_ref[:, inner:] = raw_grad.astype(bf16)
    rows = [
        part["rate"] * jnp.sum(step * decay_grad, axis=0, keepdims=True),
        jnp.sum(raw_grad, axis=0, keepdims=True),
    ]
    rows = rows + [jnp.zeros_like(rows[0])] * (head_sums_ref.shape[0] - len(rows))
    head_sums_ref[...] = head_sums_ref[...] + jnp.concatenate(rows, axis=0)


def product_kernel(place_ref, x_ref, grad_ref, keep_ref, send_ref, sum_ref, *, order):
    place = place_ref[0]
    rows = keep_ref.shape[1]
    sum_ref[...] = dot(x_ref[...], grad_ref[...], (0, 0))
    for at, mask in enumerate(order):
        start = pl.multiple_of((place ^ mask) * rows, 32)
        keep_ref[at] = sum_ref[pl.ds(start, rows), :].astype(bf16)
        start = pl.multiple_of((place ^ mask ^ 1) * rows, 32)
        send_ref[at] = sum_ref[pl.ds(start, rows), :].astype(bf16)


def whole(array):
    return pl.BlockSpec(array.shape, lambda step, *_: (0,) * array.ndim, pipeline_mode=pl.Buffered(1))


def rows_spec(length, width, column=0):
    return pl.BlockSpec((length, width), lambda step, *_: (step, column))


def fixed_spec(shape):
    return pl.BlockSpec(shape, lambda step, *_: (0,) * len(shape))


def any_spec():
    return pl.BlockSpec(memory_space=pl.ANY)


def stat_spec(length, slots, back):
    return pl.BlockSpec((sub, length), lambda step, *_: (lax.rem(step + slots - back, slots), 0))


def call_params():
    return pltpu.CompilerParams(
        dimension_semantics=("arbitrary",), vmem_limit_bytes=56 * 1024 * 1024
    )


def run_forward(place, normed, weights, bc_from, tables, seq_len, state, kernel):
    taps, cbc, head = tables
    rows, depth = normed.shape
    inner = taps.shape[1]
    split = isinstance(weights[0], (list, tuple))
    primary = bc_from is None
    if split:
        widths = [group[0].shape[1] for group in weights]
        prefix, ins = [place], [normed, *weights[0], *weights[1]]
        specs = [rows_spec(seq_len, depth)] + [any_spec()] * 16
    else:
        widths = [array.shape[1] for array in weights]
        prefix, ins = [], [normed, *weights]
        specs = [rows_spec(seq_len, depth)] + [whole(array) for array in weights]
    if not primary:
        ins.append(bc_from)
        specs.append(rows_spec(seq_len, 2 * state, inner // (2 * state)))
    for table in tables:
        ins.append(table)
        specs.append(whole(table))
    outs = [(widths[0], f32), (widths[1], f32), (inner, f32), (inner, f32)]
    out_specs = [rows_spec(seq_len, width) for width, _ in outs]
    out_shape = [jax.ShapeDtypeStruct((rows, width), kind) for width, kind in outs]
    scratch = []
    if split:
        out_specs = out_specs + [fixed_spec((depth, width)) for width in widths]
        out_shape = out_shape + [jax.ShapeDtypeStruct((depth, width), bf16) for width in widths]
        scratch = [pltpu.SemaphoreType.DMA((2, 8))]
    return pl.pallas_call(
        functools.partial(
            forward_kernel, inner=inner, state=state, kernel=kernel, split=split, primary=primary
        ),
        grid_spec=pltpu.PrefetchScalarGridSpec(
            num_scalar_prefetch=len(prefix),
            grid=(rows // seq_len,),
            in_specs=specs,
            out_specs=out_specs,
            scratch_shapes=scratch,
        ),
        out_shape=out_shape,
        compiler_params=call_params(),
        name="mixer_forward" if primary else "mixer_forward_more",
    )(*prefix, *ins)


def run_gate(place, cot, weights, gated, taps, seq_len, kernel):
    rows, inner = gated[0].shape
    slots, width = rows // seq_len, cot.shape[1]
    blocks = len(gated)
    split = isinstance(weights[0], (list, tuple))
    prefix, ins, specs, scratch = [], [cot], [rows_spec(seq_len, width)], []
    if split:
        prefix = [place]
        for group in weights:
            ins.extend(group)
            specs.extend([any_spec()] * 8)
        scratch = [pltpu.VMEM((inner, width), bf16)] * blocks + [
            pltpu.SemaphoreType.DMA((blocks, 8))
        ]
    else:
        ins.extend(weights)
        specs.extend([whole(array) for array in weights])
    ins.extend(gated)
    specs.extend([rows_spec(seq_len, inner)] * blocks)
    ins.extend(taps)
    specs.extend([whole(table) for table in taps])
    return pl.pallas_call(
        functools.partial(gate_kernel, kernel=kernel, split=split, blocks=blocks),
        grid_spec=pltpu.PrefetchScalarGridSpec(
            num_scalar_prefetch=len(prefix),
            grid=(slots,),
            in_specs=specs,
            out_specs=[rows_spec(seq_len, inner)] * blocks
            + [rows_spec(sub, seq_len), rows_spec(seq_len, width), rows_spec(seq_len, blocks * inner)],
            scratch_shapes=scratch,
        ),
        out_shape=[jax.ShapeDtypeStruct((rows, inner), f32)] * blocks
        + [
            jax.ShapeDtypeStruct((slots * sub, seq_len), f32),
            jax.ShapeDtypeStruct((rows, width), bf16),
            jax.ShapeDtypeStruct((rows, blocks * inner), bf16),
        ],
        compiler_params=call_params(),
        name="gate_products",
    )(*prefix, *ins)


def run_backward(stats, turned, proj, bc_from, joined, plain, grad, tables, seq_len, state, kernel, inner_all):
    taps, cbc, head = tables
    rows = plain.shape[0]
    inner = taps.shape[1]
    slots = rows // seq_len
    primary = bc_from is None
    ins = [*stats, *proj]
    specs = [stat_spec(seq_len, slots, back if turned else 0) for back in range(len(stats))]
    specs = specs + [rows_spec(seq_len, array.shape[1]) for array in proj]
    if not primary:
        ins.append(bc_from)
        specs.append(rows_spec(seq_len, 2 * state, inner // (2 * state)))
    if joined is not None:
        ins.append(joined)
        specs.append(rows_spec(seq_len, 2 * state))
    ins.extend([plain, grad])
    specs.extend([rows_spec(seq_len, inner)] * 2)
    for table in tables:
        ins.append(table)
        specs.append(whole(table))
    bc_shape = cbc.shape if primary else (rows, 2 * state)
    return pl.pallas_call(
        functools.partial(
            backward_kernel,
            inner=inner,
            state=state,
            kernel=kernel,
            inner_all=inner_all,
            stat_parts=len(stats),
            primary=primary,
            joined=joined is not None,
        ),
        grid=(slots,),
        in_specs=specs,
        out_specs=[
            rows_spec(seq_len, proj[0].shape[1]),
            rows_spec(seq_len, proj[1].shape[1]),
            fixed_spec(taps.shape),
            fixed_spec(head.shape),
            fixed_spec(cbc.shape) if primary else rows_spec(seq_len, 2 * state),
        ],
        out_shape=[
            jax.ShapeDtypeStruct((rows, proj[0].shape[1]), bf16),
            jax.ShapeDtypeStruct((rows, proj[1].shape[1]), bf16),
            jax.ShapeDtypeStruct(taps.shape, f32),
            jax.ShapeDtypeStruct(head.shape, f32),
            jax.ShapeDtypeStruct(bc_shape, f32),
        ],
        scratch_shapes=[pltpu.VMEM((seq_len, seq_len), f32)],
        compiler_params=call_params(),
        name="mixer_backward" if primary else "mixer_backward_more",
    )(*ins)


def run_product(place, x, grad, order, column=0, width=None):
    tokens = x.shape[0]
    depth = x.shape[1] if width is None else width
    cols = grad.shape[1]
    tile = 256 if cols % 256 == 0 else lanes
    rows = depth // 8
    block = pl.BlockSpec((4, rows, tile), lambda step, *_: (0, 0, step))
    return pl.pallas_call(
        functools.partial(product_kernel, order=order),
        grid_spec=pltpu.PrefetchScalarGridSpec(
            num_scalar_prefetch=1,
            grid=(cols // tile,),
            in_specs=[
                pl.BlockSpec(
                    (tokens, depth), lambda step, *_: (0, column), pipeline_mode=pl.Buffered(1)
                ),
                pl.BlockSpec((tokens, tile), lambda step, *_: (0, step)),
            ],
            out_specs=[block, block],
            scratch_shapes=[pltpu.VMEM((depth, tile), f32)],
        ),
        out_shape=[jax.ShapeDtypeStruct((4, rows, cols), bf16)] * 2,
        compiler_params=call_params(),
        name="weight_product",
    )(place, x, grad)


def adam_update(parameter, moments, gradient, learn_rate, decay_coef):
    first_mom = beta_one * moments[0] + (1.0 - beta_one) * gradient
    second_mom = beta_two * moments[1] * moments[1] + (1.0 - beta_two) * gradient * gradient
    second_root = jnp.sqrt(second_mom)
    first_hat = first_mom / (1.0 - beta_one**step_count)
    second_hat = second_mom / (1.0 - beta_two**step_count)
    updated = parameter - learn_rate * (
        first_hat / (jnp.sqrt(second_hat) + adam_eps) + decay_coef * parameter
    )
    return (updated, jnp.stack([first_mom, second_root]))


def swap_by(values, axis, count, mask):
    return lax.ppermute(values, axis, [(i, i ^ mask) for i in range(count)])


def pad_to(values, rows, cols):
    return jnp.pad(values, ((0, rows - values.shape[0]), (0, cols - values.shape[1])))


def gather_plane(piece, way):
    other = 6 - way
    near = swap_by(piece, "dp", 8, way)
    side = swap_by(piece, "dp", 8, other)
    far = swap_by(near, "dp", 8, other)
    mine = [piece, near, side, far] if way == 2 else [piece, side, near, far]
    return mine + [swap_by(values, "dp", 8, 1) for values in mine]


def order_of(way):
    return (0, 6 - way, way, 6)


def scatter_plane(keep, send, way):
    other = 6 - way
    got = swap_by(send, "dp", 8, 1)
    away = (keep[2:].astype(f32) + got[2:].astype(f32)).astype(bf16)
    near = swap_by(away, "dp", 8, way)
    here = keep[:2].astype(f32) + got[:2].astype(f32) + near.astype(f32)
    last = swap_by(here[1].astype(bf16), "dp", 8, other)
    return here[0] + last.astype(f32)


def sum_over(values, axis, count):
    if count & (count - 1):
        return lax.psum(values, axis)
    mask = 1
    while mask < count:
        values = values + swap_by(values, axis, count, mask)
        mask = mask * 2
    return values


def shards(
    block_input,
    seq_lengths,
    cotangent,
    norm_gain,
    proj_zx,
    proj_dt,
    proj_bc,
    chan_params,
    conv_bc,
    head_params,
    out_proj,
    gain_moments,
    zx_moments,
    dt_moments,
    bc_moments,
    chan_moments,
    convbc_moments,
    head_moments,
    out_moments,
):
    heads_axis = lax.axis_size("head")
    dp_axis = lax.axis_size("dp")
    slot_count = seq_lengths.shape[0]
    rows_own, model_width = block_input.shape
    rows_dev = rows_own * heads_axis
    seq_len = rows_dev // slot_count
    rows_dp = proj_zx.shape[0]
    inner = chan_params.shape[1]
    inner_all = inner * heads_axis
    heads_loc = head_params.shape[1]
    headdim = inner // heads_loc
    kernel = chan_params.shape[0] - 2
    state = conv_bc.shape[1] // 2
    spot = lax.axis_index("head")
    place = lax.axis_index("dp").astype(jnp.int32).reshape(1)
    paired = heads_axis == 4 and dp_axis == 8 and rows_own == seq_len

    zx_low = proj_zx.astype(bf16)
    piece_a = jnp.concatenate([zx_low[:, 0], proj_bc.astype(bf16)], axis=1)
    piece_b = jnp.concatenate([zx_low[:, 1], pad_to(proj_dt.astype(bf16), rows_dp, lanes)], axis=1)
    out_low = out_proj.astype(bf16)
    taps = pad_to(
        jnp.concatenate([chan_params, jnp.repeat(head_params[2:3], headdim, axis=1)], axis=0),
        sub,
        inner,
    )
    cbc = pad_to(conv_bc, sub, 2 * state)
    head_table = pad_to(head_params, sub, lanes)

    positions = iota((slot_count, seq_len), 1)
    live_mask = (positions < seq_lengths[:, None]).astype(f32).reshape(rows_dev, 1)
    live_own = lax.dynamic_slice_in_dim(live_mask, spot * rows_own, rows_own, 0)
    gain_float = lax.optimization_barrier(norm_gain.astype(bf16)).astype(f32)
    input_float = block_input.astype(f32)
    inv_own = lax.rsqrt(jnp.mean(input_float * input_float, axis=-1, keepdims=True) + norm_eps)
    own_hat = input_float * inv_own
    normed_own = (own_hat * gain_float[None, :]).astype(bf16)
    cot_float = cotangent.astype(f32)
    cot_own = (cot_float * live_own).astype(bf16)
    tables = (taps, cbc, head_table)

    if paired:
        more = swap_by(jnp.concatenate([zx_low[:, 0], piece_b], axis=1), "head", 4, 2)
        wide = jnp.concatenate([taps, head_table], axis=1)
        more_tables = swap_by(wide, "head", 4, 2)
        tables_more = (more_tables[:, :inner], cbc, more_tables[:, inner:])
        own_pieces = (gather_plane(piece_a, 2), gather_plane(piece_b, 4))
        normed_all = jnp.concatenate([normed_own, swap_by(normed_own, "head", 4, 1)], axis=0)
        more_pieces = (gather_plane(more[:, :inner], 2), gather_plane(more[:, inner:], 4))
        cot_all = jnp.concatenate([cot_own, swap_by(cot_own, "head", 4, 1)], axis=0)
        out_pieces = (
            gather_plane(out_low, 2),
            gather_plane(swap_by(out_low, "head", 4, 2), 4),
        )
        proj_a, proj_b, plain, gated, own_a, own_b = run_forward(
            place, normed_all, own_pieces, None, tables, seq_len, state, kernel
        )
        more_proj_a, more_proj_b, more_plain, more_gated, more_a, more_b = run_forward(
            place, normed_all, more_pieces, proj_a, tables_more, seq_len, state, kernel
        )
        grad, more_grad, stats, branch, lifted = run_gate(
            place,
            cot_all,
            out_pieces,
            (gated, more_gated),
            (taps, tables_more[0]),
            seq_len,
            kernel,
        )
        stat_parts = [stats, swap_by(stats, "head", 4, 1)]
        whole_stats = stats[:sub] + stat_parts[1][sub:], stats[sub:] + stat_parts[1][:sub]
        gate_rows = [
            lax.rsqrt(part[:1] / inner_all + norm_eps).reshape(seq_len, 1) for part in whole_stats
        ]
        gate_own = gate_rows[0]
        cot_gate = (cot_all.astype(f32) * jnp.concatenate(gate_rows, axis=0)).astype(bf16)
        out_own = run_product(place, lifted, cot_gate, order_of(2), 0, inner)
        out_more = run_product(place, lifted, cot_gate, order_of(4), 1, inner)
        more_cot_a, more_cot_b, more_tap_sums, more_head_sums, bc_part = run_backward(
            stat_parts,
            True,
            (more_proj_a, more_proj_b),
            proj_a,
            None,
            more_plain,
            more_grad,
            tables_more,
            seq_len,
            state,
            kernel,
            inner_all,
        )
        grad_more_a = run_product(place, normed_all, more_cot_a, order_of(2))
        grad_more_b = run_product(place, normed_all, more_cot_b, order_of(4))
        cot_a, cot_b, tap_sums, head_sums, cbc_sums = run_backward(
            stat_parts,
            True,
            (proj_a, proj_b),
            None,
            bc_part,
            plain,
            grad,
            tables,
            seq_len,
            state,
            kernel,
            inner_all,
        )
        grad_own_a = run_product(place, normed_all, cot_a, order_of(2))
        grad_own_b = run_product(place, normed_all, cot_b, order_of(4))
        cot_input = (
            dot(more_cot_a, more_a, (1, 1))
            + dot(more_cot_b, more_b, (1, 1))
            + dot(cot_a, own_a, (1, 1))
            + dot(cot_b, own_b, (1, 1))
        )
        grad_gain = jnp.sum(cot_input * normed_all.astype(f32), axis=0)
        cot_input = cot_input.astype(bf16)
        cot_whole = cot_input[:rows_own].astype(f32) + swap_by(
            cot_input[rows_own:], "head", 4, 1
        ).astype(f32)
        branch_own = branch[:rows_own].astype(f32) + swap_by(
            branch[rows_own:], "head", 4, 1
        ).astype(f32)
        out_sum = scatter_plane(*out_own, 2)
        out_sum = out_sum + swap_by(
            scatter_plane(*out_more, 4).astype(bf16), "head", 4, 2
        ).astype(f32)
        away = jnp.concatenate(
            [scatter_plane(*grad_more_a, 2), scatter_plane(*grad_more_b, 4)], axis=1
        ).astype(bf16)
        home = swap_by(away, "head", 4, 2).astype(f32)
        sum_a = scatter_plane(*grad_own_a, 2)
        sum_b = scatter_plane(*grad_own_b, 4)
        grad_out = out_sum
        grad_zx = jnp.stack(
            [sum_a[:, :inner] + home[:, :inner], sum_b[:, :inner] + home[:, inner : 2 * inner]],
            axis=1,
        )
        grad_dt = (sum_b[:, inner:] + home[:, 2 * inner :])[:, :heads_loc]
        grad_bc = sum_a[:, inner:]
        grad_bc = grad_bc + swap_by(grad_bc.astype(bf16), "head", 4, 1).astype(f32)
        grad_bc = grad_bc + swap_by(grad_bc.astype(bf16), "head", 4, 2).astype(f32)
        packs = [(more_tap_sums, more_head_sums), (tap_sums, head_sums)]
    else:
        normed_all = lax.all_gather(normed_own, "head", axis=0, tiled=True)
        cot_all = lax.all_gather(cot_own, "head", axis=0, tiled=True)
        own_a = lax.all_gather(piece_a, "dp", axis=0, tiled=True)
        own_b = lax.all_gather(piece_b, "dp", axis=0, tiled=True)
        out_full = lax.all_gather(out_low, "dp", axis=0, tiled=True)
        proj_a, proj_b, plain, gated = run_forward(
            None, normed_all, (own_a, own_b), None, tables, seq_len, state, kernel
        )
        grad, stats, branch, lifted = run_gate(
            None, cot_all, (out_full,), (gated,), (taps,), seq_len, kernel
        )
        stats = lax.psum(stats, "head")
        square = stats.reshape(slot_count, sub, seq_len)[:, 0].reshape(rows_dev, 1)
        gate_all = lax.rsqrt(square / inner_all + norm_eps)
        gate_own = lax.dynamic_slice_in_dim(gate_all, spot * rows_own, rows_own, 0)
        cot_gate = (cot_all.astype(f32) * gate_all).astype(bf16)
        cot_a, cot_b, tap_sums, head_sums, cbc_sums = run_backward(
            [stats],
            False,
            (proj_a, proj_b),
            None,
            None,
            plain,
            grad,
            tables,
            seq_len,
            state,
            kernel,
            inner_all,
        )
        cot_input = dot(cot_a, own_a, (1, 1)) + dot(cot_b, own_b, (1, 1))
        grad_gain = jnp.sum(cot_input * normed_all.astype(f32), axis=0)

        def scatter(values, axis):
            return lax.psum_scatter(
                values.astype(bf16), axis, scatter_dimension=0, tiled=True
            ).astype(f32)

        cot_whole = scatter(cot_input, "head")
        branch_own = scatter(branch, "head")
        grad_out = scatter(dot(lifted, cot_gate, (0, 0)), "dp")
        sum_a = scatter(dot(normed_all, cot_a, (0, 0)), "dp")
        sum_b = scatter(dot(normed_all, cot_b, (0, 0)), "dp")
        grad_zx = jnp.stack([sum_a[:, :inner], sum_b[:, :inner]], axis=1)
        grad_dt = sum_b[:, inner:][:, :heads_loc]
        grad_bc = lax.psum(sum_a[:, inner:].astype(bf16), "head").astype(f32)
        packs = [(tap_sums, head_sums)]

    block_output = (input_float + live_own * (branch_own * gate_own)).astype(bf16)
    lift_own = cot_whole * gain_float[None, :]
    row_dot = jnp.sum(lift_own * own_hat, axis=-1, keepdims=True)
    input_grad = cot_float + inv_own * (lift_own - own_hat * row_dot / model_width)

    parts = [cbc_sums.reshape(-1, lanes), grad_gain.reshape(-1, lanes)]
    both_rows = sum(part.shape[0] for part in parts)
    parts = parts + [jnp.concatenate(pack, axis=1).reshape(-1, lanes) for pack in packs]
    small = sum_over(jnp.concatenate(parts, axis=0), "dp", dp_axis)
    both = sum_over(small[:both_rows], "head", heads_axis)
    cbc_rows = sub * 2 * state // lanes
    grad_convbc = both[:cbc_rows].reshape(sub, 2 * state)[: kernel + 1]
    grad_gain = both[cbc_rows:].reshape(model_width) / gain_float
    pack_rows = sub * (inner + lanes) // lanes
    own_sums = small[small.shape[0] - pack_rows :]
    if paired:
        own_sums = own_sums + swap_by(small[both_rows : both_rows + pack_rows], "head", 4, 2)
    own_sums = own_sums.reshape(sub, inner + lanes)
    grad_chan = own_sums[: kernel + 2, :inner]
    grad_skip = jnp.sum(own_sums[kernel + 2, :inner].reshape(heads_loc, headdim), axis=1)
    grad_head = jnp.concatenate(
        [own_sums[:2, inner : inner + heads_loc], grad_skip[None, :]], axis=0
    )

    gain_next, gain_state = adam_update(norm_gain, gain_moments, grad_gain, rate_vector, 0.0)
    zx_next, zx_state = adam_update(proj_zx, zx_moments, grad_zx, rate_matrix, weight_decay)
    dt_next, dt_state = adam_update(proj_dt, dt_moments, grad_dt, rate_matrix, weight_decay)
    bc_next, bc_state = adam_update(proj_bc, bc_moments, grad_bc, rate_matrix, weight_decay)
    chan_next, chan_state = adam_update(chan_params, chan_moments, grad_chan, rate_vector, 0.0)
    convbc_next, convbc_state = adam_update(conv_bc, convbc_moments, grad_convbc, rate_vector, 0.0)
    head_next, head_state = adam_update(head_params, head_moments, grad_head, rate_vector, 0.0)
    outproj_next, outproj_state = adam_update(
        out_proj, out_moments, grad_out, rate_matrix, weight_decay
    )
    return (
        block_output,
        input_grad,
        gain_next,
        gain_state,
        zx_next,
        zx_state,
        dt_next,
        dt_state,
        bc_next,
        bc_state,
        chan_next,
        chan_state,
        convbc_next,
        convbc_state,
        head_next,
        head_state,
        outproj_next,
        outproj_state,
    )


def solution(mesh):
    placed = (
        P(("dp", "head"), None),
        P("dp"),
        P(("dp", "head"), None),
        P(),
        P("dp", None, "head"),
        P("dp", "head"),
        P("dp", None),
        P(None, "head"),
        P(),
        P(None, "head"),
        P(("head", "dp"), None),
        P(),
        P(None, "dp", None, "head"),
        P(None, "dp", "head"),
        P(None, "dp", None),
        P(None, None, "head"),
        P(),
        P(None, None, "head"),
        P(None, ("head", "dp"), None),
    )
    return jax.shard_map(
        shards,
        mesh=mesh,
        in_specs=placed,
        out_specs=(
            P(("dp", "head"), None),
            P(("dp", "head"), None),
            P(),
            P(),
            P("dp", None, "head"),
            P(None, "dp", None, "head"),
            P("dp", "head"),
            P(None, "dp", "head"),
            P("dp", None),
            P(None, "dp", None),
            P(None, "head"),
            P(None, None, "head"),
            P(),
            P(),
            P(None, "head"),
            P(None, None, "head"),
            P(("head", "dp"), None),
            P(None, ("head", "dp"), None),
        ),
        check_vma=False,
    )
```

time: 514 us -> 429 us (0.83)
  Pallas kernels: 58.4 us -> 110 us
  starting transfers between devices: 114 us -> 71.5 us
  waiting for transfers between devices: 197 us -> 160 us
  other arithmetic: 60.3 us -> 37.2 us
  local copies, waits for them, and re-layouts: 52.4 us -> 31.5 us
  matrix products: 20.2 us -> 9.35 us
    ppermute x28 -> x0, waiting for transfers between devices: 168 us -> none  [shift_by(): lax.ppermute(values, axis, [(i, (i + amount) % count) for i in range(coun...]
    ppermute x44 -> x78, waiting for transfers between devices: 28.8 us -> 160 us  [swap_by(): return lax.ppermute(values, axis, [(i, i ^ mask) for i in range(count)])]
    ppermute x28 -> x0, starting transfers between devices: 86.4 us -> none  [shift_by(): lax.ppermute(values, axis, [(i, (i + amount) % count) for i in range(coun...]
    ppermute x44 -> x78, starting transfers between devices: 27.1 us -> 71.5 us  [swap_by(): return lax.ppermute(values, axis, [(i, i ^ mask) for i in range(count)])]
    pallas_call x1 -> x7, Pallas kernels: 13.6 us -> 54.9 us  [the longest x6 39.6 us: run_product(): pl.pallas_call(functools.partial(product_kernel, order=order), grid_spec=...]
    dynamic_update_slice x18 -> x0, local copies, waits for them, and re-layouts: 13.1 us -> none  [gather_dp(): lax.dynamic_update_slice(gathered, values, ((place ^ mask) * rows + at, 0))]
    dot_general x3 -> x4, matrix products: 20.2 us -> 9.35 us  [dot(): lax.dot_general(lhs, rhs, (((over[0],), (over[1],)), ((), ())), preferred...]
    unnamed x136 -> x231, local copies, waits for them, and re-layouts: 9.49 us -> 17.8 us
  transfers between devices with their start and end apart: 72 -> 78, of which waited for: 21 -> 28; matrix products, arithmetic and copies ran while one was open for 21% -> 14% of each run, Pallas kernels for 0% -> 22%
where the time goes in v2:
time: 429 us; the launch traced here: 423 us
  waiting for transfers between devices  160 us (37%)
  Pallas kernels  110 us (26%)
  starting transfers between devices  71.5 us (17%)
  other arithmetic  37.2 us (9%)
  local copies, waits for them, and re-layouts  31.5 us (7%)
  matrix products  9.35 us (2%)
    ppermute x78, waiting for transfers between devices, swap_by(): return lax.ppermute(values, axis, [(i, i ^ mask) for i in range(count)])  160 us
    ppermute x78, starting transfers between devices, swap_by(): return lax.ppermute(values, axis, [(i, i ^ mask) for i in range(count)])  71.5 us
    pallas_call x6, Pallas kernels, run_product(): pl.pallas_call(functools.partial(product_kernel, order=order), grid_spec=...  39.6 us
    pallas_call x2, Pallas kernels, run_backward(): pl.pallas_call(functools.partial(backward_kernel, inner=inner, state=stat...  29.1 us
    pallas_call x2, Pallas kernels, run_forward(): pl.pallas_call(functools.partial(forward_kernel, inner=inner, state=state...  26.4 us
    unnamed x231, local copies, waits for them, and re-layouts  17.8 us
    pallas_call x1, Pallas kernels, run_gate(): pl.pallas_call(functools.partial(gate_kernel, kernel=kernel, split=split,...  15.2 us
    dot_general x4, matrix products, dot(): lax.dot_general(lhs, rhs, (((over[0],), (over[1],)), ((), ())), preferred...  9.35 us
  transfers between devices with their start and end apart: 78, of which 28 were waited for; matrix products, arithmetic and copies ran while one was open for 14% of the time, Pallas kernels for 22%

profile of v2, /device:TPU:0, one launch (start us, length us, event | category | flops | bytes accessed | tf_op | source)
XLA Modules:
  0.0 422.7 jit_solution(12551751482900967286)
XLA Ops:
  1.8 4.1 collective-permute-start.8
  12.8 7.7 %collective-permute-done.46 = f32[8,896]{1,0:T(8,128)S(1)} collective-permute-done((f32[8,896]{1,0:T(8,128)S(1)}, f32[8,896]{1,0:T(8,128)S(1)}, u32[]{:S(2)}, u32[]{:S(2)}) %collective-permute-start.46) | collective-permute-done | bytes 28704 | tf_op jit(solution)/shard_map/ppermute | solution.py:599
  26.1 5.4 %collective-permute-done.24.refs_11_ = bf16[192,896]{1,0:T(8,128)(2,1)} collective-permute-done((bf16[192,896]{1,0:T(8,128)(2,1)S(1)}, bf16[192,896]{1,0:T(8,128)(2,1)}, u32[]{:S(2)}, u32[]{:S(2)}) %collective-permute-start.24) | collective-permute-done | bytes 344096 | tf_op jit(solution)/shard_map/ppermute | solution.py:599
  34.6 5.4 %collective-permute-done.17.refs_3_ = bf16[192,1024]{1,0:T(8,128)(2,1)} collective-permute-done((bf16[192,1024]{1,0:T(8,128)(2,1)S(1)}, bf16[192,1024]{1,0:T(8,128)(2,1)}, u32[]{:S(2)}, u32[]{:S(2)}) %collective-permute-start.17) | collective-permute-done | bytes 393248 | tf_op jit(solution)/shard_map/ppermute | solution.py:599
  41.7 4.0 collective-permute-start.16
  51.9 16.6 %collective-permute-done.31 = bf16[192,1664]{1,0:T(8,128)(2,1)S(1)} collective-permute-done((bf16[192,1664]{1,0:T(8,128)(2,1)S(1)}, bf16[192,1664]{1,0:T(8,128)(2,1)S(1)}, u32[]{:S(2)}, u32[]{:S(2)}) %collective-permute-start.31) | collective-permute-done | bytes 639008 | tf_op jit(solution)/shard_map/ppermute | solution.py:599
  70.6 4.2 %collective-permute-done.16 = bf16[256,1536]{1,0:T(8,128)(2,1)S(1)} collective-permute-done((bf16[256,1536]{1,0:T(8,128)(2,1)S(1)}, bf16[256,1536]{1,0:T(8,128)(2,1)S(1)}, u32[]{:S(2)}, u32[]{:S(2)}) %collective-permute-start.16) | collective-permute-done | bytes 786464 | tf_op jit(solution)/shard_map/ppermute | solution.py:599
  76.3 4.0 collective-permute-done.19.refs_5_
  82.4 6.2 %collective-permute-done = bf16[256,1536]{1,0:T(8,128)(2,1)S(1)} collective-permute-done((bf16[256,1536]{1,0:T(8,128)(2,1)S(1)}, bf16[256,1536]{1,0:T(8,128)(2,1)S(1)}, u32[]{:S(2)}, u32[]{:S(2)}) %collective-permute-start) | collective-permute-done | bytes 786464 | tf_op jit(solution)/shard_map/ppermute | solution.py:599
  93.5 4.1 collective-permute-done.40.refs_12_
  102.5 3.5 collective-permute-done.41.refs_13_
  121.0 13.4 %mixer_forward.1 = (f32[512,1024]{1,0:T(8,128)}, f32[512,896]{1,0:T(8,128)}, f32[512,768]{1,0:T(8,128)}, f32[512,768]{1,0:T(8,128)}, bf16[1536,1024]{1,0:T(8,128)(2,1)}, /*index=5*/bf16[1536,896]{1,0:T(8,128)(2,1)}) custom-call(s32[1]{0:T(128)} %bitcast.1.refs_0_.place_ref, bf16[512,1536]{1,0:T(8,128)(2,1)} %pad_maximum_fusion.2.refs_1_.x_ref, ...), custom_call_target="tpu_custom_call" | custom-call | tf_op jit(solution)/shard_map/mixer_forward/pallas_call | solution.py:446
  134.4 13.0 %mixer_forward_more.1 = (f32[512,768]{1,0:T(8,128)}, f32[512,896]{1,0:T(8,128)}, f32[512,768]{1,0:T(8,128)}, f32[512,768]{1,0:T(8,128)}, bf16[1536,768]{1,0:T(8,128)(2,1)}, /*index=5*/bf16[1536,896]{1,0:T(8,128)(2,1)}) custom-call(s32[1]{0:T(128)} %bitcast.1.refs_0_.place_ref, bf16[512,1536]{1,0:T(8,128)(2,1)} %pad_maximum_fusion.2.refs_1_.x_ref, ...), custom_call_target="tpu_custom_call" | custom-call | tf_op jit(solution)/shard_map/mixer_forward_more/pallas_call | solution.py:446
  148.5 15.2 %gate_products.1 = (f32[512,768]{1,0:T(8,128)}, f32[512,768]{1,0:T(8,128)}, f32[16,256]{1,0:T(8,128)}, bf16[512,1536]{1,0:T(8,128)(2,1)}, bf16[512,1536]{1,0:T(8,128)(2,1)}) custom-call(s32[1]{0:T(128)} %bitcast.1.refs_0_.place_ref, bf16[512,1536]{1,0:T(8,128)(2,1)} %pad_maximum_fusion.1.refs_1_, bf16[96,1536]{1,0:T(8,128)(2,1)} %copy-done.28, ...), custom_call_target="tpu_custom_call" | custom-call | tf_op jit(solution)/shard_map/gate_products/pallas_call | solution.py:484
  169.3 14.3 %mixer_backward_more.1 = (bf16[512,768]{1,0:T(8,128)(2,1)}, bf16[512,896]{1,0:T(8,128)(2,1)}, f32[8,768]{1,0:T(8,128)}, f32[8,128]{1,0:T(8,128)}, f32[512,256]{1,0:T(8,128)}) custom-call(f32[16,256]{1,0:T(8,128)} %get-tuple-element.61.refs_0_, f32[16,256]{1,0:T(8,128)} %copy-done.77, f32[512,768]{1,0:T(8,128)} %get-tuple-element.62.refs_2_, ...), custom_call_target="tpu_custom_call" | custom-call | tf_op jit(solution)/shard_map/mixer_backward_more/pallas_call | solution.py:526
  184.4 14.8 %mixer_backward.1 = (bf16[512,1024]{1,0:T(8,128)(2,1)}, bf16[512,896]{1,0:T(8,128)(2,1)}, f32[8,768]{1,0:T(8,128)}, f32[8,128]{1,0:T(8,128)}, f32[8,256]{1,0:T(8,128)}) custom-call(f32[16,256]{1,0:T(8,128)} %get-tuple-element.61.refs_0_, f32[16,256]{1,0:T(8,128)} %copy-done.77, f32[512,1024]{1,0:T(8,128)} %get-tuple-element.58.refs_18_.refs_4_.refs_2_, ...), custom_call_target="tpu_custom_call" | custom-call | tf_op jit(solution)/shard_map/mixer_backward/pallas_call | solution.py:526
  200.6 4.0 fusion.86
  221.2 3.7 collective-permute-done.53
  229.2 6.4 %weight_product.10 = (bf16[4,96,1536]{2,1,0:T(8,128)(2,1)}, bf16[4,96,1536]{2,1,0:T(8,128)(2,1)}) custom-call(s32[1]{0:T(128)} %bitcast.1.refs_0_.place_ref, bf16[512,1536]{1,0:T(8,128)(2,1)} %get-tuple-element.91.x_ref, bf16[512,1536]{1,0:T(8,128)(2,1)} %multiply_convert_fusion.grad_ref), custom_call_target="tpu_custom_call" | custom-call | tf_op jit(solution)/shard_map/weight_product/pallas_call | solution.py:566
  235.6 6.3 %weight_product.11 = (bf16[4,96,1536]{2,1,0:T(8,128)(2,1)}, bf16[4,96,1536]{2,1,0:T(8,128)(2,1)}) custom-call(s32[1]{0:T(128)} %bitcast.1.refs_0_.place_ref, bf16[512,1536]{1,0:T(8,128)(2,1)} %get-tuple-element.91.x_ref, bf16[512,1536]{1,0:T(8,128)(2,1)} %multiply_convert_fusion.grad_ref), custom_call_target="tpu_custom_call" | custom-call | tf_op jit(solution)/shard_map/weight_product/pallas_call | solution.py:566
  241.8 5.7 %weight_product.6 = (bf16[4,192,1024]{2,1,0:T(8,128)(2,1)}, bf16[4,192,1024]{2,1,0:T(8,128)(2,1)}) custom-call(s32[1]{0:T(128)} %bitcast.1.refs_0_.place_ref, bf16[512,1536]{1,0:T(8,128)(2,1)} %pad_maximum_fusion.2.refs_1_.x_ref, bf16[512,1024]{1,0:T(8,128)(2,1)} %get-tuple-element.74.grad_ref), custom_call_target="tpu_custom_call" | custom-call | tf_op jit(solution)/shard_map/weight_product/pallas_call | solution.py:566
  247.5 8.1 %weight_product.9 = (bf16[4,192,896]{2,1,0:T(8,128)(2,1)}, bf16[4,192,896]{2,1,0:T(8,128)(2,1)}) custom-call(s32[1]{0:T(128)} %bitcast.1.refs_0_.place_ref, bf16[512,1536]{1,0:T(8,128)(2,1)} %pad_maximum_fusion.2.refs_1_.x_ref, bf16[512,896]{1,0:T(8,128)(2,1)} %get-tuple-element.76.grad_ref), custom_call_target="tpu_custom_call" | custom-call | tf_op jit(solution)/shard_map/weight_product/pallas_call | solution.py:566
  255.6 4.9 %weight_product.7 = (bf16[4,192,768]{2,1,0:T(8,128)(2,1)}, bf16[4,192,768]{2,1,0:T(8,128)(2,1)}) custom-call(s32[1]{0:T(128)} %bitcast.1.refs_0_.place_ref, bf16[512,1536]{1,0:T(8,128)(2,1)} %pad_maximum_fusion.2.refs_1_.x_ref, bf16[512,768]{1,0:T(8,128)(2,1)} %get-tuple-element.66.grad_ref), custom_call_target="tpu_custom_call" | custom-call | tf_op jit(solution)/shard_map/weight_product/pallas_call | solution.py:566
  260.5 8.3 %weight_product.8 = (bf16[4,192,896]{2,1,0:T(8,128)(2,1)}, bf16[4,192,896]{2,1,0:T(8,128)(2,1)}) custom-call(s32[1]{0:T(128)} %bitcast.1.refs_0_.place_ref, bf16[512,1536]{1,0:T(8,128)(2,1)} %pad_maximum_fusion.2.refs_1_.x_ref, bf16[512,896]{1,0:T(8,128)(2,1)} %get-tuple-element.68.grad_ref), custom_call_target="tpu_custom_call" | custom-call | tf_op jit(solution)/shard_map/weight_product/pallas_call | solution.py:566
  280.0 14.5 %collective-permute-done.49 = bf16[256,1536]{1,0:T(8,128)(2,1)} collective-permute-done((bf16[256,1536]{1,0:T(8,128)(2,1)}, bf16[256,1536]{1,0:T(8,128)(2,1)}, u32[]{:S(2)}, u32[]{:S(2)}) %collective-permute-start.49) | collective-permute-done | bytes 786464 | tf_op jit(solution)/shard_map/ppermute | solution.py:599
  297.0 4.1 convert_add_fusion.1
  311.8 7.0 %collective-permute-done.72 = bf16[2,96,1536]{2,1,0:T(8,128)(2,1)S(1)} collective-permute-done((bf16[2,96,1536]{2,1,0:T(8,128)(2,1)S(1)}, bf16[2,96,1536]{2,1,0:T(8,128)(2,1)S(1)}, u32[]{:S(2)}, u32[]{:S(2)}) %collective-permute-start.72) | collective-permute-done | bytes 589856 | tf_op jit(solution)/shard_map/ppermute | solution.py:599
  324.5 6.9 %collective-permute-done.59 = bf16[2,192,768]{2,1,0:T(8,128)(2,1)S(1)} collective-permute-done((bf16[2,192,768]{2,1,0:T(8,128)(2,1)S(1)}, bf16[2,192,768]{2,1,0:T(8,128)(2,1)S(1)}, u32[]{:S(2)}, u32[]{:S(2)}) %collective-permute-start.59) | collective-permute-done | bytes 589856 | tf_op jit(solution)/shard_map/ppermute | solution.py:599
  333.2 20.9 %collective-permute-done.76 = bf16[96,1536]{1,0:T(8,128)(2,1)S(1)} collective-permute-done((bf16[96,1536]{1,0:T(8,128)(2,1)S(1)}, bf16[96,1536]{1,0:T(8,128)(2,1)S(1)}, u32[]{:S(2)}, u32[]{:S(2)}) %collective-permute-start.76) | collective-permute-done | bytes 294944 | tf_op jit(solution)/shard_map/ppermute | solution.py:599
  359.5 3.5 collective-permute-done.60
  367.4 3.7 collective-permute-done.77
  383.1 26.7 %collective-permute-done.69 = bf16[192,256]{1,0:T(8,128)(2,1)S(1)} collective-permute-done((bf16[192,256]{1,0:T(8,128)(2,1)S(1)}, bf16[192,256]{1,0:T(8,128)(2,1)S(1)}, u32[]{:S(2)}, u32[]{:S(2)}) %collective-permute-start.69) | collective-permute-done | bytes 98336 | tf_op jit(solution)/shard_map/ppermute | solution.py:599
  (492 shorter events, 149.2 us)
Async XLA Ops:
  1.8 20.2 %collective-permute-start.8 = (bf16[96,1536]{1,0:T(8,128)(2,1)S(1)}, bf16[96,1536]{1,0:T(8,128)(2,1)S(1)}, u32[]{:S(2)}, u32[]{:S(2)}) collective-permute-start(bf16[96,1536]{1,0:T(8,128)(2,1)S(1)} %convert_element_type.255.refs_2_), channel_id=1, source_target_pairs={{0,2},{1,3},{2,0},{3,1},{4,6},{5,7},{6,4},{7,5},{8,10},{9,11},{10,... | collective-permute-start | bytes 884744 | tf_op jit(solution)/shard_map/ppermute | solution.py:599
  5.9 16.1 %collective-permute-start.1 = (bf16[96,1536]{1,0:T(8,128)(2,1)S(1)}, bf16[96,1536]{1,0:T(8,128)(2,1)S(1)}, u32[]{:S(2)}, u32[]{:S(2)}) collective-permute-start(bf16[96,1536]{1,0:T(8,128)(2,1)S(1)} %convert_element_type.255.refs_2_), channel_id=1, source_target_pairs={{0,8},{4,12},{8,0},{12,4},{16,24},{20,28},{24,16},{28,20},{1,9},{5... | collective-permute-start | bytes 884744 | tf_op jit(solution)/shard_map/ppermute | solution.py:599
  23.5 16.4 %collective-permute-start.17 = (bf16[192,1024]{1,0:T(8,128)(2,1)S(1)}, bf16[192,1024]{1,0:T(8,128)(2,1)}, u32[]{:S(2)}, u32[]{:S(2)}) collective-permute-start(bf16[192,1024]{1,0:T(8,128)(2,1)S(1)} %pad_maximum_fusion.8.refs_2_), channel_id=1, source_target_pairs={{0,8},{4,12},{8,0},{12,4},{16,24},{20,28},{24,16},{28,20},{1,9},{5... | collective-permute-start | bytes 1179656 | tf_op jit(solution)/shard_map/ppermute | solution.py:599
  24.3 17.3 %collective-permute-start.18 = (bf16[192,1024]{1,0:T(8,128)(2,1)S(1)}, bf16[192,1024]{1,0:T(8,128)(2,1)}, u32[]{:S(2)}, u32[]{:S(2)}) collective-permute-start(bf16[192,1024]{1,0:T(8,128)(2,1)S(1)} %pad_maximum_fusion.8.refs_2_), channel_id=1, source_target_pairs={{0,16},{4,20},{8,24},{12,28},{16,0},{20,4},{24,8},{28,12},{1,17},{... | collective-permute-start | bytes 1179656 | tf_op jit(solution)/shard_map/ppermute | solution.py:599
  41.6 26.9 %collective-permute-start.31 = (bf16[192,1664]{1,0:T(8,128)(2,1)S(1)}, bf16[192,1664]{1,0:T(8,128)(2,1)S(1)}, u32[]{:S(2)}, u32[]{:S(2)}) collective-permute-start(bf16[192,1664]{1,0:T(8,128)(2,1)S(1)} %pad_maximum_fusion.6), channel_id=1, source_target_pairs={{0,2},{1,3},{2,0},{3,1},{4,6},{5,7},{6,4},{7,5},{8,10},{9,11},{10,... | collective-permute-start | bytes 1916936 | tf_op jit(solution)/shard_map/ppermute | solution.py:599
  41.7 33.1 %collective-permute-start.16 = (bf16[256,1536]{1,0:T(8,128)(2,1)S(1)}, bf16[256,1536]{1,0:T(8,128)(2,1)S(1)}, u32[]{:S(2)}, u32[]{:S(2)}) collective-permute-start(bf16[256,1536]{1,0:T(8,128)(2,1)S(1)} %fusion.6), channel_id=1, source_target_pairs={{0,1},{1,0},{2,3},{3,2},{4,5},{5,4},{6,7},{7,6},{8,9},{9,8},{10,11... | collective-permute-start | bytes 2359304 | tf_op jit(solution)/shard_map/ppermute | solution.py:599
  48.2 20.3 %collective-permute-start.26 = (bf16[192,896]{1,0:T(8,128)(2,1)}, bf16[192,896]{1,0:T(8,128)(2,1)S(1)}, u32[]{:S(2)}, u32[]{:S(2)}) collective-permute-start(bf16[192,896]{1,0:T(8,128)(2,1)} %collective-permute-done.25.refs_12_), channel_id=1, source_target_pairs={{0,8},{4,12},{8,0},{12,4},{16,24},{20,28},{24,16},{28,20},{1,9},{5... | collective-permute-start | bytes 1032200 | tf_op jit(solution)/shard_map/ppermute | solution.py:599
  51.2 37.4 %collective-permute-start = (bf16[256,1536]{1,0:T(8,128)(2,1)S(1)}, bf16[256,1536]{1,0:T(8,128)(2,1)S(1)}, u32[]{:S(2)}, u32[]{:S(2)}) collective-permute-start(bf16[256,1536]{1,0:T(8,128)(2,1)S(1)} %fusion.5), channel_id=1, source_target_pairs={{0,1},{1,0},{2,3},{3,2},{4,5},{5,4},{6,7},{7,6},{8,9},{9,8},{10,11... | collective-permute-start | bytes 2359304 | tf_op jit(solution)/shard_map/ppermute | solution.py:599
  51.9 17.6 %collective-permute-start.29 = (bf16[192,896]{1,0:T(8,128)(2,1)}, bf16[192,896]{1,0:T(8,128)(2,1)}, u32[]{:S(2)}, u32[]{:S(2)}) collective-permute-start(bf16[192,896]{1,0:T(8,128)(2,1)} %collective-permute-done.25.refs_12_), channel_id=1, source_target_pairs={{0,4},{4,0},{8,12},{12,8},{16,20},{20,16},{24,28},{28,24},{1,5},{5... | collective-permute-start | bytes 1032200 | tf_op jit(solution)/shard_map/ppermute | solution.py:599
  74.8 16.4 %collective-permute-start.11 = (bf16[96,1536]{1,0:T(8,128)(2,1)S(1)}, bf16[96,1536]{1,0:T(8,128)(2,1)S(1)}, u32[]{:S(2)}, u32[]{:S(2)}) collective-permute-start(bf16[96,1536]{1,0:T(8,128)(2,1)S(1)} %collective-permute-done.10.refs_12_), channel_id=1, source_target_pairs={{0,8},{4,12},{8,0},{12,4},{16,24},{20,28},{24,16},{28,20},{1,9},{5... | collective-permute-start | bytes 884744 | tf_op jit(solution)/shard_map/ppermute | solution.py:599
  116.8 30.6 %collective-permute-start.6 = (bf16[96,1536]{1,0:T(8,128)(2,1)S(1)}, bf16[96,1536]{1,0:T(8,128)(2,1)S(1)}, u32[]{:S(2)}, u32[]{:S(2)}) collective-permute-start(bf16[96,1536]{1,0:T(8,128)(2,1)S(1)} %copy-done.56), channel_id=1, source_target_pairs={{0,4},{4,0},{8,12},{12,8},{16,20},{20,16},{24,28},{28,24},{1,5},{5... | collective-permute-start | bytes 884744 | tf_op jit(solution)/shard_map/ppermute | solution.py:599
  117.4 30.1 %collective-permute-start.14 = (bf16[96,1536]{1,0:T(8,128)(2,1)S(1)}, bf16[96,1536]{1,0:T(8,128)(2,1)S(1)}, u32[]{:S(2)}, u32[]{:S(2)}) collective-permute-start(bf16[96,1536]{1,0:T(8,128)(2,1)S(1)} %copy-done.59), channel_id=1, source_target_pairs={{0,4},{4,0},{8,12},{12,8},{16,20},{20,16},{24,28},{28,24},{1,5},{5... | collective-permute-start | bytes 884744 | tf_op jit(solution)/shard_map/ppermute | solution.py:599
  117.5 30.0 %collective-permute-start.13 = (bf16[96,1536]{1,0:T(8,128)(2,1)S(1)}, bf16[96,1536]{1,0:T(8,128)(2,1)S(1)}, u32[]{:S(2)}, u32[]{:S(2)}) collective-permute-start(bf16[96,1536]{1,0:T(8,128)(2,1)S(1)} %copy-done.61), channel_id=1, source_target_pairs={{0,4},{4,0},{8,12},{12,8},{16,20},{20,16},{24,28},{28,24},{1,5},{5... | collective-permute-start | bytes 884744 | tf_op jit(solution)/shard_map/ppermute | solution.py:599
  117.9 29.6 %collective-permute-start.7 = (bf16[96,1536]{1,0:T(8,128)(2,1)S(1)}, bf16[96,1536]{1,0:T(8,128)(2,1)S(1)}, u32[]{:S(2)}, u32[]{:S(2)}) collective-permute-start(bf16[96,1536]{1,0:T(8,128)(2,1)S(1)} %copy-done.63), channel_id=1, source_target_pairs={{0,4},{4,0},{8,12},{12,8},{16,20},{20,16},{24,28},{28,24},{1,5},{5... | collective-permute-start | bytes 884744 | tf_op jit(solution)/shard_map/ppermute | solution.py:599
  118.1 29.4 %collective-permute-start.15 = (bf16[96,1536]{1,0:T(8,128)(2,1)S(1)}, bf16[96,1536]{1,0:T(8,128)(2,1)S(1)}, u32[]{:S(2)}, u32[]{:S(2)}) collective-permute-start(bf16[96,1536]{1,0:T(8,128)(2,1)S(1)} %copy-done.67), channel_id=1, source_target_pairs={{0,4},{4,0},{8,12},{12,8},{16,20},{20,16},{24,28},{28,24},{1,5},{5... | collective-permute-start | bytes 884744 | tf_op jit(solution)/shard_map/ppermute | solution.py:599
  166.6 129.8 %collective-permute-start.47 = (bf16[256,1536]{1,0:T(8,128)(2,1)}, bf16[256,1536]{1,0:T(8,128)(2,1)}, u32[]{:S(2)}, u32[]{:S(2)}) collective-permute-start(bf16[256,1536]{1,0:T(8,128)(2,1)} %slice.288), channel_id=1, source_target_pairs={{0,1},{1,0},{2,3},{3,2},{4,5},{5,4},{6,7},{7,6},{8,9},{9,8},{10,11... | collective-permute-start | bytes 2359304 | tf_op jit(solution)/shard_map/ppermute | solution.py:599
  224.9 45.7 %collective-permute-start.54 = (f32[28,128]{1,0:T(8,128)S(1)}, f32[28,128]{1,0:T(8,128)S(1)}, u32[]{:S(2)}, u32[]{:S(2)}) collective-permute-start(f32[28,128]{1,0:T(8,128)S(1)} %slice_add_fusion.6), channel_id=1, source_target_pairs={{0,2},{1,3},{2,0},{3,1},{4,6},{5,7},{6,4},{7,5},{8,10},{9,11},{10,... | collective-permute-start | bytes 43016 | tf_op jit(solution)/shard_map/ppermute | solution.py:599
  269.0 32.1 %collective-permute-start.71 = (bf16[4,96,1536]{2,1,0:T(8,128)(2,1)}, bf16[4,96,1536]{2,1,0:T(8,128)(2,1)}, u32[]{:S(2)}, u32[]{:S(2)}) collective-permute-start(bf16[4,96,1536]{2,1,0:T(8,128)(2,1)} %get-tuple-element.93), channel_id=1, source_target_pairs={{0,4},{4,0},{8,12},{12,8},{16,20},{20,16},{24,28},{28,24},{1,5},{5... | collective-permute-start | bytes 3538952 | tf_op jit(solution)/shard_map/ppermute | solution.py:599
  269.0 33.5 %collective-permute-start.74 = (bf16[4,96,1536]{2,1,0:T(8,128)(2,1)}, bf16[4,96,1536]{2,1,0:T(8,128)(2,1)}, u32[]{:S(2)}, u32[]{:S(2)}) collective-permute-start(bf16[4,96,1536]{2,1,0:T(8,128)(2,1)} %get-tuple-element.95), channel_id=1, source_target_pairs={{0,4},{4,0},{8,12},{12,8},{16,20},{20,16},{24,28},{28,24},{1,5},{5... | collective-permute-start | bytes 3538952 | tf_op jit(solution)/shard_map/ppermute | solution.py:599
  269.5 39.2 %collective-permute-start.55 = (bf16[4,192,1024]{2,1,0:T(8,128)(2,1)}, bf16[4,192,1024]{2,1,0:T(8,128)(2,1)}, u32[]{:S(2)}, u32[]{:S(2)}) collective-permute-start(bf16[4,192,1024]{2,1,0:T(8,128)(2,1)} %get-tuple-element.84), channel_id=1, source_target_pairs={{0,4},{4,0},{8,12},{12,8},{16,20},{20,16},{24,28},{28,24},{1,5},{5... | collective-permute-start | bytes 4718600 | tf_op jit(solution)/shard_map/ppermute | solution.py:599
  275.4 19.1 %collective-permute-start.49 = (bf16[256,1536]{1,0:T(8,128)(2,1)}, bf16[256,1536]{1,0:T(8,128)(2,1)}, u32[]{:S(2)}, u32[]{:S(2)}) collective-permute-start(bf16[256,1536]{1,0:T(8,128)(2,1)} %slice.377), channel_id=1, source_target_pairs={{0,1},{1,0},{2,3},{3,2},{4,5},{5,4},{6,7},{7,6},{8,9},{9,8},{10,11... | collective-permute-start | bytes 2359304 | tf_op jit(solution)/shard_map/ppermute | solution.py:599
  302.5 16.3 %collective-permute-start.72 = (bf16[2,96,1536]{2,1,0:T(8,128)(2,1)S(1)}, bf16[2,96,1536]{2,1,0:T(8,128)(2,1)S(1)}, u32[]{:S(2)}, u32[]{:S(2)}) collective-permute-start(bf16[2,96,1536]{2,1,0:T(8,128)(2,1)S(1)} %add_convert_fusion.4), channel_id=1, source_target_pairs={{0,8},{4,12},{8,0},{12,4},{16,24},{20,28},{24,16},{28,20},{1,9},{5... | collective-permute-start | bytes 1769480 | tf_op jit(solution)/shard_map/ppermute | solution.py:599
  305.4 16.3 %collective-permute-start.75 = (bf16[2,96,1536]{2,1,0:T(8,128)(2,1)S(1)}, bf16[2,96,1536]{2,1,0:T(8,128)(2,1)S(1)}, u32[]{:S(2)}, u32[]{:S(2)}) collective-permute-start(bf16[2,96,1536]{2,1,0:T(8,128)(2,1)S(1)} %add_convert_fusion.3), channel_id=1, source_target_pairs={{0,16},{4,20},{8,24},{12,28},{16,0},{20,4},{24,8},{28,12},{1,17},{... | collective-permute-start | bytes 1769480 | tf_op jit(solution)/shard_map/ppermute | solution.py:599
  307.2 24.3 %collective-permute-start.59 = (bf16[2,192,768]{2,1,0:T(8,128)(2,1)S(1)}, bf16[2,192,768]{2,1,0:T(8,128)(2,1)S(1)}, u32[]{:S(2)}, u32[]{:S(2)}) collective-permute-start(bf16[2,192,768]{2,1,0:T(8,128)(2,1)S(1)} %add_convert_fusion.5), channel_id=1, source_target_pairs={{0,8},{4,12},{8,0},{12,4},{16,24},{20,28},{24,16},{28,20},{1,9},{5... | collective-permute-start | bytes 1769480 | tf_op jit(solution)/shard_map/ppermute | solution.py:599
  308.0 47.7 %collective-permute-start.66 = (bf16[2,192,896]{2,1,0:T(8,128)(2,1)S(1)}, bf16[2,192,896]{2,1,0:T(8,128)(2,1)S(1)}, u32[]{:S(2)}, u32[]{:S(2)}) collective-permute-start(bf16[2,192,896]{2,1,0:T(8,128)(2,1)S(1)} %add_convert_fusion.1), channel_id=1, source_target_pairs={{0,16},{4,20},{8,24},{12,28},{16,0},{20,4},{24,8},{28,12},{1,17},{... | collective-permute-start | bytes 2064392 | tf_op jit(solution)/shard_map/ppermute | solution.py:599
  308.7 48.9 %collective-permute-start.62 = (bf16[2,192,896]{2,1,0:T(8,128)(2,1)S(1)}, bf16[2,192,896]{2,1,0:T(8,128)(2,1)S(1)}, u32[]{:S(2)}, u32[]{:S(2)}) collective-permute-start(bf16[2,192,896]{2,1,0:T(8,128)(2,1)S(1)} %add_convert_fusion.2), channel_id=1, source_target_pairs={{0,16},{4,20},{8,24},{12,28},{16,0},{20,4},{24,8},{28,12},{1,17},{... | collective-permute-start | bytes 2064392 | tf_op jit(solution)/shard_map/ppermute | solution.py:599
  318.8 45.3 %collective-permute-start.56 = (bf16[2,192,1024]{2,1,0:T(8,128)(2,1)S(1)}, bf16[2,192,1024]{2,1,0:T(8,128)(2,1)S(1)}, u32[]{:S(2)}, u32[]{:S(2)}) collective-permute-start(bf16[2,192,1024]{2,1,0:T(8,128)(2,1)S(1)} %add_convert_fusion), channel_id=1, source_target_pairs={{0,8},{4,12},{8,0},{12,4},{16,24},{20,28},{24,16},{28,20},{1,9},{5... | collective-permute-start | bytes 2359304 | tf_op jit(solution)/shard_map/ppermute | solution.py:599
  321.7 45.8 %collective-permute-start.73 = (bf16[96,1536]{1,0:T(8,128)(2,1)S(1)}, bf16[96,1536]{1,0:T(8,128)(2,1)S(1)}, u32[]{:S(2)}, u32[]{:S(2)}) collective-permute-start(bf16[96,1536]{1,0:T(8,128)(2,1)S(1)} %fusion.37), channel_id=1, source_target_pairs={{0,16},{4,20},{8,24},{12,28},{16,0},{20,4},{24,8},{28,12},{1,17},{... | collective-permute-start | bytes 884744 | tf_op jit(solution)/shard_map/ppermute | solution.py:599
  331.5 22.6 %collective-permute-start.76 = (bf16[96,1536]{1,0:T(8,128)(2,1)S(1)}, bf16[96,1536]{1,0:T(8,128)(2,1)S(1)}, u32[]{:S(2)}, u32[]{:S(2)}) collective-permute-start(bf16[96,1536]{1,0:T(8,128)(2,1)S(1)} %fusion.38), channel_id=1, source_target_pairs={{0,8},{4,12},{8,0},{12,4},{16,24},{20,28},{24,16},{28,20},{1,9},{5... | collective-permute-start | bytes 884744 | tf_op jit(solution)/shard_map/ppermute | solution.py:599
  357.6 25.3 %collective-permute-start.67 = (bf16[192,896]{1,0:T(8,128)(2,1)S(1)}, bf16[192,896]{1,0:T(8,128)(2,1)S(1)}, u32[]{:S(2)}, u32[]{:S(2)}) collective-permute-start(bf16[192,896]{1,0:T(8,128)(2,1)S(1)} %fusion.35), channel_id=1, source_target_pairs={{0,8},{4,12},{8,0},{12,4},{16,24},{20,28},{24,16},{28,20},{1,9},{5... | collective-permute-start | bytes 1032200 | tf_op jit(solution)/shard_map/ppermute | solution.py:599
  377.4 34.1 %collective-permute-start.64 = (bf16[192,1664]{1,0:T(8,128)(2,1)S(1)}, bf16[192,1664]{1,0:T(8,128)(2,1)S(1)}, u32[]{:S(2)}, u32[]{:S(2)}) collective-permute-start(bf16[192,1664]{1,0:T(8,128)(2,1)S(1)} %pad_maximum_fusion.7), channel_id=1, source_target_pairs={{0,2},{1,3},{2,0},{3,1},{4,6},{5,7},{6,4},{7,5},{8,10},{9,11},{10,... | collective-permute-start | bytes 1916936 | tf_op jit(solution)/shard_map/ppermute | solution.py:599
  380.5 29.3 %collective-permute-start.69 = (bf16[192,256]{1,0:T(8,128)(2,1)S(1)}, bf16[192,256]{1,0:T(8,128)(2,1)S(1)}, u32[]{:S(2)}, u32[]{:S(2)}) collective-permute-start(bf16[192,256]{1,0:T(8,128)(2,1)S(1)} %fusion.45), channel_id=1, source_target_pairs={{0,2},{1,3},{2,0},{3,1},{4,6},{5,7},{6,4},{7,5},{8,10},{9,11},{10,... | collective-permute-start | bytes 294920 | tf_op jit(solution)/shard_map/ppermute | solution.py:599
  (156 other events, 2011.5 us)

commit v3 on v2

v3 whole, which is shorter than its diff:
```python
import functools
from types import SimpleNamespace

import jax
import jax.numpy as jnp
from jax import lax
from jax.experimental import pallas as pl
from jax.experimental.pallas import tpu as pltpu
from jax.sharding import PartitionSpec as P


norm_eps = 1e-05
beta_one = 0.9
beta_two = 0.95
adam_eps = 1e-08
step_count = 3.0
rate_matrix = 0.005
rate_vector = 0.2
weight_decay = 0.1
lanes = 128
HEAD = "head"
DP = "dp"
sub = 8
f32 = jnp.float32
bf16 = jnp.bfloat16


def dot(lhs, rhs, over=(1, 0)):
    return lax.dot_general(
        lhs, rhs, (((over[0],), (over[1],)), ((), ())), preferred_element_type=f32
    )


def dot_exact(lhs, rhs, over=(1, 0)):
    return lax.dot_general(
        lhs,
        rhs,
        (((over[0],), (over[1],)), ((), ())),
        precision=lax.Precision.HIGHEST,
        preferred_element_type=f32,
    )


def iota(shape, axis):
    return lax.broadcasted_iota(jnp.int32, shape, axis)


def later(values, count):
    if count == 0:
        return values
    rolled = pltpu.roll(values, count, 0)
    return jnp.where(iota(values.shape, 0) >= count, rolled, 0.0)


def earlier(values, count):
    if count == 0:
        return values
    length = values.shape[0]
    rolled = pltpu.roll(values, length - count, 0)
    return jnp.where(iota(values.shape, 0) < length - count, rolled, 0.0)


def conv(values, taps, kernel):
    summed = taps[kernel : kernel + 1] + taps[kernel - 1 : kernel] * values
    for offset in range(kernel - 1):
        summed = summed + taps[offset : offset + 1] * later(values, kernel - 1 - offset)
    return summed


def conv_back(grads, taps, kernel):
    summed = taps[kernel - 1 : kernel] * grads
    for offset in range(kernel - 1):
        summed = summed + taps[offset : offset + 1] * earlier(grads, kernel - 1 - offset)
    return summed


def conv_sums(grads, values, kernel):
    rows = [
        jnp.sum(grads * later(values, kernel - 1 - offset), axis=0, keepdims=True)
        for offset in range(kernel)
    ]
    rows.append(jnp.sum(grads, axis=0, keepdims=True))
    return rows


def sigmoid(values):
    return 1.0 / (1.0 + jnp.exp(-values))


def shared_parts(bc_rows, step_raw, cbc_ref, head_ref, state, kernel):
    step_raw = step_raw + head_ref[1:2, :]
    length = bc_rows.shape[0]
    bc_pre = conv(bc_rows, cbc_ref, kernel)
    bc_sig = sigmoid(bc_pre)
    shared = bc_pre * bc_sig
    step = jnp.maximum(step_raw, 0.0) + jnp.log1p(jnp.exp(-jnp.abs(step_raw)))
    rate = -jnp.exp(head_ref[0:1, :])
    lower = (iota((length, length), 0) >= iota((length, length), 1)).astype(f32)
    cum = dot_exact(lower, step * rate)
    in_map = shared[:, :state].astype(bf16)
    out_map = shared[:, state:].astype(bf16)
    scores = dot(out_map, in_map, (1, 1)) * lower
    return SimpleNamespace(
        bc_rows=bc_rows,
        bc_pre=bc_pre,
        bc_sig=bc_sig,
        step_raw=step_raw,
        step=step,
        rate=rate,
        cum=cum,
        cum_t=cum.T,
        in_map=in_map,
        out_map=out_map,
        scores=scores,
    )


def pick(values, pair, first):
    return jnp.where(
        first, values[:, 2 * pair : 2 * pair + 1], values[:, 2 * pair + 1 : 2 * pair + 2]
    )


def blocks_of(length):
    half = length // 2
    return [((0, half), (0, half)), ((half, length), (0, length))]


def place_pieces(place, pieces, target, sems):
    copies = []
    for at, (mask, ref) in enumerate(pieces):
        rows = ref.shape[0]
        start = pl.multiple_of((place ^ mask) * rows, 32)
        copies.append(
            pltpu.make_async_copy(ref, target.at[pl.ds(start, rows), :], sems.at[at])
        )
    for copy in copies:
        copy.start()
    return copies


piece_masks = (0, 2, 4, 6, 1, 3, 5, 7)


def forward_kernel(*refs, inner, state, kernel, split, primary):
    if split:
        place_ref, x_ref, peer_ref = refs[:3]
        pieces_a, pieces_b = refs[3:11], refs[11:19]
        rest = refs[19:]
    else:
        x_ref, wa_ref, wb_ref = refs[:3]
        rest = refs[3:]
    if not primary:
        bc_ref = rest[0]
        rest = rest[1:]
    taps_ref, cbc_ref, proja_ref, projb_ref, y_ref, gated_ref = rest[:6]
    head_ref = taps_ref.at[:, pl.ds(inner, lanes)]
    if split:
        wa_ref, wb_ref = rest[6:8]
        sems = rest[-1]

        @pl.when(pl.program_id(0) == 0)
        def assemble():
            place = place_ref[0]
            copies = place_pieces(place, list(zip(piece_masks, pieces_a)), wa_ref, sems.at[0])
            copies = copies + place_pieces(
                place, list(zip(piece_masks, pieces_b)), wb_ref, sems.at[1]
            )
            for copy in copies:
                copy.wait()

    length = x_ref.shape[0]
    rows = x_ref[...]
    if split:
        rows = jnp.where(pl.program_id(0) == 0, rows, peer_ref[...])
        if primary:
            turned_ref = rest[8]
            for start in range(0, rows.shape[1], lanes):
                turned_ref[start : start + lanes, :] = (
                    rows[:, start : start + lanes].astype(f32).T.astype(bf16)
                )
    for weights, target in ((wa_ref, proja_ref), (wb_ref, projb_ref)):
        width = weights.shape[1]
        for start in range(0, width, 256):
            stop = min(width, start + 256)
            target[:, start:stop] = dot(rows, weights[:, start:stop])
    bc_rows = proja_ref[:, inner:] if primary else bc_ref[...]
    part = shared_parts(bc_rows, projb_ref[:, inner:], cbc_ref, head_ref, state, kernel)
    step, cum, cum_t, scores = part.step, part.cum, part.cum_t, part.scores
    first = iota((length, lanes), 1) < lanes // 2
    for pair in range(inner // lanes):
        cols = slice(pair * lanes, (pair + 1) * lanes)
        taps = taps_ref[:, cols]
        gate = proja_ref[:, cols]
        values = conv(projb_ref[:, cols], taps, kernel)
        values = values * sigmoid(values)
        scaled = values * pick(step, pair, first)
        halves = (
            jnp.where(first, scaled, 0.0).astype(bf16),
            jnp.where(first, 0.0, scaled).astype(bf16),
        )
        pieces = []
        for (r0, r1), (c0, c1) in blocks_of(length):
            total = None
            for side in range(2):
                head = 2 * pair + side
                gap = cum[r0:r1, head : head + 1] - cum_t[head : head + 1, c0:c1]
                weights = (scores[r0:r1, c0:c1] * jnp.exp(jnp.minimum(gap, 0.0))).astype(bf16)
                term = dot(weights, halves[side][c0:c1])
                total = term if total is None else total + term
            pieces.append(total)
        output = jnp.concatenate(pieces, axis=0)
        y_ref[:, cols] = output
        gated_ref[:, cols] = (output + taps[kernel + 2 : kernel + 3] * values) * (
            gate * sigmoid(gate)
        )


def gate_kernel(*refs, kernel, split, blocks):
    if split:
        place_ref, cot_ref, peer_ref = refs[:3]
        pieces = [refs[3 + 8 * at : 11 + 8 * at] for at in range(blocks)]
        rest = refs[3 + 8 * blocks :]
    else:
        cot_ref = refs[0]
        out_refs = refs[1 : 1 + blocks]
        rest = refs[1 + blocks :]
    gated_refs, taps_refs = rest[:blocks], rest[blocks : 2 * blocks]
    grad_refs = rest[2 * blocks : 3 * blocks]
    stats_ref, turned_ref = rest[3 * blocks : 3 * blocks + 2]
    rest = rest[3 * blocks + 2 :]
    lifted_refs = rest[:blocks]
    if split:
        out_refs = rest[blocks : 2 * blocks]
        sems = rest[2 * blocks]

        @pl.when(pl.program_id(0) == 0)
        def assemble():
            place = place_ref[0]
            copies = []
            for at in range(blocks):
                copies = copies + place_pieces(
                    place, list(zip(piece_masks, pieces[at])), out_refs[at], sems.at[at]
                )
            for copy in copies:
                copy.wait()

    cot = cot_ref[...]
    if split:
        cot = jnp.where(pl.program_id(0) == 0, cot, peer_ref[...])
    squares, cross = None, None
    for at in range(blocks):
        grad = dot(cot, out_refs[at][...], (1, 1))
        grad_refs[at][...] = grad
        inner = grad.shape[1]
        for start in range(0, inner, lanes):
            cols = slice(start, start + lanes)
            gated = gated_refs[at][:, cols]
            lifted = gated * taps_refs[at][kernel + 1 : kernel + 2, cols]
            lifted_refs[at][:, cols] = lifted.astype(bf16)
            turned_ref[at * inner + start : at * inner + start + lanes, :] = lifted.T.astype(bf16)
            square, product = gated * gated, grad[:, cols] * lifted
            squares = square if squares is None else squares + square
            cross = product if cross is None else cross + product
    ones = jnp.ones((sub, lanes), f32)
    squares = dot_exact(ones, squares, (1, 1))
    cross = dot_exact(ones, cross, (1, 1))
    stats_ref[...] = jnp.where(iota(squares.shape, 0) == 0, squares, cross)


def backward_kernel(*refs, inner, state, kernel, inner_all, stat_parts, primary, joined):
    stat_refs = refs[:stat_parts]
    proja_ref, projb_ref = refs[stat_parts : stat_parts + 2]
    rest = refs[stat_parts + 2 :]
    if not primary:
        bc_ref = rest[0]
        rest = rest[1:]
    if joined:
        joined_ref = rest[0]
        rest = rest[1:]
    y_ref, grad_ref, taps_ref, cbc_ref, cota_ref, cotb_ref, tap_sums_ref = rest[:7]
    bc_out_ref, score_ref = rest[7:9]
    head_ref = taps_ref.at[:, pl.ds(inner, lanes)]
    length = proja_ref.shape[0]
    half_lanes = lanes // 2

    @pl.when(pl.program_id(0) == 0)
    def clear():
        tap_sums_ref[...] = jnp.zeros(tap_sums_ref.shape, f32)
        if primary:
            bc_out_ref[...] = jnp.zeros(bc_out_ref.shape, f32)

    stats = stat_refs[0][...]
    for more in stat_refs[1:]:
        stats = stats + more[...]
    unit = (iota((length, length), 0) == iota((length, length), 1)).astype(f32)
    columns = dot_exact(unit, stats, (1, 1))
    inv = lax.rsqrt(columns[:, 0:1] / inner_all + norm_eps)
    pull = inv * inv * inv * columns[:, 1:2] / inner_all

    bc_rows = proja_ref[:, inner:] if primary else bc_ref[...]
    part = shared_parts(bc_rows, projb_ref[:, inner:], cbc_ref, head_ref, state, kernel)
    step, cum, cum_t, scores = part.step, part.cum, part.cum_t, part.scores
    first = iota((length, lanes), 1) < half_lanes
    score_ref[...] = jnp.zeros(score_ref.shape, f32)
    cum_grad = jnp.zeros((length, lanes), f32)
    step_grad = jnp.zeros((length, lanes), f32)
    for pair in range(inner // lanes):
        cols = slice(pair * lanes, (pair + 1) * lanes)
        taps = taps_ref[:, cols]
        gain = taps[kernel + 1 : kernel + 2]
        skip = taps[kernel + 2 : kernel + 3]
        gate = proja_ref[:, cols]
        raw = projb_ref[:, cols]
        pre = conv(raw, taps, kernel)
        pre_sig = sigmoid(pre)
        values = pre * pre_sig
        spread = pick(step, pair, first)
        scaled = values * spread
        gate_sig = sigmoid(gate)
        lift = gate * gate_sig
        plain = y_ref[:, cols]
        output = plain + skip * values
        gated = output * lift
        normed = gated * inv
        grad = grad_ref[:, cols]
        gain_row = jnp.sum(grad * normed, axis=0, keepdims=True)
        gated_grad = inv * (grad * gain) - gated * pull
        cota_ref[:, cols] = (
            gated_grad * output * (gate_sig * (1.0 + gate * (1.0 - gate_sig)))
        ).astype(bf16)
        out_grad = gated_grad * lift
        skip_row = jnp.sum(out_grad * values, axis=0, keepdims=True)
        out_low = out_grad.astype(bf16)
        scaled_low = scaled.astype(bf16)
        zero = jnp.zeros_like(out_low)
        sides = (jnp.where(first, out_low, zero), jnp.where(first, zero, out_low))
        half = length // 2
        pulled = [jnp.zeros((half, lanes), f32), jnp.zeros((half, lanes), f32)]
        for (r0, r1), (c0, c1) in blocks_of(length):
            score_sum = score_ref[r0:r1, c0:c1]
            for side in range(2):
                head = 2 * pair + side
                gap = cum[r0:r1, head : head + 1] - cum_t[head : head + 1, c0:c1]
                decay = jnp.exp(jnp.minimum(gap, 0.0))
                weights = (scores[r0:r1, c0:c1] * decay).astype(bf16)
                score_sum = score_sum + dot(sides[side][r0:r1], scaled_low[c0:c1], (1, 1)) * decay
                back = dot(weights, sides[side][r0:r1], (0, 0))
                pulled[0] = pulled[0] + back[:half]
                if c1 > half:
                    pulled[1] = pulled[1] + back[half:]
            score_ref[r0:r1, c0:c1] = score_sum
        scaled_grad = jnp.concatenate(pulled, axis=0)
        hot = (
            2 * pair + (iota((lanes, lanes), 0) >= half_lanes).astype(jnp.int32)
            == iota((lanes, lanes), 1)
        ).astype(f32)
        balance = out_low.astype(f32) * plain - scaled_low.astype(f32) * scaled_grad
        cum_grad = cum_grad + dot_exact(balance, hot)
        step_grad = step_grad + dot_exact(values * scaled_grad, hot)
        value_grad = skip * out_grad + scaled_grad * spread
        pre_grad = value_grad * (pre_sig * (1.0 + pre * (1.0 - pre_sig)))
        cotb_ref[:, cols] = conv_back(pre_grad, taps, kernel).astype(bf16)
        rows = conv_sums(pre_grad, raw, kernel) + [gain_row, skip_row]
        rows = rows + [jnp.zeros_like(gain_row)] * (tap_sums_ref.shape[0] - len(rows))
        tap_sums_ref[:, cols] = tap_sums_ref[:, cols] + jnp.concatenate(rows, axis=0)

    lower = iota((length, length), 0) >= iota((length, length), 1)
    score_low = jnp.where(lower, score_ref[...], 0.0).astype(bf16)
    shared_grad = jnp.concatenate(
        [dot(score_low, part.out_map, (0, 0)), dot(score_low, part.in_map)], axis=1
    )
    if joined:
        shared_grad = shared_grad + joined_ref[...]
    if primary:
        bc_pre, bc_sig = part.bc_pre, part.bc_sig
        bc_grad = shared_grad * (bc_sig * (1.0 + bc_pre * (1.0 - bc_sig)))
        cota_ref[:, inner:] = conv_back(bc_grad, cbc_ref, kernel).astype(bf16)
        rows = conv_sums(bc_grad, part.bc_rows, kernel)
        rows = rows + [jnp.zeros_like(rows[0])] * (bc_out_ref.shape[0] - len(rows))
        bc_out_ref[...] = bc_out_ref[...] + jnp.concatenate(rows, axis=0)
    else:
        bc_out_ref[...] = shared_grad
    decay_grad = dot_exact(lower.astype(f32), cum_grad, (0, 0))
    raw_grad = (step_grad + decay_grad * part.rate) * sigmoid(part.step_raw)
    cotb_ref[:, inner:] = raw_grad.astype(bf16)
    rows = [
        part.rate * jnp.sum(step * decay_grad, axis=0, keepdims=True),
        jnp.sum(raw_grad, axis=0, keepdims=True),
    ]
    rows = rows + [jnp.zeros_like(rows[0])] * (tap_sums_ref.shape[0] - len(rows))
    tap_sums_ref[:, inner:] = tap_sums_ref[:, inner:] + jnp.concatenate(rows, axis=0)


def product_kernel(*refs, order, scaled, inner_all):
    if scaled:
        place_ref, turned_ref, mine_ref, peer_ref, grad_ref, more_ref = refs[:6]
        keep_ref, send_ref, sum_ref, scaled_ref = refs[6:]

        @pl.when(pl.program_id(0) == 0)
        def scale():
            half = turned_ref.shape[1] // 2
            for slot in range(2):
                mine = mine_ref[slot * sub : slot * sub + 1, :]
                peer = peer_ref[(1 - slot) * sub : (1 - slot) * sub + 1, :]
                row = lax.rsqrt((mine + peer) / inner_all + norm_eps)
                cols = slice(slot * half, (slot + 1) * half)
                scaled_ref[:, cols] = (turned_ref[:, cols].astype(f32) * row).astype(bf16)

        half = turned_ref.shape[1] // 2
        product = dot(scaled_ref[:, :half], grad_ref[...]) + dot(
            scaled_ref[:, half:], more_ref[...]
        )
    else:
        place_ref, turned_ref, grad_ref, keep_ref, send_ref, sum_ref = refs
        product = dot(turned_ref[...], grad_ref[...])
    place = place_ref[0]
    rows = keep_ref.shape[1]
    sum_ref[...] = product.astype(bf16)
    for at, mask in enumerate(order):
        start = pl.multiple_of((place ^ mask) * rows, 32)
        keep_ref[at] = sum_ref[pl.ds(start, rows), :]
        start = pl.multiple_of((place ^ mask ^ 1) * rows, 32)
        send_ref[at] = sum_ref[pl.ds(start, rows), :]


def whole(array):
    return pl.BlockSpec(array.shape, lambda step, *_: (0,) * array.ndim, pipeline_mode=pl.Buffered(1))


def rows_spec(length, width, column=0):
    return pl.BlockSpec((length, width), lambda step, *_: (step, column))


def fixed_spec(shape):
    return pl.BlockSpec(shape, lambda step, *_: (0,) * len(shape))


def any_spec():
    return pl.BlockSpec(memory_space=pl.ANY)


def stat_spec(length, slots, back):
    return pl.BlockSpec((sub, length), lambda step, *_: (lax.rem(step + slots - back, slots), 0))


def call_params(kinds=("arbitrary",)):
    return pltpu.CompilerParams(dimension_semantics=kinds, vmem_limit_bytes=56 * 1024 * 1024)


def run_forward(place, normed, weights, bc_from, tables, seq_len, state, kernel):
    table, _ = tables
    inner = table.shape[1] - lanes
    split = isinstance(weights[0], (list, tuple))
    primary = bc_from is None
    depth = normed[0].shape[1]
    rows = sum(part.shape[0] for part in normed)
    if split:
        widths = [group[0].shape[1] for group in weights]
        prefix, ins = [place], [*normed, *weights[0], *weights[1]]
        specs = [whole(part) for part in normed] + [any_spec()] * 16
    else:
        widths = [array.shape[1] for array in weights]
        prefix, ins = [], [*normed, *weights]
        specs = [rows_spec(seq_len, depth)] + [whole(array) for array in weights]
    if not primary:
        ins.append(bc_from)
        specs.append(rows_spec(seq_len, 2 * state, inner // (2 * state)))
    for array in tables:
        ins.append(array)
        specs.append(whole(array))
    outs = [(widths[0], f32), (widths[1], f32), (inner, f32), (inner, f32)]
    out_specs = [rows_spec(seq_len, width) for width, _ in outs]
    out_shape = [jax.ShapeDtypeStruct((rows, width), kind) for width, kind in outs]
    scratch = []
    if split:
        out_specs = out_specs + [fixed_spec((depth, width)) for width in widths]
        out_shape = out_shape + [jax.ShapeDtypeStruct((depth, width), bf16) for width in widths]
        scratch = [pltpu.SemaphoreType.DMA((2, 8))]
        if primary:
            out_specs.append(pl.BlockSpec((depth, seq_len), lambda step, *_: (0, step)))
            out_shape.append(jax.ShapeDtypeStruct((depth, rows), bf16))
    return pl.pallas_call(
        functools.partial(
            forward_kernel, inner=inner, state=state, kernel=kernel, split=split, primary=primary
        ),
        grid_spec=pltpu.PrefetchScalarGridSpec(
            num_scalar_prefetch=len(prefix),
            grid=(rows // seq_len,),
            in_specs=specs,
            out_specs=out_specs,
            scratch_shapes=scratch,
        ),
        out_shape=out_shape,
        compiler_params=call_params(),
        name="kf1" if primary else "kf2",
    )(*prefix, *ins)


def run_gate(place, cot, weights, gated, taps, seq_len, kernel):
    rows, inner = gated[0].shape
    slots, width = rows // seq_len, cot[0].shape[1]
    blocks = len(gated)
    split = isinstance(weights[0], (list, tuple))
    prefix, ins, scratch = [], [*cot], []
    if split:
        prefix = [place]
        specs = [whole(part) for part in cot]
        for group in weights:
            ins.extend(group)
            specs.extend([any_spec()] * 8)
        scratch = [pltpu.SemaphoreType.DMA((blocks, 8))]
    else:
        ins.extend(weights)
        specs = [rows_spec(seq_len, width)] + [whole(array) for array in weights]
    ins.extend(gated)
    specs.extend([rows_spec(seq_len, inner)] * blocks)
    ins.extend(taps)
    specs.extend([whole(table) for table in taps])
    return pl.pallas_call(
        functools.partial(gate_kernel, kernel=kernel, split=split, blocks=blocks),
        grid_spec=pltpu.PrefetchScalarGridSpec(
            num_scalar_prefetch=len(prefix),
            grid=(slots,),
            in_specs=specs,
            out_specs=[rows_spec(seq_len, inner)] * blocks
            + [
                rows_spec(sub, seq_len),
                pl.BlockSpec((blocks * inner, seq_len), lambda step, *_: (0, step)),
            ]
            + [rows_spec(seq_len, inner)] * blocks
            + [fixed_spec((inner, width))] * (blocks if split else 0),
            scratch_shapes=scratch,
        ),
        out_shape=[jax.ShapeDtypeStruct((rows, inner), f32)] * blocks
        + [
            jax.ShapeDtypeStruct((slots * sub, seq_len), f32),
            jax.ShapeDtypeStruct((blocks * inner, rows), bf16),
        ]
        + [jax.ShapeDtypeStruct((rows, inner), bf16)] * blocks
        + [jax.ShapeDtypeStruct((inner, width), bf16)] * (blocks if split else 0),
        compiler_params=call_params(),
        name="kgt",
    )(*prefix, *ins)


def run_backward(stats, turned, proj, bc_from, joined, plain, grad, tables, seq_len, state, kernel, inner_all):
    taps, cbc = tables
    rows, inner = plain.shape
    slots = rows // seq_len
    primary = bc_from is None
    ins = [*stats, *proj]
    specs = [stat_spec(seq_len, slots, back if turned else 0) for back in range(len(stats))]
    specs = specs + [rows_spec(seq_len, array.shape[1]) for array in proj]
    if not primary:
        ins.append(bc_from)
        specs.append(rows_spec(seq_len, 2 * state, inner // (2 * state)))
    if joined is not None:
        ins.append(joined)
        specs.append(rows_spec(seq_len, 2 * state))
    ins.extend([plain, grad])
    specs.extend([rows_spec(seq_len, inner)] * 2)
    for table in tables:
        ins.append(table)
        specs.append(whole(table))
    bc_shape = cbc.shape if primary else (rows, 2 * state)
    return pl.pallas_call(
        functools.partial(
            backward_kernel,
            inner=inner,
            state=state,
            kernel=kernel,
            inner_all=inner_all,
            stat_parts=len(stats),
            primary=primary,
            joined=joined is not None,
        ),
        grid=(slots,),
        in_specs=specs,
        out_specs=[
            rows_spec(seq_len, proj[0].shape[1]),
            rows_spec(seq_len, proj[1].shape[1]),
            fixed_spec(taps.shape),
            fixed_spec(cbc.shape) if primary else rows_spec(seq_len, 2 * state),
        ],
        out_shape=[
            jax.ShapeDtypeStruct((rows, proj[0].shape[1]), bf16),
            jax.ShapeDtypeStruct((rows, proj[1].shape[1]), bf16),
            jax.ShapeDtypeStruct(taps.shape, f32),
            jax.ShapeDtypeStruct(bc_shape, f32),
        ],
        scratch_shapes=[pltpu.VMEM((seq_len, seq_len), f32)],
        compiler_params=call_params(),
        name="kb1" if primary else "kb2",
    )(*ins)


def run_product(place, turned, grads, order, stats=(), part=0, parts=1, inner_all=1):
    tokens = turned.shape[1]
    depth = turned.shape[0] // parts
    cols = grads[0].shape[1]
    tile = 512 if cols % 512 == 0 else cols
    rows = depth // 8
    block = pl.BlockSpec((4, rows, tile), lambda step, *_: (0, 0, step))
    scratch = [pltpu.VMEM((depth, tile), bf16)]
    if stats:
        scratch.append(pltpu.VMEM((depth, tokens), bf16))
    return pl.pallas_call(
        functools.partial(
            product_kernel, order=order, scaled=bool(stats), inner_all=inner_all
        ),
        grid_spec=pltpu.PrefetchScalarGridSpec(
            num_scalar_prefetch=1,
            grid=(cols // tile,),
            in_specs=[
                pl.BlockSpec(
                    (depth, tokens), lambda step, *_: (part, 0), pipeline_mode=pl.Buffered(1)
                )
            ]
            + [whole(array) for array in stats]
            + [pl.BlockSpec((grad.shape[0], tile), lambda step, *_: (0, step)) for grad in grads],
            out_specs=[block, block],
            scratch_shapes=scratch,
        ),
        out_shape=[jax.ShapeDtypeStruct((4, rows, cols), bf16)] * 2,
        compiler_params=call_params(),
    )(place, turned, *stats, *grads)


def adam_parts(parameter, first, root, gradient, learn_rate, decay_coef):
    first_mom = beta_one * first + (1.0 - beta_one) * gradient
    second_mom = beta_two * root * root + (1.0 - beta_two) * gradient * gradient
    second_root = jnp.sqrt(second_mom)
    first_hat = first_mom / (1.0 - beta_one**step_count)
    second_hat = second_mom / (1.0 - beta_two**step_count)
    updated = parameter - learn_rate * (
        first_hat / (jnp.sqrt(second_hat) + adam_eps) + decay_coef * parameter
    )
    return updated, first_mom, second_root


def adam_update(parameter, moments, gradient, learn_rate, decay_coef):
    updated, first_mom, second_root = adam_parts(
        parameter, moments[0], moments[1], gradient, learn_rate, decay_coef
    )
    return (updated, jnp.stack([first_mom, second_root]))


def adam_kernel(*refs, inner, count):
    terms_a, terms_b = refs[:count], refs[count : 2 * count]
    home_a, home_b, zx_ref, zx_mom_ref, dt_ref, dt_mom_ref = refs[2 * count : 2 * count + 6]
    zx_out, zx_mom_out, dt_out, dt_mom_out = refs[2 * count + 6 :]

    def total(terms, home, start, stop):
        value = home[:, start:stop].astype(f32)
        for term in terms:
            value = value + term[..., start:stop].reshape(value.shape).astype(f32)
        return value

    for plane, (terms, home) in enumerate(((terms_a, home_a), (terms_b, home_b))):
        zx_out[:, plane, :], zx_mom_out[0, :, plane, :], zx_mom_out[1, :, plane, :] = adam_parts(
            zx_ref[:, plane, :],
            zx_mom_ref[0, :, plane, :],
            zx_mom_ref[1, :, plane, :],
            total(terms, home, 0, inner),
            rate_matrix,
            weight_decay,
        )
    grad = total(terms_b, home_b, inner, inner + lanes)[:, : dt_ref.shape[1]]
    dt_out[...], dt_mom_out[0], dt_mom_out[1] = adam_parts(
        dt_ref[...], dt_mom_ref[0], dt_mom_ref[1], grad, rate_matrix, weight_decay
    )


def run_adam(terms_a, terms_b, home_a, home_b, arrays, inner):
    rows = home_a.shape[0]
    tile = rows // 4

    def piece(array):
        width = array.shape[-1]
        if array.ndim == 3:
            return pl.BlockSpec((1, tile, width), lambda step: (0, step, 0))
        return pl.BlockSpec((tile, width), lambda step: (step, 0))

    def tiled(array, axis):
        shape = tuple(tile if at == axis else size for at, size in enumerate(array.shape))
        return pl.BlockSpec(
            shape, lambda step: tuple(step if at == axis else 0 for at in range(array.ndim))
        )

    state = [tiled(array, at % 2) for at, array in enumerate(arrays)]
    ins = [*terms_a, *terms_b, home_a, home_b]
    return pl.pallas_call(
        functools.partial(adam_kernel, inner=inner, count=len(terms_a)),
        grid=(4,),
        in_specs=[piece(array) for array in ins] + state,
        out_specs=state,
        out_shape=[jax.ShapeDtypeStruct(array.shape, f32) for array in arrays],
        compiler_params=call_params(),
        name="kad",
    )(*ins, *arrays)


def swap_by(values, axis, count, mask):
    return lax.ppermute(values, axis, [(i, i ^ mask) for i in range(count)])


def after(values, *earlier):
    return lax.optimization_barrier((values, *earlier))[0]


def pad_to(values, rows, cols):
    return jnp.pad(values, ((0, rows - values.shape[0]), (0, cols - values.shape[1])))


def gather_near(piece, way):
    other = 6 - way
    near = swap_by(piece, DP, 8, way)
    side = swap_by(piece, DP, 8, other)
    return near, side


def gather_rest(piece, near, side, way):
    far = swap_by(near, DP, 8, 6 - way)
    mine = [piece, near, side, far] if way == 2 else [piece, side, near, far]
    return mine + [swap_by(values, DP, 8, 1) for values in mine]


def order_of(way):
    return (0, 6 - way, way, 6)


def wide_sum(*parts):
    total = parts[0].astype(f32)
    for part in parts[1:]:
        total = total + part.astype(f32)
    return total


def scatter_first(keep, send):
    got = swap_by(send, DP, 8, 1)
    return wide_sum(keep[2:], got[2:]).astype(bf16), (keep, got)


def scatter_second(away, terms, way):
    terms = (*terms, swap_by(away, DP, 8, way))
    away = wide_sum(*[term[1] for term in terms]).astype(bf16)
    return away, terms


def scatter_last(away, terms, way):
    return (*terms, swap_by(away, DP, 8, 6 - way))


def scatter_third(away, terms, way):
    terms = scatter_last(away, terms, way)
    return wide_sum(*[term[0] for term in terms[:-1]], terms[-1])


def branch_kernel(*refs):
    count = (len(refs) - 2) // 2
    own_ref, peer_ref = refs[-2:]
    total = dot(refs[0][...], refs[count][...])
    for at in range(1, count):
        total = total + dot(refs[at][...], refs[count + at][...])
    half = own_ref.shape[0]
    own_ref[...] = total[:half]
    peer_ref[...] = total[half:].astype(bf16)


def cotangent_kernel(*refs):
    count = (len(refs) - 5) // 2
    mine_ref, other_ref, own_ref, peer_ref, gain_ref = refs[-5:]
    total = dot(refs[0][...], refs[count][...], (1, 1))
    for at in range(1, count):
        total = total + dot(refs[at][...], refs[count + at][...], (1, 1))
    half = own_ref.shape[0]
    own_ref[...] = total[:half]
    peer_ref[...] = total[half:].astype(bf16)
    gain = jnp.sum(
        total[:half] * mine_ref[...].astype(f32) + total[half:] * other_ref[...].astype(f32),
        axis=0,
        keepdims=True,
    )
    gain_ref[...] = jnp.broadcast_to(gain, gain_ref.shape)


def run_sum(kernel, left, right, turned, normed=()):
    rows, width = left[0].shape[0], right[0].shape[0] if turned else right[0].shape[1]
    tile = 512
    half = rows // 2
    columns = pl.BlockSpec((half, tile), lambda step: (0, step))
    specs = [whole(array) for array in left]
    for array in right:
        if turned:
            specs.append(pl.BlockSpec((tile, array.shape[1]), lambda step: (step, 0)))
        else:
            specs.append(pl.BlockSpec((array.shape[0], tile), lambda step: (0, step)))
    shapes = [jax.ShapeDtypeStruct((half, width), f32), jax.ShapeDtypeStruct((half, width), bf16)]
    outs = [columns, columns]
    if normed:
        specs = specs + [columns, columns]
        shapes.append(jax.ShapeDtypeStruct((sub, width), f32))
        outs.append(pl.BlockSpec((sub, tile), lambda step: (0, step)))
    return pl.pallas_call(
        kernel,
        grid=(width // tile,),
        in_specs=specs,
        out_specs=outs,
        out_shape=shapes,
        compiler_params=call_params(),
    )(*left, *right, *normed)


def sum_over(values, axis, count):
    if count & (count - 1):
        return lax.psum(values, axis)
    mask = 1
    while mask < count:
        values = values + swap_by(values, axis, count, mask)
        mask = mask * 2
    return values


def shards(
    block_input,
    seq_lengths,
    cotangent,
    norm_gain,
    proj_zx,
    proj_dt,
    proj_bc,
    chan_params,
    conv_bc,
    head_params,
    out_proj,
    gain_moments,
    zx_moments,
    dt_moments,
    bc_moments,
    chan_moments,
    convbc_moments,
    head_moments,
    out_moments,
):
    heads_axis = lax.axis_size(HEAD)
    dp_axis = lax.axis_size(DP)
    slot_count = seq_lengths.shape[0]
    rows_own, model_width = block_input.shape
    rows_dev = rows_own * heads_axis
    seq_len = rows_dev // slot_count
    rows_dp = proj_zx.shape[0]
    inner = chan_params.shape[1]
    inner_all = inner * heads_axis
    heads_loc = head_params.shape[1]
    headdim = inner // heads_loc
    kernel = chan_params.shape[0] - 2
    state = conv_bc.shape[1] // 2
    spot = lax.axis_index(HEAD)
    place = lax.axis_index(DP).astype(jnp.int32).reshape(1)
    paired = heads_axis == 4 and dp_axis == 8 and rows_own == seq_len

    zx_low = proj_zx.astype(bf16)
    piece_a = jnp.concatenate([zx_low[:, 0], proj_bc.astype(bf16)], axis=1)
    piece_b = jnp.concatenate([zx_low[:, 1], pad_to(proj_dt.astype(bf16), rows_dp, lanes)], axis=1)
    out_low = out_proj.astype(bf16)
    taps = pad_to(
        jnp.concatenate([chan_params, jnp.repeat(head_params[2:3], headdim, axis=1)], axis=0),
        sub,
        inner,
    )
    cbc = pad_to(conv_bc, sub, 2 * state)
    table = jnp.concatenate([taps, pad_to(head_params, sub, lanes)], axis=1)

    positions = iota((slot_count, seq_len), 1)
    live_mask = (positions < seq_lengths[:, None]).astype(f32).reshape(rows_dev, 1)
    live_own = lax.dynamic_slice_in_dim(live_mask, spot * rows_own, rows_own, 0)
    gain_float = lax.optimization_barrier(norm_gain.astype(bf16)).astype(f32)
    input_float = block_input.astype(f32)
    inv_own = lax.rsqrt(jnp.mean(input_float * input_float, axis=-1, keepdims=True) + norm_eps)
    own_hat = input_float * inv_own
    normed_own = (own_hat * gain_float[None, :]).astype(bf16)
    cot_float = cotangent.astype(f32)
    cot_own = (cot_float * live_own).astype(bf16)
    tables = (table, cbc)

    if paired:
        more_a = swap_by(zx_low[:, 0], HEAD, 4, 2)
        more_b = swap_by(piece_b, HEAD, 4, 2)
        near_a = gather_near(piece_a, 2)
        near_b = gather_near(piece_b, 4)
        normed_all = (normed_own, swap_by(normed_own, HEAD, 4, 1))
        out_more_low = swap_by(out_low, HEAD, 4, 2)
        tables_more = (swap_by(table, HEAD, 4, 2), cbc)
        own_pieces = (gather_rest(piece_a, *near_a, 2), gather_rest(piece_b, *near_b, 4))
        more_a, more_b = after((more_a, more_b), *near_a, *near_b)
        near_a = gather_near(more_a, 2)
        near_b = gather_near(more_b, 4)
        more_pieces = (gather_rest(more_a, *near_a, 2), gather_rest(more_b, *near_b, 4))
        out_low, out_more_low = after((out_low, out_more_low), *near_a, *near_b)
        near_a = gather_near(out_low, 2)
        near_b = gather_near(out_more_low, 4)
        out_pieces = (gather_rest(out_low, *near_a, 2), gather_rest(out_more_low, *near_b, 4))
        cot_all = (cot_own, swap_by(cot_own, HEAD, 4, 1))
        proj_a, proj_b, plain, gated, own_a, own_b, turned = run_forward(
            place, normed_all, own_pieces, None, tables, seq_len, state, kernel
        )
        more_proj_a, more_proj_b, more_plain, more_gated, more_a, more_b = run_forward(
            place, normed_all, more_pieces, proj_a, tables_more, seq_len, state, kernel
        )
        grad, more_grad, stats, lifted_turned, lifted, more_lifted, out_a, out_b = run_gate(
            place, cot_all, out_pieces, (gated, more_gated), (table, tables_more[0]), seq_len, kernel
        )
        stat_parts = [stats, swap_by(stats, HEAD, 4, 1)]
        out_own = run_product(
            place, lifted_turned, cot_all, order_of(2), stat_parts, 0, 2, inner_all
        )
        out_more = run_product(
            place, lifted_turned, cot_all, order_of(4), stat_parts, 1, 2, inner_all
        )
        lifted, more_lifted = after((lifted, more_lifted), out_own[0], out_more[0])
        branch_own, branch_peer = run_sum(
            branch_kernel, (lifted, more_lifted), (out_a, out_b), False
        )
        branch_own = branch_own + swap_by(branch_peer, HEAD, 4, 1).astype(f32)
        square_own = stats[:1] + stat_parts[1][sub : sub + 1]
        gate_own = lax.rsqrt(square_own / inner_all + norm_eps).reshape(seq_len, 1)
        out_own = scatter_first(*out_own)
        out_more = scatter_first(*out_more)
        more_grad = after(more_grad, branch_peer, out_own[0], out_more[0])
        more_cot_a, more_cot_b, more_sums, bc_part = run_backward(
            stat_parts,
            True,
            (more_proj_a, more_proj_b),
            proj_a,
            None,
            more_plain,
            more_grad,
            tables_more,
            seq_len,
            state,
            kernel,
            inner_all,
        )
        grad_more_a = run_product(place, turned, (more_cot_a,), order_of(2))
        grad_more_b = run_product(place, turned, (more_cot_b,), order_of(4))
        out_own = scatter_second(*out_own, 2)
        out_more = scatter_second(*out_more, 4)
        grad = after(grad, grad_more_a[0], grad_more_b[0], out_own[0], out_more[0])
        cot_a, cot_b, own_sums, cbc_sums = run_backward(
            stat_parts,
            True,
            (proj_a, proj_b),
            None,
            bc_part,
            plain,
            grad,
            tables,
            seq_len,
            state,
            kernel,
            inner_all,
        )
        grad_more_a = scatter_first(*grad_more_a)
        grad_more_b = scatter_first(*grad_more_b)
        out_away = scatter_third(*out_more, 4).astype(bf16)
        cot_a, cot_b = after((cot_a, cot_b), out_away, grad_more_a[0], grad_more_b[0])
        grad_own_a = run_product(place, turned, (cot_a,), order_of(2))
        grad_own_b = run_product(place, turned, (cot_b,), order_of(4))
        grad_more_a = scatter_second(*grad_more_a, 2)
        grad_more_b = scatter_second(*grad_more_b, 4)
        grad_own_a = scatter_first(*grad_own_a)
        grad_own_b = scatter_first(*grad_own_b)
        cot_a, cot_b, more_cot_a, more_cot_b = after(
            (cot_a, cot_b, more_cot_a, more_cot_b),
            grad_more_a[0],
            grad_more_b[0],
            grad_own_a[0],
            grad_own_b[0],
        )
        grad_out = scatter_third(*out_own, 2) + swap_by(out_away, HEAD, 4, 2).astype(f32)
        cot_whole, cot_peer, grad_gain = run_sum(
            cotangent_kernel,
            (more_cot_a, more_cot_b, cot_a, cot_b),
            (more_a, more_b, own_a, own_b),
            True,
            normed_all,
        )
        cot_whole = cot_whole + swap_by(cot_peer, HEAD, 4, 1).astype(f32)
        away_a = scatter_third(*grad_more_a, 2).astype(bf16)
        away_b = scatter_third(*grad_more_b, 4).astype(bf16)
        home_a = swap_by(away_a, HEAD, 4, 2)
        home_b = swap_by(away_b, HEAD, 4, 2)
        grad_own_a = scatter_second(*grad_own_a, 2)
        grad_own_b = scatter_second(*grad_own_b, 4)
        terms_a = scatter_last(*grad_own_a, 2)
        terms_b = scatter_last(*grad_own_b, 4)
        zx_next, zx_state, dt_next, dt_state = run_adam(
            terms_a, terms_b, home_a, home_b, (proj_zx, zx_moments, proj_dt, dt_moments), inner
        )
        grad_bc = wide_sum(*[term[0, :, inner:] for term in terms_a[:-1]], terms_a[-1][:, inner:])
        bc_low = grad_bc.astype(bf16)
        for mask in (1, 2, 3):
            grad_bc = grad_bc + swap_by(bc_low, HEAD, 4, mask).astype(f32)
        wide = inner + lanes
        small = jnp.concatenate([more_sums, own_sums, cbc_sums, grad_gain], axis=1)
        small = small + swap_by(small, DP, 8, 1)
        small = small + sum(swap_by(small, DP, 8, mask) for mask in (2, 4, 6))
        both = small[:, 2 * wide :]
        both = both + sum(swap_by(both, HEAD, 4, mask) for mask in (1, 2, 3))
        own_sums = small[:, wide : 2 * wide] + swap_by(small[:, :wide], HEAD, 4, 2)
        cbc_sums, grad_gain = both[:, : 2 * state], both[0, 2 * state :]
    else:
        normed_all = lax.all_gather(normed_own, HEAD, axis=0, tiled=True)
        cot_all = lax.all_gather(cot_own, HEAD, axis=0, tiled=True)
        own_a = lax.all_gather(piece_a, DP, axis=0, tiled=True)
        own_b = lax.all_gather(piece_b, DP, axis=0, tiled=True)
        out_full = lax.all_gather(out_low, DP, axis=0, tiled=True)
        proj_a, proj_b, plain, gated = run_forward(
            None, (normed_all,), (own_a, own_b), None, tables, seq_len, state, kernel
        )
        grad, stats, _, lifted = run_gate(
            None, (cot_all,), (out_full,), (gated,), (table,), seq_len, kernel
        )
        branch = dot(lifted, out_full)
        stats = lax.psum(stats, HEAD)
        square = stats.reshape(slot_count, sub, seq_len)[:, 0].reshape(rows_dev, 1)
        gate_all = lax.rsqrt(square / inner_all + norm_eps)
        gate_own = lax.dynamic_slice_in_dim(gate_all, spot * rows_own, rows_own, 0)
        cot_gate = (cot_all.astype(f32) * gate_all).astype(bf16)
        cot_a, cot_b, own_sums, cbc_sums = run_backward(
            [stats],
            False,
            (proj_a, proj_b),
            None,
            None,
            plain,
            grad,
            tables,
            seq_len,
            state,
            kernel,
            inner_all,
        )
        cot_input = dot(cot_a, own_a, (1, 1)) + dot(cot_b, own_b, (1, 1))
        grad_gain = jnp.sum(cot_input * normed_all.astype(f32), axis=0)

        def scatter(values, axis):
            return lax.psum_scatter(
                values.astype(bf16), axis, scatter_dimension=0, tiled=True
            ).astype(f32)

        cot_whole = scatter(cot_input, HEAD)
        branch_own = scatter(branch, HEAD)
        grad_out = scatter(dot(lifted, cot_gate, (0, 0)), DP)
        sum_a = scatter(dot(normed_all, cot_a, (0, 0)), DP)
        sum_b = scatter(dot(normed_all, cot_b, (0, 0)), DP)
        grad_zx = jnp.stack([sum_a[:, :inner], sum_b[:, :inner]], axis=1)
        grad_dt = sum_b[:, inner:][:, :heads_loc]
        zx_next, zx_state = adam_update(proj_zx, zx_moments, grad_zx, rate_matrix, weight_decay)
        dt_next, dt_state = adam_update(proj_dt, dt_moments, grad_dt, rate_matrix, weight_decay)
        grad_bc = lax.psum(sum_a[:, inner:].astype(bf16), HEAD).astype(f32)
        own_sums = sum_over(own_sums, DP, dp_axis)
        cbc_sums = sum_over(sum_over(cbc_sums, DP, dp_axis), HEAD, heads_axis)
        grad_gain = sum_over(sum_over(grad_gain, DP, dp_axis), HEAD, heads_axis)

    block_output = (input_float + live_own * (branch_own * gate_own)).astype(bf16)
    lift_own = cot_whole * gain_float[None, :]
    row_dot = jnp.sum(lift_own * own_hat, axis=-1, keepdims=True)
    input_grad = cot_float + inv_own * (lift_own - own_hat * row_dot / model_width)

    grad_convbc = cbc_sums[: kernel + 1]
    grad_gain = grad_gain / gain_float
    grad_chan = own_sums[: kernel + 2, :inner]
    grad_skip = jnp.sum(own_sums[kernel + 2, :inner].reshape(heads_loc, headdim), axis=1)
    grad_head = jnp.concatenate(
        [own_sums[:2, inner : inner + heads_loc], grad_skip[None, :]], axis=0
    )

    gain_next, gain_state = adam_update(norm_gain, gain_moments, grad_gain, rate_vector, 0.0)
    bc_next, bc_state = adam_update(proj_bc, bc_moments, grad_bc, rate_matrix, weight_decay)
    chan_next, chan_state = adam_update(chan_params, chan_moments, grad_chan, rate_vector, 0.0)
    convbc_next, convbc_state = adam_update(conv_bc, convbc_moments, grad_convbc, rate_vector, 0.0)
    head_next, head_state = adam_update(head_params, head_moments, grad_head, rate_vector, 0.0)
    outproj_next, outproj_state = adam_update(
        out_proj, out_moments, grad_out, rate_matrix, weight_decay
    )
    return (
        block_output,
        input_grad,
        gain_next,
        gain_state,
        zx_next,
        zx_state,
        dt_next,
        dt_state,
        bc_next,
        bc_state,
        chan_next,
        chan_state,
        convbc_next,
        convbc_state,
        head_next,
        head_state,
        outproj_next,
        outproj_state,
    )


def solution(mesh):
    placed = (
        P((DP, HEAD), None),
        P(DP),
        P((DP, HEAD), None),
        P(),
        P(DP, None, HEAD),
        P(DP, HEAD),
        P(DP, None),
        P(None, HEAD),
        P(),
        P(None, HEAD),
        P((HEAD, DP), None),
        P(),
        P(None, DP, None, HEAD),
        P(None, DP, HEAD),
        P(None, DP, None),
        P(None, None, HEAD),
        P(),
        P(None, None, HEAD),
        P(None, (HEAD, DP), None),
    )
    return jax.shard_map(
        shards,
        mesh=mesh,
        in_specs=placed,
        out_specs=(
            P((DP, HEAD), None),
            P((DP, HEAD), None),
            P(),
            P(),
            P(DP, None, HEAD),
            P(None, DP, None, HEAD),
            P(DP, HEAD),
            P(None, DP, HEAD),
            P(DP, None),
            P(None, DP, None),
            P(None, HEAD),
            P(None, None, HEAD),
            P(),
            P(),
            P(None, HEAD),
            P(None, None, HEAD),
            P((HEAD, DP), None),
            P(None, (HEAD, DP), None),
        ),
        check_vma=False,
    )
```

time: 429 us -> 406 us (0.946)
  waiting for transfers between devices: 160 us -> 142 us
  Pallas kernels: 110 us -> 122 us
  local copies, waits for them, and re-layouts: 31.5 us -> 21.5 us
  matrix products: 9.35 us -> 0 us
  other arithmetic: 37.2 us -> 44.7 us
    ppermute x78 -> x83, waiting for transfers between devices: 160 us -> 142 us  [swap_by(): return lax.ppermute(values, axis, [(i, i ^ mask) for i in range(count)])]
    pallas_call x6 -> x9, Pallas kernels: 39.6 us -> 55.2 us  [the longest x6 29.9 us: run_product(): pl.pallas_call(functools.partial(product_kernel, order=order, scaled=bool...]
    convert_element_type x10 -> x17, other arithmetic: 7.35 us -> 21 us  [the longest x6 8.21 us: scatter_second(): away = wide_sum(*[term[1] for term in terms]).astype(bf16)]
    dot_general x4 -> x0, matrix products: 9.35 us -> none  [dot(): lax.dot_general(lhs, rhs, (((over[0],), (over[1],)), ((), ())), preferred...]
    slice x19 -> x4, local copies, waits for them, and re-layouts: 8.71 us -> 1.25 us  [the longest x1 0.63 us: shards(): both = small[:, 2 * wide:]]
    pallas_call x1, Pallas kernels: 15.2 us -> 10.6 us  [run_gate(): pl.pallas_call(functools.partial(gate_kernel, kernel=kernel, split=split,...]
    ppermute x78 -> x83, starting transfers between devices: 71.5 us -> 68 us  [swap_by(): return lax.ppermute(values, axis, [(i, i ^ mask) for i in range(count)])]
    unnamed x231 -> x190, local copies, waits for them, and re-layouts: 17.8 us -> 14.8 us
  transfers between devices with their start and end apart: 78 -> 83, of which waited for: 28 -> 24; matrix products, arithmetic and copies ran while one was open for 14% -> 14% of each run, Pallas kernels for 22% -> 27%
where the time goes in v3:
time: 406 us; the launch traced here: 401 us
  waiting for transfers between devices  142 us (35%)
  Pallas kernels  122 us (30%)
  starting transfers between devices  68 us (17%)
  other arithmetic  44.7 us (11%)
  local copies, waits for them, and re-layouts  21.5 us (5%)
    ppermute x83, waiting for transfers between devices, swap_by(): return lax.ppermute(values, axis, [(i, i ^ mask) for i in range(count)])  142 us
    ppermute x83, starting transfers between devices, swap_by(): return lax.ppermute(values, axis, [(i, i ^ mask) for i in range(count)])  68 us
    pallas_call x6, Pallas kernels, run_product(): pl.pallas_call(functools.partial(product_kernel, order=order, scaled=bool...  29.9 us
    pallas_call x2, Pallas kernels, run_backward(): pl.pallas_call(functools.partial(backward_kernel, inner=inner, state=stat...  29.2 us
    pallas_call x2, Pallas kernels, run_forward(): pl.pallas_call(functools.partial(forward_kernel, inner=inner, state=state...  27.4 us
    pallas_call x2, Pallas kernels, run_sum(): pl.pallas_call(kernel, grid=(width // tile,), in_specs=specs, out_specs=o...  18.3 us
    unnamed x190, local copies, waits for them, and re-layouts  14.8 us
    pallas_call x1, Pallas kernels, run_gate(): pl.pallas_call(functools.partial(gate_kernel, kernel=kernel, split=split,...  10.6 us
  transfers between devices with their start and end apart: 83, of which 24 were waited for; matrix products, arithmetic and copies ran while one was open for 14% of the time, Pallas kernels for 27%

profile of v3, /device:TPU:0, one launch (start us, length us, event | category | flops | bytes accessed | tf_op | source)
XLA Modules:
  0.0 400.5 jit_solution(13842548528961116653)
XLA Ops:
  12.9 23.1 %collective-permute-done.47.refs_20_.refs_22_.refs_7_ = f32[8,896]{1,0:T(8,128)S(1)} collective-permute-done((f32[8,896]{1,0:T(8,128)S(1)}, f32[8,896]{1,0:T(8,128)S(1)}, u32[]{:S(2)}, u32[]{:S(2)}) %collective-permute-start.47) | collective-permute-done | bytes 28704 | tf_op jit(solution)/shard_map/ppermute | solution.py:705
  37.4 7.9 %collective-permute-done.6.refs_13_ = bf16[192,896]{1,0:T(8,128)(2,1)} collective-permute-done((bf16[192,896]{1,0:T(8,128)(2,1)S(1)}, bf16[192,896]{1,0:T(8,128)(2,1)}, u32[]{:S(2)}, u32[]{:S(2)}) %collective-permute-start.6) | collective-permute-done | bytes 344096 | tf_op jit(solution)/shard_map/ppermute | solution.py:705
  45.8 8.0 %collective-permute-done.3.refs_11_ = bf16[192,896]{1,0:T(8,128)(2,1)S(1)} collective-permute-done((bf16[192,896]{1,0:T(8,128)(2,1)S(1)}, bf16[192,896]{1,0:T(8,128)(2,1)S(1)}, u32[]{:S(2)}, u32[]{:S(2)}) %collective-permute-start.3) | collective-permute-done | bytes 344096 | tf_op jit(solution)/shard_map/ppermute | solution.py:705
  58.6 6.4 %collective-permute-done.32.refs_14_ = bf16[192,896]{1,0:T(8,128)(2,1)} collective-permute-done((bf16[192,896]{1,0:T(8,128)(2,1)}, bf16[192,896]{1,0:T(8,128)(2,1)}, u32[]{:S(2)}, u32[]{:S(2)}) %collective-permute-start.32) | collective-permute-done | bytes 344096 | tf_op jit(solution)/shard_map/ppermute | solution.py:705
  68.2 3.2 collective-permute-done.8.refs_4_
  76.4 6.6 %collective-permute-done.26.refs_2_.refs_9_ = bf16[256,1536]{1,0:T(8,128)(2,1)S(1)} collective-permute-done((bf16[256,1536]{1,0:T(8,128)(2,1)S(1)}, bf16[256,1536]{1,0:T(8,128)(2,1)S(1)}, u32[]{:S(2)}, u32[]{:S(2)}) %collective-permute-start.26) | collective-permute-done | bytes 786464 | tf_op jit(solution)/shard_map/ppermute | solution.py:705
  86.4 9.8 %collective-permute-done.refs_2_.refs_5_ = bf16[256,1536]{1,0:T(8,128)(2,1)S(1)} collective-permute-done((bf16[256,1536]{1,0:T(8,128)(2,1)S(1)}, bf16[256,1536]{1,0:T(8,128)(2,1)S(1)}, u32[]{:S(2)}, u32[]{:S(2)}) %collective-permute-start) | collective-permute-done | bytes 786464 | tf_op jit(solution)/shard_map/ppermute | solution.py:705
  101.2 5.2 %collective-permute-done.12.refs_4_ = bf16[96,1536]{1,0:T(8,128)(2,1)S(1)} collective-permute-done((bf16[96,1536]{1,0:T(8,128)(2,1)S(1)}, bf16[96,1536]{1,0:T(8,128)(2,1)S(1)}, u32[]{:S(2)}, u32[]{:S(2)}) %collective-permute-start.12) | collective-permute-done | bytes 294944 | tf_op jit(solution)/shard_map/ppermute | solution.py:705
  111.8 5.1 %collective-permute-done.42.refs_14_ = bf16[192,896]{1,0:T(8,128)(2,1)S(1)} collective-permute-done((bf16[192,896]{1,0:T(8,128)(2,1)S(1)}, bf16[192,896]{1,0:T(8,128)(2,1)S(1)}, u32[]{:S(2)}, u32[]{:S(2)}) %collective-permute-start.42) | collective-permute-done | bytes 344096 | tf_op jit(solution)/shard_map/ppermute | solution.py:705
  121.3 5.2 %collective-permute-done.14.refs_6_ = bf16[96,1536]{1,0:T(8,128)(2,1)} collective-permute-done((bf16[96,1536]{1,0:T(8,128)(2,1)S(1)}, bf16[96,1536]{1,0:T(8,128)(2,1)}, u32[]{:S(2)}, u32[]{:S(2)}) %collective-permute-start.14) | collective-permute-done | bytes 294944 | tf_op jit(solution)/shard_map/ppermute | solution.py:705
  129.9 14.3 %kf1.1 = (f32[512,1024]{1,0:T(8,128)}, f32[512,896]{1,0:T(8,128)}, f32[512,768]{1,0:T(8,128)}, f32[512,768]{1,0:T(8,128)}, bf16[1536,1024]{1,0:T(8,128)(2,1)}, /...) custom-call(s32[1]{0:T(128)} %bitcast.1.refs_0_, bf16[256,1536]{1,0:T(8,128)(2,1)} %copy-done, ...), custom_call_target="tpu_custom_call" | custom-call | tf_op jit(solution)/shard_map/kf1/pallas_call | solution.py:483
  144.2 13.2 %kf2.1 = (f32[512,768]{1,0:T(8,128)}, f32[512,896]{1,0:T(8,128)}, f32[512,768]{1,0:T(8,128)}, f32[512,768]{1,0:T(8,128)}, bf16[1536,768]{1,0:T(8,128)(2,1)}, /*index=5*/bf16[1536,896]{1,0:T(8,128)(2,1)}) custom-call(s32[1]{0:T(128)} %bitcast.1.refs_0_, bf16[256,1536]{1,0:T(8,128)(2,1)} %copy-done, bf16[256,1536]{1,0:T(8,128)(2,1)} %copy-done.3, ...), custom_call_target="tpu_custom_call" | custom-call | tf_op jit(solution)/shard_map/kf2/pallas_call | solution.py:483
  157.4 10.6 %kgt.1 = (f32[512,768]{1,0:T(8,128)}, f32[512,768]{1,0:T(8,128)}, f32[16,256]{1,0:T(8,128)}, bf16[1536,512]{1,0:T(8,128)(2,1)}, bf16[512,768]{1,0:T(8,128)(2,1)}...) custom-call(s32[1]{0:T(128)} %bitcast.1.refs_0_, bf16[256,1536]{1,0:T(8,128)(2,1)} %copy-done.2, ...), custom_call_target="tpu_custom_call" | custom-call | tf_op jit(solution)/shard_map/kgt/pallas_call | solution.py:520
  168.4 3.7 collective-permute-done.48.refs_3_.refs_1_
  172.7 4.9 %shard_map.323 = (bf16[4,96,1536]{2,1,0:T(8,128)(2,1)}, bf16[4,96,1536]{2,1,0:T(8,128)(2,1)}) custom-call(s32[1]{0:T(128)} %bitcast.1.refs_0_, bf16[1536,512]{1,0:T(8,128)(2,1)} %get-tuple-element.91.refs_1_, f32[16,256]{1,0:T(8,128)} %get-tuple-element.92.refs_2_.refs_0_, f32[16,256]{1,0:T(8,128)} %copy-done.66, bf16[256,1536]{1,0:T(8,128)(2,1)} %copy-done.2, ...), custom_call_target="tpu_custom_call" | custom-call | tf_op jit(solution)/shard_map/pallas_call | solution.py:608
  180.4 5.0 %shard_map.322 = (bf16[4,96,1536]{2,1,0:T(8,128)(2,1)}, bf16[4,96,1536]{2,1,0:T(8,128)(2,1)}) custom-call(s32[1]{0:T(128)} %bitcast.1.refs_0_, bf16[1536,512]{1,0:T(8,128)(2,1)} %get-tuple-element.91.refs_1_, f32[16,256]{1,0:T(8,128)} %get-tuple-element.92.refs_2_.refs_0_, f32[16,256]{1,0:T(8,128)} %copy-done.66, bf16[256,1536]{1,0:T(8,128)(2,1)} %copy-done.2, ...), custom_call_target="tpu_custom_call" | custom-call | tf_op jit(solution)/shard_map/pallas_call | solution.py:608
  187.2 6.4 %shard_map.324 = (f32[256,1536]{1,0:T(8,128)}, bf16[256,1536]{1,0:T(8,128)(2,1)}) custom-call(bf16[512,768]{1,0:T(8,128)(2,1)} %get-tuple-element.95.refs_0_, bf16[512,768]{1,0:T(8,128)(2,1)} %get-tuple-element.96.refs_1_, bf16[768,1536]{1,0:T(8,128)(2,1)} %get-tuple-element.97.refs_2_, bf16[768,1536]{1,0:T(8,128)(2,1)} %get-tuple-element.98.refs_3_), custom_call_target="tpu_custom_call" | custom-call | tf_op jit(solution)/shard_map/pallas_call | solution.py:805
  199.4 14.4 %kb2.1 = (bf16[512,768]{1,0:T(8,128)(2,1)}, bf16[512,896]{1,0:T(8,128)(2,1)}, f32[8,896]{1,0:T(8,128)}, f32[512,256]{1,0:T(8,128)}) custom-call(f32[16,256]{1,0:T(8,128)} %get-tuple-element.92.refs_2_.refs_0_, f32[16,256]{1,0:T(8,128)} %copy-done.66, f32[512,768]{1,0:T(8,128)} %get-tuple-element.102.refs_2_, f32[512,896]{1,0:T(8,128)} %get-tuple-element.103.refs_3_, ...), custom_call_target="tpu_custom_call" | custom-call | tf_op jit(solution)/shard_map/kb2/pallas_call | solution.py:567
  213.8 5.2 %shard_map.326 = (bf16[4,192,896]{2,1,0:T(8,128)(2,1)}, bf16[4,192,896]{2,1,0:T(8,128)(2,1)}) custom-call(s32[1]{0:T(128)} %bitcast.1.refs_0_, bf16[1536,512]{1,0:T(8,128)(2,1)} %get-tuple-element.112.refs_1_, bf16[512,896]{1,0:T(8,128)(2,1)} %get-tuple-element.129.refs_2_.refs_1_), custom_call_target="tpu_custom_call" | custom-call | tf_op jit(solution)/shard_map/pallas_call | solution.py:608
  219.0 4.5 %shard_map.325 = (bf16[4,192,768]{2,1,0:T(8,128)(2,1)}, bf16[4,192,768]{2,1,0:T(8,128)(2,1)}) custom-call(s32[1]{0:T(128)} %bitcast.1.refs_0_, bf16[1536,512]{1,0:T(8,128)(2,1)} %get-tuple-element.112.refs_1_, bf16[512,768]{1,0:T(8,128)(2,1)} %get-tuple-element.128.refs_2_.refs_0_), custom_call_target="tpu_custom_call" | custom-call | tf_op jit(solution)/shard_map/pallas_call | solution.py:608
  228.9 14.9 %kb1.1 = (bf16[512,1024]{1,0:T(8,128)(2,1)}, bf16[512,896]{1,0:T(8,128)(2,1)}, f32[8,896]{1,0:T(8,128)}, f32[8,256]{1,0:T(8,128)}) custom-call(f32[16,256]{1,0:T(8,128)} %get-tuple-element.92.refs_2_.refs_0_, f32[16,256]{1,0:T(8,128)} %copy-done.66, f32[512,1024]{1,0:T(8,128)} %get-tuple-element.87.refs_19_.refs_4_.refs_2_, ...), custom_call_target="tpu_custom_call" | custom-call | tf_op jit(solution)/shard_map/kb1/pallas_call | solution.py:567
  247.4 4.9 %collective-permute-start.82 = (bf16[96,1536]{1,0:T(8,128)(2,1)}, bf16[96,1536]{1,0:T(8,128)(2,1)}, u32[]{:S(2)}, u32[]{:S(2)}) collective-permute-start(bf16[96,1536]{1,0:T(8,128)(2,1)} %fusion.16), channel_id=1, source_target_pairs={{0,2},{1,3},{2,0},{3,1},{4,6},{5,7},{6,4},{7,5},{8,10},{9,11},{10,... | collective-permute-start | bytes 884744 | tf_op jit(solution)/shard_map/ppermute | solution.py:705
  255.1 5.4 %shard_map.328 = (bf16[4,192,896]{2,1,0:T(8,128)(2,1)}, bf16[4,192,896]{2,1,0:T(8,128)(2,1)}) custom-call(s32[1]{0:T(128)} %bitcast.1.refs_0_, bf16[1536,512]{1,0:T(8,128)(2,1)} %get-tuple-element.112.refs_1_, bf16[512,896]{1,0:T(8,128)(2,1)} %get-tuple-element.131.refs_2_.refs_3_), custom_call_target="tpu_custom_call" | custom-call | tf_op jit(solution)/shard_map/pallas_call | solution.py:608
  260.5 5.0 %shard_map.327 = (bf16[4,192,1024]{2,1,0:T(8,128)(2,1)}, bf16[4,192,1024]{2,1,0:T(8,128)(2,1)}) custom-call(s32[1]{0:T(128)} %bitcast.1.refs_0_, bf16[1536,512]{1,0:T(8,128)(2,1)} %get-tuple-element.112.refs_1_, bf16[512,1024]{1,0:T(8,128)(2,1)} %get-tuple-element.130.refs_2_), custom_call_target="tpu_custom_call" | custom-call | tf_op jit(solution)/shard_map/pallas_call | solution.py:608
  272.1 13.5 %collective-permute-done.58 = bf16[2,192,896]{2,1,0:T(8,128)(2,1)S(1)} collective-permute-done((bf16[2,192,896]{2,1,0:T(8,128)(2,1)S(1)}, bf16[2,192,896]{2,1,0:T(8,128)(2,1)S(1)}, u32[]{:S(2)}, u32[]{:S(2)}) %collective-permute-start.58) | collective-permute-done | bytes 688160 | tf_op jit(solution)/shard_map/ppermute | solution.py:705
  290.6 11.9 %shard_map.329 = (f32[256,1536]{1,0:T(8,128)}, bf16[256,1536]{1,0:T(8,128)(2,1)}, f32[8,1536]{1,0:T(8,128)}) custom-call(bf16[512,768]{1,0:T(8,128)(2,1)} %get-tuple-element.128.refs_2_.refs_0_, bf16[512,896]{1,0:T(8,128)(2,1)} %get-tuple-element.129.refs_2_.refs_1_, bf16[512,1024]{1,0:T(8,128)(2,1)} %get-tuple-element.130.refs_2_, ...), custom_call_target="tpu_custom_call" | custom-call | tf_op jit(solution)/shard_map/pallas_call | solution.py:805
  311.1 6.8 %collective-permute-done.63 = f32[8,3584]{1,0:T(8,128)S(1)} collective-permute-done((f32[8,3584]{1,0:T(8,128)S(1)}, f32[8,3584]{1,0:T(8,128)S(1)}, u32[]{:S(2)}, u32[]{:S(2)}) %collective-permute-start.63) | collective-permute-done | bytes 114720 | tf_op jit(solution)/shard_map/ppermute | solution.py:705
  326.3 9.6 %collective-permute-done.80 = f32[8,896]{1,0:T(8,128)S(1)} collective-permute-done((f32[8,896]{1,0:T(8,128)S(1)}, f32[8,896]{1,0:T(8,128)S(1)}, u32[]{:S(2)}, u32[]{:S(2)}) %collective-permute-start.80) | collective-permute-done | bytes 28704 | tf_op jit(solution)/shard_map/ppermute | solution.py:705
  352.4 12.7 %collective-permute-done.69.refs_2_ = bf16[2,192,1024]{2,1,0:T(8,128)(2,1)S(1)} collective-permute-done((bf16[2,192,1024]{2,1,0:T(8,128)(2,1)S(1)}, bf16[2,192,1024]{2,1,0:T(8,128)(2,1)S(1)}, u32[]{:S(2)}, u32[]{:S(2)}) %collective-permute-start.69) | collective-permute-done | bytes 786464 | tf_op jit(solution)/shard_map/ppermute | solution.py:705
  371.0 5.1 %collective-permute-done.70.refs_3_ = bf16[192,1024]{1,0:T(8,128)(2,1)S(1)} collective-permute-done((bf16[192,1024]{1,0:T(8,128)(2,1)S(1)}, bf16[192,1024]{1,0:T(8,128)(2,1)S(1)}, u32[]{:S(2)}, u32[]{:S(2)}) %collective-permute-start.70) | collective-permute-done | bytes 393248 | tf_op jit(solution)/shard_map/ppermute | solution.py:705
  382.3 3.3 convert_add_fusion.1
  387.1 7.0 %kad.1 = (f32[192,2,768]{2,1,0:T(2,128)}, f32[2,192,2,768]{3,2,1,0:T(2,128)}, f32[192,12]{1,0:T(8,128)}, f32[2,192,12]{2,1,0:T(8,128)}) custom-call(bf16[4,192,1024]{2,1,0:T(8,128)(2,1)} %get-tuple-element.124.refs_0_, bf16[4,192,1024]{2,1,0:T(8,128)(2,1)} %copy-done.7, bf16[2,192,1024]{2,1,0:T(8,128)(2,1)} %copy-done.12, bf16[192,1024]{1,0:T(8,128)(2,1)} %copy-done.28, ...), custom_call_target="tpu_custom_call" | custom-call | tf_op jit(solution)/shard_map/kad/pallas_call | solution.py:693
  (411 shorter events, 136.0 us)
Async XLA Ops:
  2.3 53.2 %collective-permute-start.4 = (bf16[192,1024]{1,0:T(8,128)(2,1)S(1)}, bf16[192,1024]{1,0:T(8,128)(2,1)S(1)}, u32[]{:S(2)}, u32[]{:S(2)}) collective-permute-start(bf16[192,1024]{1,0:T(8,128)(2,1)S(1)} %pad_maximum_fusion.1.refs_3_), channel_id=1, source_target_pairs={{0,8},{4,12},{8,0},{12,4},{16,24},{20,28},{24,16},{28,20},{1,9},{5... | collective-permute-start | bytes 1179656 | tf_op jit(solution)/shard_map/ppermute | solution.py:705
  5.3 50.1 %collective-permute-start.5 = (bf16[192,1024]{1,0:T(8,128)(2,1)S(1)}, bf16[192,1024]{1,0:T(8,128)(2,1)S(1)}, u32[]{:S(2)}, u32[]{:S(2)}) collective-permute-start(bf16[192,1024]{1,0:T(8,128)(2,1)S(1)} %pad_maximum_fusion.1.refs_3_), channel_id=1, source_target_pairs={{0,16},{4,20},{8,24},{12,28},{16,0},{20,4},{24,8},{28,12},{1,17},{... | collective-permute-start | bytes 1179656 | tf_op jit(solution)/shard_map/ppermute | solution.py:705
  6.8 29.8 %collective-permute-start.2 = (bf16[192,768]{1,0:T(8,128)(2,1)S(1)}, bf16[192,768]{1,0:T(8,128)(2,1)}, u32[]{:S(2)}, u32[]{:S(2)}) collective-permute-start(bf16[192,768]{1,0:T(8,128)(2,1)S(1)} %get-tuple-element.195), channel_id=1, source_target_pairs={{0,2},{1,3},{2,0},{3,1},{4,6},{5,7},{6,4},{7,5},{8,10},{9,11},{10,... | collective-permute-start | bytes 884744 | tf_op jit(solution)/shard_map/ppermute | solution.py:705
  9.4 27.6 %collective-permute-start.1 = (bf16[96,1536]{1,0:T(8,128)(2,1)S(1)}, bf16[96,1536]{1,0:T(8,128)(2,1)}, u32[]{:S(2)}, u32[]{:S(2)}) collective-permute-start(bf16[96,1536]{1,0:T(8,128)(2,1)S(1)} %convert_element_type.326.refs_3_), channel_id=1, source_target_pairs={{0,2},{1,3},{2,0},{3,1},{4,6},{5,7},{6,4},{7,5},{8,10},{9,11},{10,... | collective-permute-start | bytes 884744 | tf_op jit(solution)/shard_map/ppermute | solution.py:705
  10.1 26.0 %collective-permute-start.47 = (f32[8,896]{1,0:T(8,128)S(1)}, f32[8,896]{1,0:T(8,128)S(1)}, u32[]{:S(2)}, u32[]{:S(2)}) collective-permute-start(f32[8,896]{1,0:T(8,128)S(1)} %select_maximum_fusion.refs_19_.refs_21_.refs_7_), channel_id=1, source_target_pairs={{0,2},{1,3},{2,0},{3,1},{4,6},{5,7},{6,4},{7,5},{8,10},{9,11},{10,... | collective-permute-start | bytes 86024 | tf_op jit(solution)/shard_map/ppermute | solution.py:705
  65.1 17.9 %collective-permute-start.26 = (bf16[256,1536]{1,0:T(8,128)(2,1)S(1)}, bf16[256,1536]{1,0:T(8,128)(2,1)S(1)}, u32[]{:S(2)}, u32[]{:S(2)}) collective-permute-start(bf16[256,1536]{1,0:T(8,128)(2,1)S(1)} %fusion.4.refs_1_.refs_8_), channel_id=1, source_target_pairs={{0,1},{1,0},{2,3},{3,2},{4,5},{5,4},{6,7},{7,6},{8,9},{9,8},{10,11... | collective-permute-start | bytes 2359304 | tf_op jit(solution)/shard_map/ppermute | solution.py:705
  73.7 22.5 %collective-permute-start = (bf16[256,1536]{1,0:T(8,128)(2,1)S(1)}, bf16[256,1536]{1,0:T(8,128)(2,1)S(1)}, u32[]{:S(2)}, u32[]{:S(2)}) collective-permute-start(bf16[256,1536]{1,0:T(8,128)(2,1)S(1)} %fusion.3.refs_1_.refs_4_), channel_id=1, source_target_pairs={{0,1},{1,0},{2,3},{3,2},{4,5},{5,4},{6,7},{7,6},{8,9},{9,8},{10,11... | collective-permute-start | bytes 2359304 | tf_op jit(solution)/shard_map/ppermute | solution.py:705
  121.3 36.1 %collective-permute-start.24 = (bf16[96,1536]{1,0:T(8,128)(2,1)}, bf16[96,1536]{1,0:T(8,128)(2,1)}, u32[]{:S(2)}, u32[]{:S(2)}) collective-permute-start(bf16[96,1536]{1,0:T(8,128)(2,1)} %collective-permute-done.20.refs_13_), channel_id=1, source_target_pairs={{0,4},{4,0},{8,12},{12,8},{16,20},{20,16},{24,28},{28,24},{1,5},{5... | collective-permute-start | bytes 884744 | tf_op jit(solution)/shard_map/ppermute | solution.py:705
  126.5 30.9 %collective-permute-start.17 = (bf16[96,1536]{1,0:T(8,128)(2,1)}, bf16[96,1536]{1,0:T(8,128)(2,1)}, u32[]{:S(2)}, u32[]{:S(2)}) collective-permute-start(bf16[96,1536]{1,0:T(8,128)(2,1)} %collective-permute-done.13.refs_5_), channel_id=1, source_target_pairs={{0,4},{4,0},{8,12},{12,8},{16,20},{20,16},{24,28},{28,24},{1,5},{5... | collective-permute-start | bytes 884744 | tf_op jit(solution)/shard_map/ppermute | solution.py:705
  128.1 29.3 %collective-permute-start.23 = (bf16[96,1536]{1,0:T(8,128)(2,1)}, bf16[96,1536]{1,0:T(8,128)(2,1)}, u32[]{:S(2)}, u32[]{:S(2)}) collective-permute-start(bf16[96,1536]{1,0:T(8,128)(2,1)} %collective-permute-done.19.refs_12_), channel_id=1, source_target_pairs={{0,4},{4,0},{8,12},{12,8},{16,20},{20,16},{24,28},{28,24},{1,5},{5... | collective-permute-start | bytes 884744 | tf_op jit(solution)/shard_map/ppermute | solution.py:705
  128.1 29.3 %collective-permute-start.18 = (bf16[96,1536]{1,0:T(8,128)(2,1)}, bf16[96,1536]{1,0:T(8,128)(2,1)}, u32[]{:S(2)}, u32[]{:S(2)}) collective-permute-start(bf16[96,1536]{1,0:T(8,128)(2,1)} %collective-permute-done.14.refs_6_), channel_id=1, source_target_pairs={{0,4},{4,0},{8,12},{12,8},{16,20},{20,16},{24,28},{28,24},{1,5},{5... | collective-permute-start | bytes 884744 | tf_op jit(solution)/shard_map/ppermute | solution.py:705
  128.8 28.6 %collective-permute-start.25 = (bf16[96,1536]{1,0:T(8,128)(2,1)}, bf16[96,1536]{1,0:T(8,128)(2,1)}, u32[]{:S(2)}, u32[]{:S(2)}) collective-permute-start(bf16[96,1536]{1,0:T(8,128)(2,1)} %collective-permute-done.21.refs_14_), channel_id=1, source_target_pairs={{0,4},{4,0},{8,12},{12,8},{16,20},{20,16},{24,28},{28,24},{1,5},{5... | collective-permute-start | bytes 884744 | tf_op jit(solution)/shard_map/ppermute | solution.py:705
  193.6 186.3 %collective-permute-start.49 = (bf16[256,1536]{1,0:T(8,128)(2,1)}, bf16[256,1536]{1,0:T(8,128)(2,1)}, u32[]{:S(2)}, u32[]{:S(2)}) collective-permute-start(bf16[256,1536]{1,0:T(8,128)(2,1)} %get-tuple-element.100), channel_id=1, source_target_pairs={{0,1},{1,0},{2,3},{3,2},{4,5},{5,4},{6,7},{7,6},{8,9},{9,8},{10,11... | collective-permute-start | bytes 2359304 | tf_op jit(solution)/shard_map/ppermute | solution.py:705
  196.4 27.6 %collective-permute-start.53 = (bf16[2,96,1536]{2,1,0:T(8,128)(2,1)S(1)}, bf16[2,96,1536]{2,1,0:T(8,128)(2,1)}, u32[]{:S(2)}, u32[]{:S(2)}) collective-permute-start(bf16[2,96,1536]{2,1,0:T(8,128)(2,1)S(1)} %add_convert_fusion.4), channel_id=1, source_target_pairs={{0,16},{4,20},{8,24},{12,28},{16,0},{20,4},{24,8},{28,12},{1,17},{... | collective-permute-start | bytes 1769480 | tf_op jit(solution)/shard_map/ppermute | solution.py:705
  197.8 28.5 %collective-permute-start.52 = (bf16[2,96,1536]{2,1,0:T(8,128)(2,1)}, bf16[2,96,1536]{2,1,0:T(8,128)(2,1)S(1)}, u32[]{:S(2)}, u32[]{:S(2)}) collective-permute-start(bf16[2,96,1536]{2,1,0:T(8,128)(2,1)} %add_convert_fusion.5), channel_id=1, source_target_pairs={{0,8},{4,12},{8,0},{12,4},{16,24},{20,28},{24,16},{28,20},{1,9},{5... | collective-permute-start | bytes 1769480 | tf_op jit(solution)/shard_map/ppermute | solution.py:705
  223.5 31.4 %collective-permute-start.56 = (bf16[4,192,896]{2,1,0:T(8,128)(2,1)}, bf16[4,192,896]{2,1,0:T(8,128)(2,1)S(1)}, u32[]{:S(2)}, u32[]{:S(2)}) collective-permute-start(bf16[4,192,896]{2,1,0:T(8,128)(2,1)} %get-tuple-element.121), channel_id=1, source_target_pairs={{0,4},{4,0},{8,12},{12,8},{16,20},{20,16},{24,28},{28,24},{1,5},{5... | collective-permute-start | bytes 4128776 | tf_op jit(solution)/shard_map/ppermute | solution.py:705
  223.5 28.8 %collective-permute-start.55 = (bf16[4,192,768]{2,1,0:T(8,128)(2,1)}, bf16[4,192,768]{2,1,0:T(8,128)(2,1)S(1)}, u32[]{:S(2)}, u32[]{:S(2)}) collective-permute-start(bf16[4,192,768]{2,1,0:T(8,128)(2,1)} %get-tuple-element.120), channel_id=1, source_target_pairs={{0,4},{4,0},{8,12},{12,8},{16,20},{20,16},{24,28},{28,24},{1,5},{5... | collective-permute-start | bytes 3538952 | tf_op jit(solution)/shard_map/ppermute | solution.py:705
  225.9 19.4 %collective-permute-start.54 = (bf16[96,1536]{1,0:T(8,128)(2,1)}, bf16[96,1536]{1,0:T(8,128)(2,1)S(1)}, u32[]{:S(2)}, u32[]{:S(2)}) collective-permute-start(bf16[96,1536]{1,0:T(8,128)(2,1)} %fusion.22), channel_id=1, source_target_pairs={{0,8},{4,12},{8,0},{12,4},{16,24},{20,28},{24,16},{28,20},{1,9},{5... | collective-permute-start | bytes 884744 | tf_op jit(solution)/shard_map/ppermute | solution.py:705
  227.3 38.2 %collective-permute-start.81 = (bf16[96,1536]{1,0:T(8,128)(2,1)}, bf16[96,1536]{1,0:T(8,128)(2,1)S(1)}, u32[]{:S(2)}, u32[]{:S(2)}) collective-permute-start(bf16[96,1536]{1,0:T(8,128)(2,1)} %fusion.21), channel_id=1, source_target_pairs={{0,16},{4,20},{8,24},{12,28},{16,0},{20,4},{24,8},{28,12},{1,17},{... | collective-permute-start | bytes 884744 | tf_op jit(solution)/shard_map/ppermute | solution.py:705
  247.4 18.5 %collective-permute-start.82 = (bf16[96,1536]{1,0:T(8,128)(2,1)}, bf16[96,1536]{1,0:T(8,128)(2,1)}, u32[]{:S(2)}, u32[]{:S(2)}) collective-permute-start(bf16[96,1536]{1,0:T(8,128)(2,1)} %fusion.16), channel_id=1, source_target_pairs={{0,2},{1,3},{2,0},{3,1},{4,6},{5,7},{6,4},{7,5},{8,10},{9,11},{10,... | collective-permute-start | bytes 884744 | tf_op jit(solution)/shard_map/ppermute | solution.py:705
  260.5 26.6 %collective-permute-start.60 = (bf16[4,192,896]{2,1,0:T(8,128)(2,1)}, bf16[4,192,896]{2,1,0:T(8,128)(2,1)S(1)}, u32[]{:S(2)}, u32[]{:S(2)}) collective-permute-start(bf16[4,192,896]{2,1,0:T(8,128)(2,1)} %get-tuple-element.127), channel_id=1, source_target_pairs={{0,4},{4,0},{8,12},{12,8},{16,20},{20,16},{24,28},{28,24},{1,5},{5... | collective-permute-start | bytes 4128776 | tf_op jit(solution)/shard_map/ppermute | solution.py:705
  265.4 22.8 %collective-permute-start.59 = (bf16[4,192,1024]{2,1,0:T(8,128)(2,1)}, bf16[4,192,1024]{2,1,0:T(8,128)(2,1)S(1)}, u32[]{:S(2)}, u32[]{:S(2)}) collective-permute-start(bf16[4,192,1024]{2,1,0:T(8,128)(2,1)} %get-tuple-element.125), channel_id=1, source_target_pairs={{0,4},{4,0},{8,12},{12,8},{16,20},{20,16},{24,28},{28,24},{1,5},{5... | collective-permute-start | bytes 4718600 | tf_op jit(solution)/shard_map/ppermute | solution.py:705
  267.2 18.4 %collective-permute-start.58 = (bf16[2,192,896]{2,1,0:T(8,128)(2,1)S(1)}, bf16[2,192,896]{2,1,0:T(8,128)(2,1)S(1)}, u32[]{:S(2)}, u32[]{:S(2)}) collective-permute-start(bf16[2,192,896]{2,1,0:T(8,128)(2,1)S(1)} %add_convert_fusion.2), channel_id=1, source_target_pairs={{0,16},{4,20},{8,24},{12,28},{16,0},{20,4},{24,8},{28,12},{1,17},{... | collective-permute-start | bytes 2064392 | tf_op jit(solution)/shard_map/ppermute | solution.py:705
  270.5 36.6 %collective-permute-start.73 = (bf16[192,768]{1,0:T(8,128)(2,1)S(1)}, bf16[192,768]{1,0:T(8,128)(2,1)S(1)}, u32[]{:S(2)}, u32[]{:S(2)}) collective-permute-start(bf16[192,768]{1,0:T(8,128)(2,1)S(1)} %fusion.23), channel_id=1, source_target_pairs={{0,16},{4,20},{8,24},{12,28},{16,0},{20,4},{24,8},{28,12},{1,17},{... | collective-permute-start | bytes 884744 | tf_op jit(solution)/shard_map/ppermute | solution.py:705
  317.8 62.6 %collective-permute-start.74 = (bf16[192,768]{1,0:T(8,128)(2,1)}, bf16[192,768]{1,0:T(8,128)(2,1)S(1)}, u32[]{:S(2)}, u32[]{:S(2)}) collective-permute-start(bf16[192,768]{1,0:T(8,128)(2,1)} %fusion.15), channel_id=1, source_target_pairs={{0,2},{1,3},{2,0},{3,1},{4,6},{5,7},{6,4},{7,5},{8,10},{9,11},{10,... | collective-permute-start | bytes 884744 | tf_op jit(solution)/shard_map/ppermute | solution.py:705
  323.5 22.2 %collective-permute-start.66 = (f32[8,1792]{1,0:T(8,128)}, f32[8,1792]{1,0:T(8,128)}, u32[]{:S(2)}, u32[]{:S(2)}) collective-permute-start(f32[8,1792]{1,0:T(8,128)} %slice.309), channel_id=1, source_target_pairs={{0,1},{1,0},{2,3},{3,2},{4,5},{5,4},{6,7},{7,6},{8,9},{9,8},{10,11... | collective-permute-start | bytes 172040 | tf_op jit(solution)/shard_map/ppermute | solution.py:705
  325.2 21.0 %collective-permute-start.67 = (f32[8,1792]{1,0:T(8,128)}, f32[8,1792]{1,0:T(8,128)}, u32[]{:S(2)}, u32[]{:S(2)}) collective-permute-start(f32[8,1792]{1,0:T(8,128)} %slice.309), channel_id=1, source_target_pairs={{0,2},{1,3},{2,0},{3,1},{4,6},{5,7},{6,4},{7,5},{8,10},{9,11},{10,... | collective-permute-start | bytes 172040 | tf_op jit(solution)/shard_map/ppermute | solution.py:705
  345.7 20.8 %collective-permute-start.71 = (bf16[2,192,896]{2,1,0:T(8,128)(2,1)}, bf16[2,192,896]{2,1,0:T(8,128)(2,1)S(1)}, u32[]{:S(2)}, u32[]{:S(2)}) collective-permute-start(bf16[2,192,896]{2,1,0:T(8,128)(2,1)} %add_convert_fusion.1), channel_id=1, source_target_pairs={{0,16},{4,20},{8,24},{12,28},{16,0},{20,4},{24,8},{28,12},{1,17},{... | collective-permute-start | bytes 2064392 | tf_op jit(solution)/shard_map/ppermute | solution.py:705
  346.2 18.8 %collective-permute-start.69 = (bf16[2,192,1024]{2,1,0:T(8,128)(2,1)S(1)}, bf16[2,192,1024]{2,1,0:T(8,128)(2,1)S(1)}, u32[]{:S(2)}, u32[]{:S(2)}) collective-permute-start(bf16[2,192,1024]{2,1,0:T(8,128)(2,1)S(1)} %copy-done.32), channel_id=1, source_target_pairs={{0,8},{4,12},{8,0},{12,4},{16,24},{20,28},{24,16},{28,20},{1,9},{5... | collective-permute-start | bytes 2359304 | tf_op jit(solution)/shard_map/ppermute | solution.py:705
  347.4 21.9 %collective-permute-start.61 = (bf16[256,1536]{1,0:T(8,128)(2,1)}, bf16[256,1536]{1,0:T(8,128)(2,1)S(1)}, u32[]{:S(2)}, u32[]{:S(2)}) collective-permute-start(bf16[256,1536]{1,0:T(8,128)(2,1)} %get-tuple-element.137), channel_id=1, source_target_pairs={{0,1},{1,0},{2,3},{3,2},{4,5},{5,4},{6,7},{7,6},{8,9},{9,8},{10,11... | collective-permute-start | bytes 2359304 | tf_op jit(solution)/shard_map/ppermute | solution.py:705
  365.0 20.6 %collective-permute-start.76 = (bf16[192,896]{1,0:T(8,128)(2,1)}, bf16[192,896]{1,0:T(8,128)(2,1)S(1)}, u32[]{:S(2)}, u32[]{:S(2)}) collective-permute-start(bf16[192,896]{1,0:T(8,128)(2,1)} %fusion.11), channel_id=1, source_target_pairs={{0,2},{1,3},{2,0},{3,1},{4,6},{5,7},{6,4},{7,5},{8,10},{9,11},{10,... | collective-permute-start | bytes 1032200 | tf_op jit(solution)/shard_map/ppermute | solution.py:705
  377.2 20.2 %collective-permute-start.77 = (bf16[192,256]{1,0:T(8,128)(2,1)S(1)}, bf16[192,256]{1,0:T(8,128)(2,1)S(1)}, u32[]{:S(2)}, u32[]{:S(2)}) collective-permute-start(bf16[192,256]{1,0:T(8,128)(2,1)S(1)} %fusion.30), channel_id=1, source_target_pairs={{0,1},{1,0},{2,3},{3,2},{4,5},{5,4},{6,7},{7,6},{8,9},{9,8},{10,11... | collective-permute-start | bytes 294920 | tf_op jit(solution)/shard_map/ppermute | solution.py:705
  (140 other events, 2308.4 us)

commit v4 on v3

--- a/solution.py
+++ b/solution.py
@@ -20,6 +20,7 @@
 lanes = 128
 HEAD = "head"
 DP = "dp"
+WEIGHT_PLACE, TOKEN_PLACE = 2, 1
 sub = 8
 f32 = jnp.float32
 bf16 = jnp.bfloat16
@@ -39,6 +40,14 @@
         precision=lax.Precision.HIGHEST,
         preferred_element_type=f32,
     )
+
+
+def dot_chosen(lhs, chosen):
+    high = lhs.astype(bf16)
+    rest = lhs - high.astype(f32)
+    middle = rest.astype(bf16)
+    low = (rest - middle.astype(f32)).astype(bf16)
+    return dot(high, chosen) + dot(middle, chosen) + dot(low, chosen)
 
 
 def iota(shape, axis):
@@ -354,10 +363,10 @@
         hot = (
             2 * pair + (iota((lanes, lanes), 0) >= half_lanes).astype(jnp.int32)
             == iota((lanes, lanes), 1)
-        ).astype(f32)
+        ).astype(bf16)
         balance = out_low.astype(f32) * plain - scaled_low.astype(f32) * scaled_grad
-        cum_grad = cum_grad + dot_exact(balance, hot)
-        step_grad = step_grad + dot_exact(values * scaled_grad, hot)
+        cum_grad = cum_grad + dot_chosen(balance, hot)
+        step_grad = step_grad + dot_chosen(values * scaled_grad, hot)
         value_grad = skip * out_grad + scaled_grad * spread
         pre_grad = value_grad * (pre_sig * (1.0 + pre * (1.0 - pre_sig)))
         cotb_ref[:, cols] = conv_back(pre_grad, taps, kernel).astype(bf16)
@@ -885,15 +894,15 @@
     tables = (table, cbc)
 
     if paired:
-        more_a = swap_by(zx_low[:, 0], HEAD, 4, 2)
-        more_b = swap_by(piece_b, HEAD, 4, 2)
+        more_a = swap_by(zx_low[:, 0], HEAD, 4, WEIGHT_PLACE)
+        more_b = swap_by(piece_b, HEAD, 4, WEIGHT_PLACE)
         near_a = gather_near(piece_a, 2)
         near_b = gather_near(piece_b, 4)
-        normed_all = (normed_own, swap_by(normed_own, HEAD, 4, 1))
-        out_more_low = swap_by(out_low, HEAD, 4, 2)
-        tables_more = (swap_by(table, HEAD, 4, 2), cbc)
+        normed_all = (normed_own, swap_by(normed_own, HEAD, 4, TOKEN_PLACE))
+        out_more_low = swap_by(out_low, HEAD, 4, WEIGHT_PLACE)
+        tables_more = (swap_by(table, HEAD, 4, WEIGHT_PLACE), cbc)
         own_pieces = (gather_rest(piece_a, *near_a, 2), gather_rest(piece_b, *near_b, 4))
-        more_a, more_b = after((more_a, more_b), *near_a, *near_b)
+        more_a, more_b = after((more_a, more_b), *own_pieces[0], *own_pieces[1])
         near_a = gather_near(more_a, 2)
         near_b = gather_near(more_b, 4)
         more_pieces = (gather_rest(more_a, *near_a, 2), gather_rest(more_b, *near_b, 4))
@@ -901,7 +910,7 @@
         near_a = gather_near(out_low, 2)
         near_b = gather_near(out_more_low, 4)
         out_pieces = (gather_rest(out_low, *near_a, 2), gather_rest(out_more_low, *near_b, 4))
-        cot_all = (cot_own, swap_by(cot_own, HEAD, 4, 1))
+        cot_all = (cot_own, swap_by(cot_own, HEAD, 4, TOKEN_PLACE))
         proj_a, proj_b, plain, gated, own_a, own_b, turned = run_forward(
             place, normed_all, own_pieces, None, tables, seq_len, state, kernel
         )
@@ -911,7 +920,7 @@
         grad, more_grad, stats, lifted_turned, lifted, more_lifted, out_a, out_b = run_gate(
             place, cot_all, out_pieces, (gated, more_gated), (table, tables_more[0]), seq_len, kernel
         )
-        stat_parts = [stats, swap_by(stats, HEAD, 4, 1)]
+        stat_parts = [stats, swap_by(stats, HEAD, 4, TOKEN_PLACE)]
         out_own = run_product(
             place, lifted_turned, cot_all, order_of(2), stat_parts, 0, 2, inner_all
         )
@@ -922,7 +931,7 @@
         branch_own, branch_peer = run_sum(
             branch_kernel, (lifted, more_lifted), (out_a, out_b), False
         )
-        branch_own = branch_own + swap_by(branch_peer, HEAD, 4, 1).astype(f32)
+        branch_own = branch_own + swap_by(branch_peer, HEAD, 4, TOKEN_PLACE).astype(f32)
         square_own = stats[:1] + stat_parts[1][sub : sub + 1]
         gate_own = lax.rsqrt(square_own / inner_all + norm_eps).reshape(seq_len, 1)
         out_own = scatter_first(*out_own)
@@ -978,7 +987,7 @@
             grad_own_a[0],
             grad_own_b[0],
         )
-        grad_out = scatter_third(*out_own, 2) + swap_by(out_away, HEAD, 4, 2).astype(f32)
+        grad_out = scatter_third(*out_own, 2) + swap_by(out_away, HEAD, 4, WEIGHT_PLACE).astype(f32)
         cot_whole, cot_peer, grad_gain = run_sum(
             cotangent_kernel,
             (more_cot_a, more_cot_b, cot_a, cot_b),
@@ -986,11 +995,11 @@
             True,
             normed_all,
         )
-        cot_whole = cot_whole + swap_by(cot_peer, HEAD, 4, 1).astype(f32)
+        cot_whole = cot_whole + swap_by(cot_peer, HEAD, 4, TOKEN_PLACE).astype(f32)
         away_a = scatter_third(*grad_more_a, 2).astype(bf16)
         away_b = scatter_third(*grad_more_b, 4).astype(bf16)
-        home_a = swap_by(away_a, HEAD, 4, 2)
-        home_b = swap_by(away_b, HEAD, 4, 2)
+        home_a = swap_by(away_a, HEAD, 4, WEIGHT_PLACE)
+        home_b = swap_by(away_b, HEAD, 4, WEIGHT_PLACE)
         grad_own_a = scatter_second(*grad_own_a, 2)
         grad_own_b = scatter_second(*grad_own_b, 4)
         terms_a = scatter_last(*grad_own_a, 2)
@@ -1008,7 +1017,7 @@
         small = small + sum(swap_by(small, DP, 8, mask) for mask in (2, 4, 6))
         both = small[:, 2 * wide :]
         both = both + sum(swap_by(both, HEAD, 4, mask) for mask in (1, 2, 3))
-        own_sums = small[:, wide : 2 * wide] + swap_by(small[:, :wide], HEAD, 4, 2)
+        own_sums = small[:, wide : 2 * wide] + swap_by(small[:, :wide], HEAD, 4, WEIGHT_PLACE)
         cbc_sums, grad_gain = both[:, : 2 * state], both[0, 2 * state :]
     else:
         normed_all = lax.all_gather(normed_own, HEAD, axis=0, tiled=True)

time: 406 us -> 417 us (1.027)
  waiting for transfers between devices: 142 us -> 151 us
  other arithmetic: 44.7 us -> 49.7 us
    ppermute x83, waiting for transfers between devices: 142 us -> 151 us  [swap_by(): return lax.ppermute(values, axis, [(i, i ^ mask) for i in range(count)])]
    unnamed x190 -> x186, local copies, waits for them, and re-layouts: 14.8 us -> 14.8 us
  transfers between devices with their start and end apart: 83 -> 83, of which waited for: 24 -> 23; matrix products, arithmetic and copies ran while one was open for 14% -> 15% of each run, Pallas kernels for 27% -> 26%
where the time goes in v4:
time: 417 us; the launch traced here: 411 us
  waiting for transfers between devices  151 us (36%)
  Pallas kernels  121 us (29%)
  starting transfers between devices  64.4 us (15%)
  other arithmetic  49.7 us (12%)
  local copies, waits for them, and re-layouts  22.9 us (5%)
    ppermute x83, waiting for transfers between devices, swap_by(): return lax.ppermute(values, axis, [(i, i ^ mask) for i in range(count)])  151 us
    ppermute x83, starting transfers between devices, swap_by(): return lax.ppermute(values, axis, [(i, i ^ mask) for i in range(count)])  64.4 us
    pallas_call x6, Pallas kernels, run_product(): pl.pallas_call(functools.partial(product_kernel, order=order, scaled=bool...  29.5 us
    pallas_call x2, Pallas kernels, run_backward(): pl.pallas_call(functools.partial(backward_kernel, inner=inner, state=stat...  28.1 us
    pallas_call x2, Pallas kernels, run_forward(): pl.pallas_call(functools.partial(forward_kernel, inner=inner, state=state...  27.5 us
    pallas_call x2, Pallas kernels, run_sum(): pl.pallas_call(kernel, grid=(width // tile,), in_specs=specs, out_specs=o...  18.3 us
    unnamed x186, local copies, waits for them, and re-layouts  14.8 us
    pallas_call x1, Pallas kernels, run_gate(): pl.pallas_call(functools.partial(gate_kernel, kernel=kernel, split=split,...  10.6 us
  transfers between devices with their start and end apart: 83, of which 23 were waited for; matrix products, arithmetic and copies ran while one was open for 15% of the time, Pallas kernels for 26%

profile of v4, /device:TPU:0, one launch (start us, length us, event | category | flops | bytes accessed | tf_op | source)
XLA Modules:
  0.0 411.4 jit_solution(16760477382929941526)
XLA Ops:
  10.4 27.9 %collective-permute-done.2.refs_3_ = bf16[192,768]{1,0:T(8,128)(2,1)S(1)} collective-permute-done((bf16[192,768]{1,0:T(8,128)(2,1)S(1)}, bf16[192,768]{1,0:T(8,128)(2,1)S(1)}, u32[]{:S(2)}, u32[]{:S(2)}) %collective-permute-start.2) | collective-permute-done | bytes 294944 | tf_op jit(solution)/shard_map/ppermute | solution.py:714
  41.5 8.8 %collective-permute-done.4.refs_4_ = bf16[192,1024]{1,0:T(8,128)(2,1)S(1)} collective-permute-done((bf16[192,1024]{1,0:T(8,128)(2,1)S(1)}, bf16[192,1024]{1,0:T(8,128)(2,1)S(1)}, u32[]{:S(2)}, u32[]{:S(2)}) %collective-permute-start.4) | collective-permute-done | bytes 393248 | tf_op jit(solution)/shard_map/ppermute | solution.py:714
  51.6 4.9 %collective-permute-done.13.refs_14_ = bf16[192,896]{1,0:T(8,128)(2,1)} collective-permute-done((bf16[192,896]{1,0:T(8,128)(2,1)}, bf16[192,896]{1,0:T(8,128)(2,1)}, u32[]{:S(2)}, u32[]{:S(2)}) %collective-permute-start.13) | collective-permute-done | bytes 344096 | tf_op jit(solution)/shard_map/ppermute | solution.py:714
  65.9 3.4 collective-permute-start.1
  71.4 18.7 %collective-permute-done.47.refs_20_.refs_22_.refs_7_ = f32[8,896]{1,0:T(8,128)S(1)} collective-permute-done((f32[8,896]{1,0:T(8,128)S(1)}, f32[8,896]{1,0:T(8,128)S(1)}, u32[]{:S(2)}, u32[]{:S(2)}) %collective-permute-start.47) | collective-permute-done | bytes 28704 | tf_op jit(solution)/shard_map/ppermute | solution.py:714
  92.7 7.5 %collective-permute-done.18.refs_4_ = bf16[192,768]{1,0:T(8,128)(2,1)S(1)} collective-permute-done((bf16[192,768]{1,0:T(8,128)(2,1)}, bf16[192,768]{1,0:T(8,128)(2,1)S(1)}, u32[]{:S(2)}, u32[]{:S(2)}) %collective-permute-start.18) | collective-permute-done | bytes 294944 | tf_op jit(solution)/shard_map/ppermute | solution.py:714
  105.3 4.9 %collective-permute-done.37.refs_6_ = bf16[192,768]{1,0:T(8,128)(2,1)S(1)} collective-permute-done((bf16[192,768]{1,0:T(8,128)(2,1)S(1)}, bf16[192,768]{1,0:T(8,128)(2,1)S(1)}, u32[]{:S(2)}, u32[]{:S(2)}) %collective-permute-start.37) | collective-permute-done | bytes 294944 | tf_op jit(solution)/shard_map/ppermute | solution.py:714
  116.6 5.8 %collective-permute-done.23.refs_5_ = bf16[96,1536]{1,0:T(8,128)(2,1)} collective-permute-done((bf16[96,1536]{1,0:T(8,128)(2,1)S(1)}, bf16[96,1536]{1,0:T(8,128)(2,1)}, u32[]{:S(2)}, u32[]{:S(2)}) %collective-permute-start.23) | collective-permute-done | bytes 294944 | tf_op jit(solution)/shard_map/ppermute | solution.py:714
  122.9 4.4 %collective-permute-done.42.refs_14_ = bf16[192,896]{1,0:T(8,128)(2,1)S(1)} collective-permute-done((bf16[192,896]{1,0:T(8,128)(2,1)S(1)}, bf16[192,896]{1,0:T(8,128)(2,1)S(1)}, u32[]{:S(2)}, u32[]{:S(2)}) %collective-permute-start.42) | collective-permute-done | bytes 344096 | tf_op jit(solution)/shard_map/ppermute | solution.py:714
  129.6 7.4 %collective-permute-done.24.refs_6_ = bf16[96,1536]{1,0:T(8,128)(2,1)} collective-permute-done((bf16[96,1536]{1,0:T(8,128)(2,1)S(1)}, bf16[96,1536]{1,0:T(8,128)(2,1)}, u32[]{:S(2)}, u32[]{:S(2)}) %collective-permute-start.24) | collective-permute-done | bytes 294944 | tf_op jit(solution)/shard_map/ppermute | solution.py:714
  140.8 14.3 %kf1.1 = (f32[512,1024]{1,0:T(8,128)}, f32[512,896]{1,0:T(8,128)}, f32[512,768]{1,0:T(8,128)}, f32[512,768]{1,0:T(8,128)}, bf16[1536,1024]{1,0:T(8,128)(2,1)}, /...) custom-call(s32[1]{0:T(128)} %bitcast.1.refs_0_, bf16[256,1536]{1,0:T(8,128)(2,1)} %copy-done, ...), custom_call_target="tpu_custom_call" | custom-call | tf_op jit(solution)/shard_map/kf1/pallas_call | solution.py:492
  155.1 13.2 %kf2.1 = (f32[512,768]{1,0:T(8,128)}, f32[512,896]{1,0:T(8,128)}, f32[512,768]{1,0:T(8,128)}, f32[512,768]{1,0:T(8,128)}, bf16[1536,768]{1,0:T(8,128)(2,1)}, /*index=5*/bf16[1536,896]{1,0:T(8,128)(2,1)}) custom-call(s32[1]{0:T(128)} %bitcast.1.refs_0_, bf16[256,1536]{1,0:T(8,128)(2,1)} %copy-done, bf16[256,1536]{1,0:T(8,128)(2,1)} %copy-done.3, ...), custom_call_target="tpu_custom_call" | custom-call | tf_op jit(solution)/shard_map/kf2/pallas_call | solution.py:492
  168.3 10.6 %kgt.1 = (f32[512,768]{1,0:T(8,128)}, f32[512,768]{1,0:T(8,128)}, f32[16,256]{1,0:T(8,128)}, bf16[1536,512]{1,0:T(8,128)(2,1)}, bf16[512,768]{1,0:T(8,128)(2,1)}...) custom-call(s32[1]{0:T(128)} %bitcast.1.refs_0_, bf16[256,1536]{1,0:T(8,128)(2,1)} %copy-done.2, ...), custom_call_target="tpu_custom_call" | custom-call | tf_op jit(solution)/shard_map/kgt/pallas_call | solution.py:529
  178.9 4.5 %collective-permute-start.48 = (f32[16,256]{1,0:T(8,128)}, f32[16,256]{1,0:T(8,128)S(1)}, u32[]{:S(2)}, u32[]{:S(2)}) collective-permute-start(f32[16,256]{1,0:T(8,128)} %get-tuple-element.92.refs_2_.refs_0_), channel_id=1, source_target_pairs={{0,1},{1,0},{2,3},{3,2},{4,5},{5,4},{6,7},{7,6},{8,9},{9,8},{10,11... | collective-permute-start | bytes 49160 | tf_op jit(solution)/shard_map/ppermute | solution.py:714
  186.0 4.9 %shard_map.323 = (bf16[4,96,1536]{2,1,0:T(8,128)(2,1)}, bf16[4,96,1536]{2,1,0:T(8,128)(2,1)}) custom-call(s32[1]{0:T(128)} %bitcast.1.refs_0_, bf16[1536,512]{1,0:T(8,128)(2,1)} %get-tuple-element.91.refs_1_, f32[16,256]{1,0:T(8,128)} %get-tuple-element.92.refs_2_.refs_0_, f32[16,256]{1,0:T(8,128)} %copy-done.65, bf16[256,1536]{1,0:T(8,128)(2,1)} %copy-done.2, ...), custom_call_target="tpu_custom_call" | custom-call | tf_op jit(solution)/shard_map/pallas_call | solution.py:617
  193.7 4.9 %shard_map.322 = (bf16[4,96,1536]{2,1,0:T(8,128)(2,1)}, bf16[4,96,1536]{2,1,0:T(8,128)(2,1)}) custom-call(s32[1]{0:T(128)} %bitcast.1.refs_0_, bf16[1536,512]{1,0:T(8,128)(2,1)} %get-tuple-element.91.refs_1_, f32[16,256]{1,0:T(8,128)} %get-tuple-element.92.refs_2_.refs_0_, f32[16,256]{1,0:T(8,128)} %copy-done.65, bf16[256,1536]{1,0:T(8,128)(2,1)} %copy-done.2, ...), custom_call_target="tpu_custom_call" | custom-call | tf_op jit(solution)/shard_map/pallas_call | solution.py:617
  200.4 6.4 %shard_map.324 = (f32[256,1536]{1,0:T(8,128)}, bf16[256,1536]{1,0:T(8,128)(2,1)}) custom-call(bf16[512,768]{1,0:T(8,128)(2,1)} %get-tuple-element.95.refs_0_, bf16[512,768]{1,0:T(8,128)(2,1)} %get-tuple-element.96.refs_1_, bf16[768,1536]{1,0:T(8,128)(2,1)} %get-tuple-element.97.refs_2_, bf16[768,1536]{1,0:T(8,128)(2,1)} %get-tuple-element.98.refs_3_), custom_call_target="tpu_custom_call" | custom-call | tf_op jit(solution)/shard_map/pallas_call | solution.py:814
  215.2 13.9 %kb2.1 = (bf16[512,768]{1,0:T(8,128)(2,1)}, bf16[512,896]{1,0:T(8,128)(2,1)}, f32[8,896]{1,0:T(8,128)}, f32[512,256]{1,0:T(8,128)}) custom-call(f32[16,256]{1,0:T(8,128)} %get-tuple-element.92.refs_2_.refs_0_, f32[16,256]{1,0:T(8,128)} %copy-done.65, f32[512,768]{1,0:T(8,128)} %get-tuple-element.102.refs_2_, f32[512,896]{1,0:T(8,128)} %get-tuple-element.103.refs_3_, ...), custom_call_target="tpu_custom_call" | custom-call | tf_op jit(solution)/shard_map/kb2/pallas_call | solution.py:576
  229.2 5.2 %shard_map.326 = (bf16[4,192,896]{2,1,0:T(8,128)(2,1)}, bf16[4,192,896]{2,1,0:T(8,128)(2,1)}) custom-call(s32[1]{0:T(128)} %bitcast.1.refs_0_, bf16[1536,512]{1,0:T(8,128)(2,1)} %get-tuple-element.112.refs_1_, bf16[512,896]{1,0:T(8,128)(2,1)} %get-tuple-element.129.refs_2_.refs_1_), custom_call_target="tpu_custom_call" | custom-call | tf_op jit(solution)/shard_map/pallas_call | solution.py:617
  234.4 4.5 %shard_map.325 = (bf16[4,192,768]{2,1,0:T(8,128)(2,1)}, bf16[4,192,768]{2,1,0:T(8,128)(2,1)}) custom-call(s32[1]{0:T(128)} %bitcast.1.refs_0_, bf16[1536,512]{1,0:T(8,128)(2,1)} %get-tuple-element.112.refs_1_, bf16[512,768]{1,0:T(8,128)(2,1)} %get-tuple-element.128.refs_2_.refs_0_), custom_call_target="tpu_custom_call" | custom-call | tf_op jit(solution)/shard_map/pallas_call | solution.py:617
  244.2 14.2 %kb1.1 = (bf16[512,1024]{1,0:T(8,128)(2,1)}, bf16[512,896]{1,0:T(8,128)(2,1)}, f32[8,896]{1,0:T(8,128)}, f32[8,256]{1,0:T(8,128)}) custom-call(f32[16,256]{1,0:T(8,128)} %get-tuple-element.92.refs_2_.refs_0_, f32[16,256]{1,0:T(8,128)} %copy-done.65, f32[512,1024]{1,0:T(8,128)} %get-tuple-element.87.refs_19_.refs_4_.refs_2_, ...), custom_call_target="tpu_custom_call" | custom-call | tf_op jit(solution)/shard_map/kb1/pallas_call | solution.py:576
  264.9 5.1 %shard_map.328 = (bf16[4,192,896]{2,1,0:T(8,128)(2,1)}, bf16[4,192,896]{2,1,0:T(8,128)(2,1)}) custom-call(s32[1]{0:T(128)} %bitcast.1.refs_0_, bf16[1536,512]{1,0:T(8,128)(2,1)} %get-tuple-element.112.refs_1_, bf16[512,896]{1,0:T(8,128)(2,1)} %get-tuple-element.131.refs_2_.refs_3_), custom_call_target="tpu_custom_call" | custom-call | tf_op jit(solution)/shard_map/pallas_call | solution.py:617
  269.9 4.9 %shard_map.327 = (bf16[4,192,1024]{2,1,0:T(8,128)(2,1)}, bf16[4,192,1024]{2,1,0:T(8,128)(2,1)}) custom-call(s32[1]{0:T(128)} %bitcast.1.refs_0_, bf16[1536,512]{1,0:T(8,128)(2,1)} %get-tuple-element.112.refs_1_, bf16[512,1024]{1,0:T(8,128)(2,1)} %get-tuple-element.130.refs_2_), custom_call_target="tpu_custom_call" | custom-call | tf_op jit(solution)/shard_map/pallas_call | solution.py:617
  284.2 12.9 %collective-permute-done.58 = bf16[2,192,896]{2,1,0:T(8,128)(2,1)S(1)} collective-permute-done((bf16[2,192,896]{2,1,0:T(8,128)(2,1)S(1)}, bf16[2,192,896]{2,1,0:T(8,128)(2,1)S(1)}, u32[]{:S(2)}, u32[]{:S(2)}) %collective-permute-start.58) | collective-permute-done | bytes 688160 | tf_op jit(solution)/shard_map/ppermute | solution.py:714
  302.2 11.8 %shard_map.329 = (f32[256,1536]{1,0:T(8,128)}, bf16[256,1536]{1,0:T(8,128)(2,1)}, f32[8,1536]{1,0:T(8,128)}) custom-call(bf16[512,768]{1,0:T(8,128)(2,1)} %get-tuple-element.128.refs_2_.refs_0_, bf16[512,896]{1,0:T(8,128)(2,1)} %get-tuple-element.129.refs_2_.refs_1_, bf16[512,1024]{1,0:T(8,128)(2,1)} %get-tuple-element.130.refs_2_, ...), custom_call_target="tpu_custom_call" | custom-call | tf_op jit(solution)/shard_map/pallas_call | solution.py:814
  322.1 7.3 %collective-permute-done.63 = f32[8,3584]{1,0:T(8,128)S(1)} collective-permute-done((f32[8,3584]{1,0:T(8,128)S(1)}, f32[8,3584]{1,0:T(8,128)S(1)}, u32[]{:S(2)}, u32[]{:S(2)}) %collective-permute-start.63) | collective-permute-done | bytes 114720 | tf_op jit(solution)/shard_map/ppermute | solution.py:714
  338.0 7.8 %collective-permute-done.80 = f32[8,896]{1,0:T(8,128)S(1)} collective-permute-done((f32[8,896]{1,0:T(8,128)S(1)}, f32[8,896]{1,0:T(8,128)S(1)}, u32[]{:S(2)}, u32[]{:S(2)}) %collective-permute-start.80) | collective-permute-done | bytes 28704 | tf_op jit(solution)/shard_map/ppermute | solution.py:714
  365.0 11.3 %collective-permute-done.69.refs_2_ = bf16[2,192,1024]{2,1,0:T(8,128)(2,1)S(1)} collective-permute-done((bf16[2,192,1024]{2,1,0:T(8,128)(2,1)S(1)}, bf16[2,192,1024]{2,1,0:T(8,128)(2,1)S(1)}, u32[]{:S(2)}, u32[]{:S(2)}) %collective-permute-start.69) | collective-permute-done | bytes 786464 | tf_op jit(solution)/shard_map/ppermute | solution.py:714
  381.1 4.8 %collective-permute-done.70.refs_3_ = bf16[192,1024]{1,0:T(8,128)(2,1)S(1)} collective-permute-done((bf16[192,1024]{1,0:T(8,128)(2,1)S(1)}, bf16[192,1024]{1,0:T(8,128)(2,1)S(1)}, u32[]{:S(2)}, u32[]{:S(2)}) %collective-permute-start.70) | collective-permute-done | bytes 393248 | tf_op jit(solution)/shard_map/ppermute | solution.py:714
  387.0 3.8 collective-permute-start.77
  393.2 3.3 convert_add_fusion.1
  398.0 7.0 %kad.1 = (f32[192,2,768]{2,1,0:T(2,128)}, f32[2,192,2,768]{3,2,1,0:T(2,128)}, f32[192,12]{1,0:T(8,128)}, f32[2,192,12]{2,1,0:T(8,128)}) custom-call(bf16[4,192,1024]{2,1,0:T(8,128)(2,1)} %get-tuple-element.124.refs_0_, bf16[4,192,1024]{2,1,0:T(8,128)(2,1)} %copy-done.6, bf16[2,192,1024]{2,1,0:T(8,128)(2,1)} %copy-done.11, bf16[192,1024]{1,0:T(8,128)(2,1)} %copy-done.25, ...), custom_call_target="tpu_custom_call" | custom-call | tf_op jit(solution)/shard_map/kad/pallas_call | solution.py:702
  (407 shorter events, 139.2 us)
Async XLA Ops:
  2.4 36.5 %collective-permute-start.12 = (bf16[192,896]{1,0:T(8,128)(2,1)S(1)}, bf16[192,896]{1,0:T(8,128)(2,1)}, u32[]{:S(2)}, u32[]{:S(2)}) collective-permute-start(bf16[192,896]{1,0:T(8,128)(2,1)S(1)} %fusion.18.refs_11_), channel_id=1, source_target_pairs={{0,16},{4,20},{8,24},{12,28},{16,0},{20,4},{24,8},{28,12},{1,17},{... | collective-permute-start | bytes 1032200 | tf_op jit(solution)/shard_map/ppermute | solution.py:714
  5.4 33.9 %collective-permute-start.11 = (bf16[192,896]{1,0:T(8,128)(2,1)S(1)}, bf16[192,896]{1,0:T(8,128)(2,1)S(1)}, u32[]{:S(2)}, u32[]{:S(2)}) collective-permute-start(bf16[192,896]{1,0:T(8,128)(2,1)S(1)} %fusion.18.refs_11_), channel_id=1, source_target_pairs={{0,8},{4,12},{8,0},{12,4},{16,24},{20,28},{24,16},{28,20},{1,9},{5... | collective-permute-start | bytes 1032200 | tf_op jit(solution)/shard_map/ppermute | solution.py:714
  6.9 32.5 %collective-permute-start.14 = (bf16[192,896]{1,0:T(8,128)(2,1)S(1)}, bf16[192,896]{1,0:T(8,128)(2,1)}, u32[]{:S(2)}, u32[]{:S(2)}) collective-permute-start(bf16[192,896]{1,0:T(8,128)(2,1)S(1)} %fusion.18.refs_11_), channel_id=1, source_target_pairs={{0,4},{4,0},{8,12},{12,8},{16,20},{20,16},{24,28},{28,24},{1,5},{5... | collective-permute-start | bytes 1032200 | tf_op jit(solution)/shard_map/ppermute | solution.py:714
  6.9 34.1 %collective-permute-start.3 = (bf16[192,896]{1,0:T(8,128)(2,1)S(1)}, bf16[192,896]{1,0:T(8,128)(2,1)S(1)}, u32[]{:S(2)}, u32[]{:S(2)}) collective-permute-start(bf16[192,896]{1,0:T(8,128)(2,1)S(1)} %fusion.18.refs_11_), channel_id=1, source_target_pairs={{0,2},{1,3},{2,0},{3,1},{4,6},{5,7},{6,4},{7,5},{8,10},{9,11},{10,... | collective-permute-start | bytes 1032200 | tf_op jit(solution)/shard_map/ppermute | solution.py:714
  9.5 28.8 %collective-permute-start.2 = (bf16[192,768]{1,0:T(8,128)(2,1)S(1)}, bf16[192,768]{1,0:T(8,128)(2,1)S(1)}, u32[]{:S(2)}, u32[]{:S(2)}) collective-permute-start(bf16[192,768]{1,0:T(8,128)(2,1)S(1)} %get-tuple-element.195), channel_id=1, source_target_pairs={{0,2},{1,3},{2,0},{3,1},{4,6},{5,7},{6,4},{7,5},{8,10},{9,11},{10,... | collective-permute-start | bytes 884744 | tf_op jit(solution)/shard_map/ppermute | solution.py:714
  50.3 40.9 %collective-permute-start.36 = (bf16[256,1536]{1,0:T(8,128)(2,1)S(1)}, bf16[256,1536]{1,0:T(8,128)(2,1)S(1)}, u32[]{:S(2)}, u32[]{:S(2)}) collective-permute-start(bf16[256,1536]{1,0:T(8,128)(2,1)S(1)} %fusion.4.refs_1_.refs_8_), channel_id=1, source_target_pairs={{0,1},{1,0},{2,3},{3,2},{4,5},{5,4},{6,7},{7,6},{8,9},{9,8},{10,11... | collective-permute-start | bytes 2359304 | tf_op jit(solution)/shard_map/ppermute | solution.py:714
  58.4 34.3 %collective-permute-start = (bf16[256,1536]{1,0:T(8,128)(2,1)S(1)}, bf16[256,1536]{1,0:T(8,128)(2,1)}, u32[]{:S(2)}, u32[]{:S(2)}) collective-permute-start(bf16[256,1536]{1,0:T(8,128)(2,1)S(1)} %fusion.3.refs_1_.refs_4_), channel_id=1, source_target_pairs={{0,1},{1,0},{2,3},{3,2},{4,5},{5,4},{6,7},{7,6},{8,9},{9,8},{10,11... | collective-permute-start | bytes 2359304 | tf_op jit(solution)/shard_map/ppermute | solution.py:714
  65.9 24.8 %collective-permute-start.1 = (bf16[96,1536]{1,0:T(8,128)(2,1)S(1)}, bf16[96,1536]{1,0:T(8,128)(2,1)S(1)}, u32[]{:S(2)}, u32[]{:S(2)}) collective-permute-start(bf16[96,1536]{1,0:T(8,128)(2,1)S(1)} %convert_element_type.326.refs_3_), channel_id=1, source_target_pairs={{0,2},{1,3},{2,0},{3,1},{4,6},{5,7},{6,4},{7,5},{8,10},{9,11},{10,... | collective-permute-start | bytes 884744 | tf_op jit(solution)/shard_map/ppermute | solution.py:714
  70.8 19.4 %collective-permute-start.47 = (f32[8,896]{1,0:T(8,128)S(1)}, f32[8,896]{1,0:T(8,128)S(1)}, u32[]{:S(2)}, u32[]{:S(2)}) collective-permute-start(f32[8,896]{1,0:T(8,128)S(1)} %select_maximum_fusion.refs_19_.refs_21_.refs_7_), channel_id=1, source_target_pairs={{0,2},{1,3},{2,0},{3,1},{4,6},{5,7},{6,4},{7,5},{8,10},{9,11},{10,... | collective-permute-start | bytes 86024 | tf_op jit(solution)/shard_map/ppermute | solution.py:714
  70.9 30.0 %collective-permute-start.20 = (bf16[192,896]{1,0:T(8,128)(2,1)}, bf16[192,896]{1,0:T(8,128)(2,1)S(1)}, u32[]{:S(2)}, u32[]{:S(2)}) collective-permute-start(bf16[192,896]{1,0:T(8,128)(2,1)} %copy-done.38), channel_id=1, source_target_pairs={{0,16},{4,20},{8,24},{12,28},{16,0},{20,4},{24,8},{28,12},{1,17},{... | collective-permute-start | bytes 1032200 | tf_op jit(solution)/shard_map/ppermute | solution.py:714
  129.4 38.9 %collective-permute-start.34 = (bf16[96,1536]{1,0:T(8,128)(2,1)}, bf16[96,1536]{1,0:T(8,128)(2,1)}, u32[]{:S(2)}, u32[]{:S(2)}) collective-permute-start(bf16[96,1536]{1,0:T(8,128)(2,1)} %collective-permute-done.30.refs_13_), channel_id=1, source_target_pairs={{0,4},{4,0},{8,12},{12,8},{16,20},{20,16},{24,28},{28,24},{1,5},{5... | collective-permute-start | bytes 884744 | tf_op jit(solution)/shard_map/ppermute | solution.py:714
  137.0 31.3 %collective-permute-start.27 = (bf16[96,1536]{1,0:T(8,128)(2,1)}, bf16[96,1536]{1,0:T(8,128)(2,1)}, u32[]{:S(2)}, u32[]{:S(2)}) collective-permute-start(bf16[96,1536]{1,0:T(8,128)(2,1)} %collective-permute-done.23.refs_5_), channel_id=1, source_target_pairs={{0,4},{4,0},{8,12},{12,8},{16,20},{20,16},{24,28},{28,24},{1,5},{5... | collective-permute-start | bytes 884744 | tf_op jit(solution)/shard_map/ppermute | solution.py:714
  137.5 30.8 %collective-permute-start.33 = (bf16[96,1536]{1,0:T(8,128)(2,1)}, bf16[96,1536]{1,0:T(8,128)(2,1)}, u32[]{:S(2)}, u32[]{:S(2)}) collective-permute-start(bf16[96,1536]{1,0:T(8,128)(2,1)} %collective-permute-done.29.refs_12_), channel_id=1, source_target_pairs={{0,4},{4,0},{8,12},{12,8},{16,20},{20,16},{24,28},{28,24},{1,5},{5... | collective-permute-start | bytes 884744 | tf_op jit(solution)/shard_map/ppermute | solution.py:714
  137.5 30.8 %collective-permute-start.28 = (bf16[96,1536]{1,0:T(8,128)(2,1)}, bf16[96,1536]{1,0:T(8,128)(2,1)}, u32[]{:S(2)}, u32[]{:S(2)}) collective-permute-start(bf16[96,1536]{1,0:T(8,128)(2,1)} %collective-permute-done.24.refs_6_), channel_id=1, source_target_pairs={{0,4},{4,0},{8,12},{12,8},{16,20},{20,16},{24,28},{28,24},{1,5},{5... | collective-permute-start | bytes 884744 | tf_op jit(solution)/shard_map/ppermute | solution.py:714
  139.0 29.4 %collective-permute-start.35 = (bf16[96,1536]{1,0:T(8,128)(2,1)}, bf16[96,1536]{1,0:T(8,128)(2,1)}, u32[]{:S(2)}, u32[]{:S(2)}) collective-permute-start(bf16[96,1536]{1,0:T(8,128)(2,1)} %collective-permute-done.31.refs_14_), channel_id=1, source_target_pairs={{0,4},{4,0},{8,12},{12,8},{16,20},{20,16},{24,28},{28,24},{1,5},{5... | collective-permute-start | bytes 884744 | tf_op jit(solution)/shard_map/ppermute | solution.py:714
  190.9 19.3 %collective-permute-start.51 = (bf16[4,96,1536]{2,1,0:T(8,128)(2,1)}, bf16[4,96,1536]{2,1,0:T(8,128)(2,1)}, u32[]{:S(2)}, u32[]{:S(2)}) collective-permute-start(bf16[4,96,1536]{2,1,0:T(8,128)(2,1)} %get-tuple-element.107), channel_id=1, source_target_pairs={{0,4},{4,0},{8,12},{12,8},{16,20},{20,16},{24,28},{28,24},{1,5},{5... | collective-permute-start | bytes 3538952 | tf_op jit(solution)/shard_map/ppermute | solution.py:714
  206.8 183.9 %collective-permute-start.49 = (bf16[256,1536]{1,0:T(8,128)(2,1)}, bf16[256,1536]{1,0:T(8,128)(2,1)}, u32[]{:S(2)}, u32[]{:S(2)}) collective-permute-start(bf16[256,1536]{1,0:T(8,128)(2,1)} %get-tuple-element.100), channel_id=1, source_target_pairs={{0,1},{1,0},{2,3},{3,2},{4,5},{5,4},{6,7},{7,6},{8,9},{9,8},{10,11... | collective-permute-start | bytes 2359304 | tf_op jit(solution)/shard_map/ppermute | solution.py:714
  212.2 27.2 %collective-permute-start.53 = (bf16[2,96,1536]{2,1,0:T(8,128)(2,1)}, bf16[2,96,1536]{2,1,0:T(8,128)(2,1)}, u32[]{:S(2)}, u32[]{:S(2)}) collective-permute-start(bf16[2,96,1536]{2,1,0:T(8,128)(2,1)} %add_convert_fusion.4), channel_id=1, source_target_pairs={{0,16},{4,20},{8,24},{12,28},{16,0},{20,4},{24,8},{28,12},{1,17},{... | collective-permute-start | bytes 1769480 | tf_op jit(solution)/shard_map/ppermute | solution.py:714
  214.7 28.1 %collective-permute-start.52 = (bf16[2,96,1536]{2,1,0:T(8,128)(2,1)}, bf16[2,96,1536]{2,1,0:T(8,128)(2,1)S(1)}, u32[]{:S(2)}, u32[]{:S(2)}) collective-permute-start(bf16[2,96,1536]{2,1,0:T(8,128)(2,1)} %add_convert_fusion.5), channel_id=1, source_target_pairs={{0,8},{4,12},{8,0},{12,4},{16,24},{20,28},{24,16},{28,20},{1,9},{5... | collective-permute-start | bytes 1769480 | tf_op jit(solution)/shard_map/ppermute | solution.py:714
  238.9 24.8 %collective-permute-start.56 = (bf16[4,192,896]{2,1,0:T(8,128)(2,1)}, bf16[4,192,896]{2,1,0:T(8,128)(2,1)S(1)}, u32[]{:S(2)}, u32[]{:S(2)}) collective-permute-start(bf16[4,192,896]{2,1,0:T(8,128)(2,1)} %get-tuple-element.121), channel_id=1, source_target_pairs={{0,4},{4,0},{8,12},{12,8},{16,20},{20,16},{24,28},{28,24},{1,5},{5... | collective-permute-start | bytes 4128776 | tf_op jit(solution)/shard_map/ppermute | solution.py:714
  238.9 23.1 %collective-permute-start.55 = (bf16[4,192,768]{2,1,0:T(8,128)(2,1)}, bf16[4,192,768]{2,1,0:T(8,128)(2,1)S(1)}, u32[]{:S(2)}, u32[]{:S(2)}) collective-permute-start(bf16[4,192,768]{2,1,0:T(8,128)(2,1)} %get-tuple-element.120), channel_id=1, source_target_pairs={{0,4},{4,0},{8,12},{12,8},{16,20},{20,16},{24,28},{28,24},{1,5},{5... | collective-permute-start | bytes 3538952 | tf_op jit(solution)/shard_map/ppermute | solution.py:714
  243.7 31.2 %collective-permute-start.81 = (bf16[96,1536]{1,0:T(8,128)(2,1)}, bf16[96,1536]{1,0:T(8,128)(2,1)S(1)}, u32[]{:S(2)}, u32[]{:S(2)}) collective-permute-start(bf16[96,1536]{1,0:T(8,128)(2,1)} %fusion.21), channel_id=1, source_target_pairs={{0,16},{4,20},{8,24},{12,28},{16,0},{20,4},{24,8},{28,12},{1,17},{... | collective-permute-start | bytes 884744 | tf_op jit(solution)/shard_map/ppermute | solution.py:714
  269.9 28.7 %collective-permute-start.60 = (bf16[4,192,896]{2,1,0:T(8,128)(2,1)}, bf16[4,192,896]{2,1,0:T(8,128)(2,1)S(1)}, u32[]{:S(2)}, u32[]{:S(2)}) collective-permute-start(bf16[4,192,896]{2,1,0:T(8,128)(2,1)} %get-tuple-element.127), channel_id=1, source_target_pairs={{0,4},{4,0},{8,12},{12,8},{16,20},{20,16},{24,28},{28,24},{1,5},{5... | collective-permute-start | bytes 4128776 | tf_op jit(solution)/shard_map/ppermute | solution.py:714
  274.9 24.9 %collective-permute-start.59 = (bf16[4,192,1024]{2,1,0:T(8,128)(2,1)}, bf16[4,192,1024]{2,1,0:T(8,128)(2,1)S(1)}, u32[]{:S(2)}, u32[]{:S(2)}) collective-permute-start(bf16[4,192,1024]{2,1,0:T(8,128)(2,1)} %get-tuple-element.125), channel_id=1, source_target_pairs={{0,4},{4,0},{8,12},{12,8},{16,20},{20,16},{24,28},{28,24},{1,5},{5... | collective-permute-start | bytes 4718600 | tf_op jit(solution)/shard_map/ppermute | solution.py:714
  283.7 35.9 %collective-permute-start.73 = (bf16[192,768]{1,0:T(8,128)(2,1)}, bf16[192,768]{1,0:T(8,128)(2,1)}, u32[]{:S(2)}, u32[]{:S(2)}) collective-permute-start(bf16[192,768]{1,0:T(8,128)(2,1)} %fusion.23), channel_id=1, source_target_pairs={{0,16},{4,20},{8,24},{12,28},{16,0},{20,4},{24,8},{28,12},{1,17},{... | collective-permute-start | bytes 884744 | tf_op jit(solution)/shard_map/ppermute | solution.py:714
  329.4 61.9 %collective-permute-start.74 = (bf16[192,768]{1,0:T(8,128)(2,1)}, bf16[192,768]{1,0:T(8,128)(2,1)S(1)}, u32[]{:S(2)}, u32[]{:S(2)}) collective-permute-start(bf16[192,768]{1,0:T(8,128)(2,1)} %fusion.15), channel_id=1, source_target_pairs={{0,2},{1,3},{2,0},{3,1},{4,6},{5,7},{6,4},{7,5},{8,10},{9,11},{10,... | collective-permute-start | bytes 884744 | tf_op jit(solution)/shard_map/ppermute | solution.py:714
  335.9 21.5 %collective-permute-start.66 = (f32[8,1792]{1,0:T(8,128)}, f32[8,1792]{1,0:T(8,128)}, u32[]{:S(2)}, u32[]{:S(2)}) collective-permute-start(f32[8,1792]{1,0:T(8,128)} %slice.309), channel_id=1, source_target_pairs={{0,1},{1,0},{2,3},{3,2},{4,5},{5,4},{6,7},{7,6},{8,9},{9,8},{10,11... | collective-permute-start | bytes 172040 | tf_op jit(solution)/shard_map/ppermute | solution.py:714
  336.4 22.5 %collective-permute-start.67 = (f32[8,1792]{1,0:T(8,128)}, f32[8,1792]{1,0:T(8,128)}, u32[]{:S(2)}, u32[]{:S(2)}) collective-permute-start(f32[8,1792]{1,0:T(8,128)} %slice.309), channel_id=1, source_target_pairs={{0,2},{1,3},{2,0},{3,1},{4,6},{5,7},{6,4},{7,5},{8,10},{9,11},{10,... | collective-permute-start | bytes 172040 | tf_op jit(solution)/shard_map/ppermute | solution.py:714
  357.4 20.4 %collective-permute-start.71 = (bf16[2,192,896]{2,1,0:T(8,128)(2,1)}, bf16[2,192,896]{2,1,0:T(8,128)(2,1)S(1)}, u32[]{:S(2)}, u32[]{:S(2)}) collective-permute-start(bf16[2,192,896]{2,1,0:T(8,128)(2,1)} %add_convert_fusion.1), channel_id=1, source_target_pairs={{0,16},{4,20},{8,24},{12,28},{16,0},{20,4},{24,8},{28,12},{1,17},{... | collective-permute-start | bytes 2064392 | tf_op jit(solution)/shard_map/ppermute | solution.py:714
  359.9 19.6 %collective-permute-start.61 = (bf16[256,1536]{1,0:T(8,128)(2,1)}, bf16[256,1536]{1,0:T(8,128)(2,1)S(1)}, u32[]{:S(2)}, u32[]{:S(2)}) collective-permute-start(bf16[256,1536]{1,0:T(8,128)(2,1)} %get-tuple-element.137), channel_id=1, source_target_pairs={{0,1},{1,0},{2,3},{3,2},{4,5},{5,4},{6,7},{7,6},{8,9},{9,8},{10,11... | collective-permute-start | bytes 2359304 | tf_op jit(solution)/shard_map/ppermute | solution.py:714
  376.3 20.3 %collective-permute-start.76 = (bf16[192,896]{1,0:T(8,128)(2,1)}, bf16[192,896]{1,0:T(8,128)(2,1)S(1)}, u32[]{:S(2)}, u32[]{:S(2)}) collective-permute-start(bf16[192,896]{1,0:T(8,128)(2,1)} %fusion.11), channel_id=1, source_target_pairs={{0,2},{1,3},{2,0},{3,1},{4,6},{5,7},{6,4},{7,5},{8,10},{9,11},{10,... | collective-permute-start | bytes 1032200 | tf_op jit(solution)/shard_map/ppermute | solution.py:714
  387.0 21.4 %collective-permute-start.77 = (bf16[192,256]{1,0:T(8,128)(2,1)S(1)}, bf16[192,256]{1,0:T(8,128)(2,1)S(1)}, u32[]{:S(2)}, u32[]{:S(2)}) collective-permute-start(bf16[192,256]{1,0:T(8,128)(2,1)S(1)} %fusion.30), channel_id=1, source_target_pairs={{0,1},{1,0},{2,3},{3,2},{4,5},{5,4},{6,7},{7,6},{8,9},{9,8},{10,11... | collective-permute-start | bytes 294920 | tf_op jit(solution)/shard_map/ppermute | solution.py:714
  (138 other events, 2086.6 us)
